TPU v7x, 32 devices: a whole 2x2x4 slice. The times are simulated.
32 devices in a mesh: stn: 8 (over z, core), win: 4 (over y, x).
Axes of the slice: x: 2, y: 2, z: 4, core: 2. Of those that a mesh axis runs over, the one named last changes fastest.
Arguments:
- records: bfloat16 [128, 4, 3, 8192], P('stn', 'win'), may hold values from -6 to 6
- observed: float32 [128, 3, 3, 256], P('stn'), may hold values from -6 to 6
- lag_lo: int32 [128], P('stn'), may hold values from 0 to 63
- lag_hi: int32 [128], P('stn'), may hold values from 192 to 256
- send_table: int32 [8, 8, 1], P('stn'), may hold values from 0 to 15, as said below
- pair_first: int32 [128], P('stn'), may hold values from 0 to 7, as said below
- pair_second: int32 [128], P('stn'), may hold values from 0 to 7, as said below
Outputs:
- station_adjoint: bfloat16 [128, 4, 3, 8192], P('stn', 'win')
- residual: float32 [128, 3, 3, 256], P(('stn', 'win'))
Inputs may be any that keep to these rules, and one draw needn't show every extreme that they name: Each entry send_table[g, o, :] names 1 different local stations of group g. `pair_first`: slot indices at the pair's owner; a pair's two slots differ, no two pairs of an owner join the same two slots, and every slot of an owner is named by some pair. `pair_second`: slot indices at the pair's owner, as for pair_first.
All inputs are finite; a program needn't handle non-finite values.
Results may differ from a plain program's by a relative error of at most 0.0053.
Values may be sent and summed in bfloat16 or wider, within the bound.
No kernel may reach another device: no remote copies, remote signals or barrier semaphores. Data moves between devices by JAX's collectives and lax.ppermute only.
A program may use at most 192 MiB of HBM per device.

v0:
```python
import math

import jax
import jax.numpy as jnp
from jax import lax
from jax.sharding import PartitionSpec as P

LAGS = 256


def forward_table(lag_count):
    period = 2 * lag_count
    sample_ids = jnp.arange(lag_count, dtype=jnp.int32)
    freq_ids = jnp.arange(lag_count, dtype=jnp.int32)
    phase = (sample_ids[:, None] * freq_ids[None, :] % period).astype(jnp.float32) * (
        math.pi / lag_count
    )
    parity = (1 - 2 * (sample_ids % 2)).astype(jnp.float32)
    cosines = jnp.cos(phase)
    sines = jnp.where(freq_ids[None, :] == 0, parity[:, None], jnp.sin(phase))
    return jnp.concatenate([cosines, sines], axis=1)


def inverse_rows(positions, sine_sign, lag_count):
    period = 2 * lag_count
    freq_ids = jnp.arange(lag_count, dtype=jnp.int32)
    wrapped = positions % period
    phase = (freq_ids[:, None] * wrapped[None, :] % period).astype(jnp.float32) * (
        math.pi / lag_count
    )
    weight = jnp.where(freq_ids == 0, 1.0 / period, 2.0 / period).astype(jnp.float32)
    cos_rows = weight[:, None] * jnp.cos(phase)
    parity = (1 - 2 * (wrapped % 2)).astype(jnp.float32) / period
    sin_rows = jnp.where(
        freq_ids[:, None] == 0, parity[None, :], sine_sign * (2.0 / period) * jnp.sin(phase)
    )
    return jnp.concatenate([cos_rows, sin_rows], axis=0)


def shards(records, observed, lag_lo, lag_hi, send_table, pair_first, pair_second):
    owner_count = lax.axis_size("stn")
    window_groups = lax.axis_size("win")
    send_rows = send_table[0]
    cap_count = send_rows.shape[1]
    slot_count = owner_count * cap_count
    local_windows = records.shape[1]
    samples = records.shape[3]
    station_count = records.shape[0]
    lag_count = LAGS
    half_lag = lag_count // 2
    block_total = samples // lag_count
    highest = lax.Precision.HIGHEST
    outgoing = jnp.take(records, send_rows.reshape(-1), axis=0)
    outgoing = outgoing.reshape((owner_count, cap_count) + records.shape[1:])
    arrived = lax.all_to_all(outgoing, "stn", split_axis=0, concat_axis=0, tiled=True)
    slot_records = arrived.reshape((slot_count,) + records.shape[1:])
    spectral = forward_table(lag_count)
    lag_ids = jnp.arange(lag_count, dtype=jnp.int32)
    corr_table = inverse_rows(lag_ids, -1.0, lag_count)
    middle_table = inverse_rows(lag_ids + half_lag, 1.0, lag_count)
    lower_table = (
        inverse_rows(lag_ids + 3 * half_lag, 1.0, lag_count)
        * (lag_ids < half_lag).astype(jnp.float32)[None, :]
    )
    upper_table = (
        inverse_rows(lag_ids - half_lag, 1.0, lag_count)
        * (lag_ids >= half_lag).astype(jnp.float32)[None, :]
    )
    column_ids = jnp.arange(2 * lag_count, dtype=jnp.int32)
    shift_sign = (1 - 2 * (column_ids % lag_count % 2)).astype(jnp.float32)
    first_col = (lag_ids == 0).astype(jnp.float32)
    other_cols = 1.0 - first_col
    block_shape = (slot_count, local_windows, 3, block_total, lag_count)
    first_blocks = slot_records.astype(jnp.float32).reshape(block_shape)
    x_spec = jnp.dot(first_blocks, spectral, precision=highest)
    shifted = jnp.pad(slot_records, ((0, 0), (0, 0), (0, 0), (half_lag, lag_count - half_lag)))
    shifted = shifted.astype(jnp.float32).reshape(
        (slot_count, local_windows, 3, block_total + 1, lag_count)
    )
    z_spec = jnp.dot(shifted, spectral, precision=highest)
    y_spec = z_spec[..., :-1, :] + shift_sign * z_spec[..., 1:, :]
    slot_ids = jnp.arange(slot_count, dtype=jnp.int32)
    first_hot = (pair_first[:, None] == slot_ids[None, :]).astype(jnp.float32)
    second_hot = (pair_second[:, None] == slot_ids[None, :]).astype(jnp.float32)
    x_pair = jnp.einsum("ps,swakf->pwakf", first_hot, x_spec, precision=highest)
    y_pair = jnp.einsum("ps,swakf->pwakf", second_hot, y_spec, precision=highest)
    x_cos = x_pair[..., :lag_count]
    x_sin = x_pair[..., lag_count:]
    y_cos = y_pair[..., :lag_count]
    y_sin = y_pair[..., lag_count:]
    y_sin_other = y_sin * other_cols
    y_mixed = y_sin * first_col + y_cos * other_cols

    def cross_terms(left, right):
        return jnp.einsum("pwakf,pwbkf->pabf", left, right, precision=highest)

    real_part = cross_terms(x_cos, y_cos) + cross_terms(x_sin, y_sin_other)
    imag_part = cross_terms(x_sin, y_mixed) - cross_terms(x_cos, y_sin_other)
    cross = jnp.concatenate([real_part, imag_part], axis=-1)
    partial_corr = jnp.dot(cross, corr_table, precision=highest)
    pair_count = partial_corr.shape[0]
    corr_scale = 1.0 / math.sqrt(samples * local_windows * window_groups)
    lag_mask = (lag_ids[None, :] >= lag_lo[:, None]) & (lag_ids[None, :] < lag_hi[:, None])
    share_rows = pair_count // window_groups
    offset = lax.axis_index("win") * share_rows
    summed = lax.psum(partial_corr, "win")
    residual_all = jnp.where(lag_mask[:, None, None, :], summed * corr_scale - observed, 0.0)
    adjoint_source = residual_all.astype(jnp.bfloat16)
    residual_share = lax.dynamic_slice_in_dim(residual_all, offset, share_rows, 0)
    source_spec = jnp.dot(adjoint_source.astype(jnp.float32), spectral, precision=highest)
    src_cos = source_spec[..., :lag_count]
    src_sin = source_spec[..., lag_count:]
    src_cos_other = src_cos * other_cols
    src_sin_other = src_sin * other_cols
    src_sin_first = src_sin * first_col

    def first_terms(source, data):
        return jnp.einsum("pabf,pwbkf->pwakf", source, data, precision=highest)

    first_real = first_terms(src_cos, y_cos) + first_terms(src_sin_other, y_sin)
    first_imag = first_terms(src_sin, y_mixed) - first_terms(src_cos_other, y_sin)
    first_pair = jnp.concatenate([first_real, first_imag], axis=-1)
    first_acc = jnp.einsum("ps,pwakf->swakf", first_hot, first_pair, precision=highest)

    def second_terms(data, source):
        return jnp.einsum("pwakf,pabf->pwbkf", data, source, precision=highest)

    second_real = second_terms(x_cos, src_cos) - second_terms(x_sin, src_sin_other)
    second_imag = (
        second_terms(x_cos, src_sin_other)
        + second_terms(x_sin, src_cos_other)
        + second_terms(x_sin, src_sin_first)
    )
    second_pair = jnp.concatenate([second_real, second_imag], axis=-1)
    second_acc = jnp.einsum("ps,pwakf->swakf", second_hot, second_pair, precision=highest)
    first_time = jnp.dot(first_acc, corr_table, precision=highest)
    middle = jnp.dot(second_acc, middle_table, precision=highest)
    from_lower = jnp.dot(second_acc, lower_table, precision=highest)
    from_upper = jnp.dot(second_acc, upper_table, precision=highest)
    spacer = ((0, 0), (0, 0), (0, 0))
    from_lower = jnp.pad(from_lower[..., :-1, :], spacer + ((1, 0), (0, 0)))
    from_upper = jnp.pad(from_upper[..., 1:, :], spacer + ((0, 1), (0, 0)))
    slot_sum = (first_time + middle + from_lower + from_upper).reshape(
        (slot_count,) + records.shape[1:]
    )
    adj_scale = 1.0 / math.sqrt(3 * lag_count)
    slot_adjoint = (slot_sum * adj_scale).astype(jnp.bfloat16)
    slot_adjoint = slot_adjoint.reshape((owner_count, cap_count) + records.shape[1:])
    station_ids = jnp.arange(station_count, dtype=jnp.int32)
    station_hot = (send_rows.reshape(-1)[None, :] == station_ids[:, None]).astype(jnp.bfloat16)
    returned = lax.all_to_all(slot_adjoint, "stn", split_axis=0, concat_axis=0, tiled=True)
    flat_rows = returned.reshape((slot_count, -1))
    totals = jnp.dot(station_hot, flat_rows, preferred_element_type=jnp.float32)
    station_adjoint = totals.reshape((station_count,) + returned.shape[2:]).astype(jnp.bfloat16)
    return (station_adjoint, residual_share)


def solution(mesh):
    placed = (
        P("stn", "win", None, None),
        P("stn", None, None, None),
        P("stn"),
        P("stn"),
        P("stn", None, None),
        P("stn"),
        P("stn"),
    )
    return jax.shard_map(
        shards,
        mesh=mesh,
        in_specs=placed,
        out_specs=(P("stn", "win", None, None), P(("stn", "win"), None, None, None)),
        check_vma=False,
    )
```

profile of v0, /device:TPU:0, one launch (start us, length us, event | category | flops | bytes accessed | tf_op | source)
XLA Modules:
  0.0 665.9 jit_solution(7594870986401893331)
XLA Ops:
  7.2 0.7 fusion.137
  7.8 0.7 compare_and_fusion
  8.5 1.8 copy.236
  10.3 1.0 gather_fusion
  11.3 1.1 fusion.46
  12.4 6.3 all-to-all-start
  18.9 1.0 fusion.86
  19.9 0.7 fusion.88
  20.7 6.3 cosine_multiply_fusion.2
  27.0 7.1 %all-to-all-done = bf16[8,1,1,3,8192]{4,3,2,1,0:T(4,128)(2,1)S(1)} async-done(((bf16[8,1,1,3,8192]{4,3,2,1,0:T(4,128)(2,1)}), bf16[8,1,1,3,8192]{4,3,2,1,0:T(4,128)(2,1)S(1)}, u32[]{:S(2)}, u32[]{:S(2)}) %all-to-all-start) | async-done | bytes 393248 | tf_op jit(solution)/shard_map/all_to_all | solution.py:55
  34.3 0.5 reshape.439
  34.8 1.0 convolution_bitcast_fusion.2
  36.1 2.1 convolution_bitcast_fusion.1
  38.3 2.9 multiply_bitcast_fusion
  41.2 6.1 copy.158
  47.3 0.5 reshape.440
  47.8 0.9 fusion.48
  48.7 1.4 convolution_bitcast_fusion
  50.2 2.1 slice_bitcast_fusion.1
  52.3 6.2 copy.157
  58.5 6.1 copy.156
  64.6 6.1 copy.155
  70.7 30.7 %fusion.150 = f32[16,256,3,3]{3,2,1,0:T(4,128)S(1)} fusion(f32[16,3,32,256]{2,1,3,0:T(4,128)} %copy.158, f32[16,3,32,256]{2,1,3,0:T(4,128)} %copy.157), kind=kOutput, calls=%fused_computation.225 | convolution fusion | flops 14155776 | bytes 3293184 | tf_op jit(solution)/shard_map/pwakf,pwbkf->pabf/dot_general | solution.py:95
  101.4 29.8 %subtract_bitcast_fusion.2 = f32[16,3,3,256]{1,2,3,0:T(4,128)} fusion(f32[16,256,3,3]{3,2,1,0:T(4,128)S(1)} %fusion.150, f32[16,3,32,256]{2,1,3,0:T(4,128)S(1)} %copy-done.1, f32[16,3,32,256]{2,1,3,0:T(4,128)S(1)} %copy-done), kind=kOutput, calls=%fused_computation.9 | convolution fusion | flops 14192640 | bytes 3440640 | tf_op jit(solution)/shard_map/pwakf,pwbkf->pabf/dot_general | solution.py:95
  131.2 4.9 copy.163
  136.2 6.1 copy.164
  142.3 30.4 %fusion.149 = f32[16,256,3,3]{3,2,1,0:T(4,128)S(1)} fusion(f32[16,3,32,256]{2,1,3,0:T(4,128)} %copy.164, f32[16,3,32,256]{2,1,3,0:T(4,128)} %copy.155), kind=kOutput, calls=%fused_computation.224 | convolution fusion | flops 14155776 | bytes 3293184 | tf_op jit(solution)/shard_map/pwakf,pwbkf->pabf/dot_general | solution.py:95
  172.7 31.9 %add_bitcast_fusion.2 = f32[16,3,3,256]{1,2,3,0:T(4,128)} fusion(f32[16,256,3,3]{3,2,1,0:T(4,128)S(1)} %fusion.149, f32[16,3,32,256]{2,1,3,0:T(4,128)} %copy.156, f32[16,3,32,256]{2,1,3,0:T(4,128)} %copy.157), kind=kOutput, calls=%fused_computation.10 | convolution fusion | flops 14192640 | bytes 3440640 | tf_op jit(solution)/shard_map/pwakf,pwbkf->pabf/dot_general | solution.py:95
  204.6 5.0 copy.162
  209.6 1.1 fusion.47
  210.7 0.5 compare_convert_fusion
  211.3 0.6 compare_convert_fusion.1
  211.8 4.7 copy.166
  216.6 35.3 %all-reduce.5.cloned.1.call-done = f32[16,3,3,256]{3,0,2,1:T(8,128)} async-done(((f32[16,3,3,256]{3,0,2,1:T(8,128)}), f32[16,3,3,256]{3,0,2,1:T(8,128)}) %all-reduce.5.cloned.1.call-update) | async-done | bytes 147472 | tf_op jit(solution)/shard_map/psum | solution.py:106
  251.9 0.9 subtract_select_fusion
  253.5 4.7 copy.174
  258.2 37.4 %fusion.151 = f32[16,256,32,3]{2,3,1,0:T(4,128)} fusion(f32[16,3,32,256]{2,1,3,0:T(4,128)} %copy.164, f32[16,3,3,256]{1,2,3,0:T(4,128)} %copy.174), kind=kOutput, calls=%fused_computation.226 | convolution fusion | flops 14155776 | bytes 3293184 | tf_op jit(solution)/shard_map/pabf,pwbkf->pwakf/dot_general | solution.py:118
  295.6 30.2 %fusion.153 = f32[16,256,3,32]{3,2,1,0:T(4,128)} fusion(f32[16,3,3,256]{1,2,3,0:T(4,128)S(1)} %copy-done.3, f32[16,3,32,256]{2,1,3,0:T(4,128)} %copy.155), kind=kOutput, calls=%fused_computation.228 | convolution fusion | flops 14155776 | bytes 3293184 | tf_op jit(solution)/shard_map/pwakf,pabf->pwbkf/dot_general | solution.py:126
  325.8 4.6 copy.169
  330.4 32.4 %fusion.152 = f32[16,256,32,3]{2,3,1,0:T(4,128)} fusion(f32[16,3,32,256]{2,1,3,0:T(4,128)} %copy.158, f32[16,3,3,256]{2,1,3,0:T(4,128)} %copy.169), kind=kOutput, calls=%fused_computation.227 | convolution fusion | flops 14155776 | bytes 3293184 | tf_op jit(solution)/shard_map/pabf,pwbkf->pwakf/dot_general | solution.py:118
  362.8 4.7 copy.180
  367.5 4.6 copy.176
  372.1 31.0 %fusion.154 = f32[16,256,3,32]{3,2,1,0:T(4,128)} fusion(f32[16,3,3,256]{1,2,3,0:T(4,128)} %copy.176, f32[16,3,32,256]{2,1,3,0:T(4,128)} %copy.155), kind=kOutput, calls=%fused_computation.229 | convolution fusion | flops 14155776 | bytes 3293184 | tf_op jit(solution)/shard_map/pwakf,pabf->pwbkf/dot_general | solution.py:126
  403.1 30.8 %fusion.155 = f32[16,256,3,32]{3,2,1,0:T(4,128)} fusion(f32[16,3,3,256]{1,2,3,0:T(4,128)S(1)} %copy-done.2, f32[16,3,32,256]{2,1,3,0:T(4,128)} %copy.157), kind=kOutput, calls=%fused_computation.230 | convolution fusion | flops 14155776 | bytes 3293184 | tf_op jit(solution)/shard_map/pwakf,pabf->pwbkf/dot_general | solution.py:126
  433.9 36.6 %subtract_bitcast_fusion.1 = f32[16,1,3,32,256]{3,2,4,0,1:T(4,128)} fusion(f32[16,256,32,3]{2,3,1,0:T(4,128)} %fusion.152, f32[16,3,32,256]{2,1,3,0:T(4,128)S(1)} %bitcast.169, f32[16,3,3,256]{1,2,3,0:T(4,128)S(1)} %copy-done.2), kind=kOutput, calls=%fused_computation.7 | convolution fusion | flops 14548992 | bytes 4866048 | tf_op jit(solution)/shard_map/pabf,pwbkf->pwakf/dot_general | solution.py:118
  470.6 36.0 %add_bitcast_fusion.1 = f32[16,1,3,32,256]{3,2,4,0,1:T(4,128)} fusion(f32[16,256,32,3]{2,3,1,0:T(4,128)S(1)} %bitcast.171, f32[16,3,32,256]{2,1,3,0:T(4,128)S(1)} %bitcast.169, f32[16,3,3,256]{1,2,3,0:T(4,128)S(1)} %bitcast.167), kind=kOutput, calls=%fused_computation.8 | convolution fusion | flops 14548992 | bytes 4866048 | tf_op jit(solution)/shard_map/pabf,pwbkf->pwakf/dot_general | solution.py:118
  506.5 12.0 %maximum_bitcast_fusion = f32[16,3,32,512]{2,1,3,0:T(4,128)} fusion(f32[16,1,3,32,256]{3,2,4,0,1:T(4,128)S(1)} %copy-done.5, f32[16,1,3,32,256]{3,2,4,0,1:T(4,128)} %add_bitcast_fusion.1), kind=kLoop, calls=%fused_computation.1 | loop fusion | flops 786432 | bytes 6291456 | tf_op jit(solution)/shard_map/reshape.43
  518.5 9.5 %copy.172 = f32[16,3,32,512]{3,0,2,1:T(8,128)S(1)} copy(f32[16,3,32,512]{2,1,3,0:T(4,128)} %maximum_bitcast_fusion) | data formatting | bytes 6291456 | tf_op jit(solution)/shard_map/reshape.43
  528.0 1.9 fusion.92
  529.9 4.0 fusion.3
  534.0 4.6 copy.182
  538.6 31.8 %subtract_bitcast_fusion = f32[16,1,3,32,256]{3,2,4,0,1:T(4,128)} fusion(f32[16,256,3,32]{3,2,1,0:T(4,128)} %fusion.153, f32[16,3,3,256]{1,2,3,0:T(4,128)} %copy.176, f32[16,3,32,256]{2,1,3,0:T(4,128)} %copy.157), kind=kOutput, calls=%fused_computation.6 | convolution fusion | flops 14548992 | bytes 4866048 | tf_op jit(solution)/shard_map/pwakf,pabf->pwbkf/dot_general | solution.py:126
  570.4 31.8 %add_bitcast_fusion = f32[16,1,3,32,256]{3,2,4,0,1:T(4,128)} fusion(f32[16,256,3,32]{3,2,1,0:T(4,128)} %fusion.154, f32[16,256,3,32]{3,2,1,0:T(4,128)} %fusion.155, f32[16,3,3,256]{1,2,3,0:T(4,128)S(1)} %copy-done.4, f32[16,3,32,256]{2,1,3,0:T(4,128)} %copy.157), kind=kOutput, calls=%fused_computation.5 | convolution fusion | flops 14942208 | bytes 6438912 | tf_op jit(solution)/shard_map/pwakf,pabf->pwbkf/dot_general | solution.py:126
  602.2 15.0 %maximum_bitcast_fusion.1 = f32[16,3,32,512]{2,1,3,0:T(4,128)} fusion(f32[16,1,3,32,256]{3,2,4,0,1:T(4,128)} %add_bitcast_fusion, f32[16,1,3,32,256]{3,2,4,0,1:T(4,128)} %subtract_bitcast_fusion), kind=kLoop, calls=%fused_computation.2 | loop fusion | flops 786432 | bytes 6291456 | tf_op jit(solution)/shard_map/reshape.57
  617.2 9.8 %copy.184 = f32[16,3,32,512]{3,0,2,1:T(8,128)S(1)} copy(f32[16,3,32,512]{2,1,3,0:T(4,128)} %maximum_bitcast_fusion.1) | data formatting | bytes 6291456 | tf_op jit(solution)/shard_map/reshape.57
  627.1 1.2 fusion.96
  628.3 3.1 fusion.21
  631.6 2.2 fusion.18
  633.8 2.3 fusion.33
  636.1 1.0 reshape.441
  637.0 4.6 all-to-all-start.1
  641.7 1.5 constant_dynamic-slice_fusion
  643.2 13.9 %all-to-all-done.1 = bf16[8,1,1,3,8192]{4,3,2,1,0:T(4,128)(2,1)S(1)} async-done(((bf16[8,1,1,3,8192]{4,3,2,1,0:T(4,128)(2,1)}), bf16[8,1,1,3,8192]{4,3,2,1,0:T(4,128)(2,1)S(1)}, u32[]{:S(2)}, u32[]{:S(2)}) %all-to-all-start.1) | async-done | bytes 393248 | tf_op jit(solution)/shard_map/all_to_all | solution.py:151
  657.0 1.5 fusion
  (87 shorter events, 1.5 us)
Async XLA Ops:
  8.5 27.6 %copy-start.22 = (s32[16]{0:T(128)S(1)}, s32[16]{0:T(128)}, u32[]{:S(2)}) copy-start(s32[16]{0:T(128)} %param.13) | copy-start | bytes 196
  12.4 21.7 %all-to-all-start = ((bf16[8,1,1,3,8192]{4,3,2,1,0:T(4,128)(2,1)}), bf16[8,1,1,3,8192]{4,3,2,1,0:T(4,128)(2,1)S(1)}, u32[]{:S(2)}, u32[]{:S(2)}) async-start(bf16[8,1,1,3,8192]{4,3,2,1,0:T(4,128)(2,1)} %fusion.46), calls=%async_computation | async-start | bytes 1048576 | tf_op jit(solution)/shard_map/all_to_all | solution.py:55
  18.7 233.2 %all-reduce.5.cloned.1.call-start = ((), (), s32[]{:S(2)}) async-start(), calls=%async_computation.2 | async-start | bytes 294912 | tf_op jit(solution)/shard_map/psum | solution.py:106
  18.9 19.3 %copy-start.17 = (f32[256]{0:T(256)}, f32[256]{0:T(256)S(1)}, u32[]{:S(2)}) copy-start(f32[256]{0:T(256)S(1)} %broadcast_subtract_fusion) | copy-start | bytes 3076
  18.9 19.3 %copy-start.19 = (f32[256]{0:T(256)}, f32[256]{0:T(256)S(1)}, u32[]{:S(2)}) copy-start(f32[256]{0:T(256)S(1)} %fusion.138) | copy-start | bytes 3076
  41.2 7.6 %copy-start.21 = (s32[16]{0:T(128)S(1)}, s32[16]{0:T(128)}, u32[]{:S(2)}) copy-start(s32[16]{0:T(128)} %param.12) | copy-start | bytes 196
  70.7 30.7 %copy-start = (f32[16,3,32,256]{2,1,3,0:T(4,128)S(1)}, f32[16,3,32,256]{2,1,3,0:T(4,128)}, u32[]{:S(2)}) copy-start(f32[16,3,32,256]{2,1,3,0:T(4,128)} %copy.155) | copy-start | bytes 4718596
  70.7 30.7 %copy-start.1 = (f32[16,3,32,256]{2,1,3,0:T(4,128)S(1)}, f32[16,3,32,256]{2,1,3,0:T(4,128)}, u32[]{:S(2)}) copy-start(f32[16,3,32,256]{2,1,3,0:T(4,128)} %copy.156) | copy-start | bytes 4718596
  204.6 5.0 copy-start.7
  204.6 5.0 copy-start.9
  204.6 47.3 %copy-start.16 = (f32[16,3,3,256]{3,0,2,1:T(8,128)S(1)}, f32[16,3,3,256]{3,0,2,1:T(8,128)}, u32[]{:S(2)}) copy-start(f32[16,3,3,256]{3,0,2,1:T(8,128)} %param.8) | copy-start | bytes 442372
  204.6 48.6 %copy-start.18 = (f32[256]{0:T(256)S(1)}, f32[256]{0:T(256)}, u32[]{:S(2)}) copy-start(f32[256]{0:T(256)} %copy-done.17) | copy-start | bytes 3076
  204.6 48.6 %copy-start.20 = (f32[256]{0:T(256)S(1)}, f32[256]{0:T(256)}, u32[]{:S(2)}) copy-start(f32[256]{0:T(256)} %copy-done.19) | copy-start | bytes 3076
  252.8 0.7 copy-start.15
  258.2 37.4 %copy-start.3 = (f32[16,3,3,256]{1,2,3,0:T(4,128)S(1)}, f32[16,3,3,256]{1,2,3,0:T(4,128)}, u32[]{:S(2)}) copy-start(f32[16,3,3,256]{1,2,3,0:T(4,128)} %copy.174) | copy-start | bytes 442372
  372.1 31.0 %copy-start.2 = (f32[16,3,3,256]{1,2,3,0:T(4,128)S(1)}, f32[16,3,3,256]{1,2,3,0:T(4,128)}, u32[]{:S(2)}) copy-start(f32[16,3,3,256]{1,2,3,0:T(4,128)} %copy.180) | copy-start | bytes 442372
  372.1 61.8 %slice-start.2 = ((s8[8388608]{0:T(1024)(128)(4,1)}), s8[4194304]{0:T(1024)(128)(4,1)S(1)}, s32[]{:S(2)}) async-start(s8[8388608]{0:T(1024)(128)(4,1)} %bitcast.168), calls=%async_computation.5 | async-start | bytes 8388608
  403.1 30.8 %slice-start.3 = ((s8[8388608]{0:T(1024)(128)(4,1)}), s8[4194304]{0:T(1024)(128)(4,1)S(1)}, s32[]{:S(2)}) async-start(s8[8388608]{0:T(1024)(128)(4,1)} %bitcast.168), calls=%async_computation.6 | async-start | bytes 8388608
  403.1 67.5 %slice-start = ((s8[8388608]{0:T(1024)(128)(4,1)}), s8[4194304]{0:T(1024)(128)(4,1)S(1)}, s32[]{:S(2)}) async-start(s8[8388608]{0:T(1024)(128)(4,1)} %bitcast.166), calls=%async_computation.3 | async-start | bytes 8388608
  403.1 67.5 %slice-start.4 = ((s8[8388608]{0:T(1024)(128)(4,1)}), s8[4194304]{0:T(1024)(128)(4,1)S(1)}, s32[]{:S(2)}) async-start(s8[8388608]{0:T(1024)(128)(4,1)} %bitcast.170), calls=%async_computation.7 | async-start | bytes 8388608
  433.9 36.6 %slice-start.1 = ((s8[8388608]{0:T(1024)(128)(4,1)}), s8[4194304]{0:T(1024)(128)(4,1)S(1)}, s32[]{:S(2)}) async-start(s8[8388608]{0:T(1024)(128)(4,1)} %bitcast.166), calls=%async_computation.4 | async-start | bytes 8388608
  433.9 36.6 %slice-start.5 = ((s8[8388608]{0:T(1024)(128)(4,1)}), s8[4194304]{0:T(1024)(128)(4,1)S(1)}, s32[]{:S(2)}) async-start(s8[8388608]{0:T(1024)(128)(4,1)} %bitcast.170), calls=%async_computation.8 | async-start | bytes 8388608
  470.6 36.0 %copy-start.5 = (f32[16,1,3,32,256]{3,2,4,0,1:T(4,128)S(1)}, f32[16,1,3,32,256]{3,2,4,0,1:T(4,128)}, u32[]{:S(2)}) copy-start(f32[16,1,3,32,256]{3,2,4,0,1:T(4,128)} %subtract_bitcast_fusion.1) | copy-start | bytes 4718596
  518.5 11.4 %copy-start.8 = (f32[256,256]{1,0:T(8,128)S(1)}, f32[256,256]{1,0:T(8,128)}, u32[]{:S(2)}) copy-start(f32[256,256]{1,0:T(8,128)} %get-tuple-element.19) | copy-start | bytes 786436
  538.6 31.8 %copy-start.4 = (f32[16,3,3,256]{1,2,3,0:T(4,128)S(1)}, f32[16,3,3,256]{1,2,3,0:T(4,128)}, u32[]{:S(2)}) copy-start(f32[16,3,3,256]{1,2,3,0:T(4,128)} %copy.182) | copy-start | bytes 442372
  617.2 9.8 %copy-start.23 = (s32[16]{0:T(128)S(1)}, s32[16]{0:T(128)}, u32[]{:S(2)}) copy-start(s32[16]{0:T(128)} %param.13) | copy-start | bytes 196
  617.2 11.1 %copy-start.14 = (f32[256,256]{1,0:T(8,128)S(1)}, f32[256,256]{1,0:T(8,128)}, u32[]{:S(2)}) copy-start(f32[256,256]{1,0:T(8,128)} %get-tuple-element.17) | copy-start | bytes 786436
  617.2 11.1 %copy-start.25 = (f32[256]{0:T(256)S(1)}, f32[256]{0:T(256)}, u32[]{:S(2)}) copy-start(f32[256]{0:T(256)} %compare_convert_fusion) | copy-start | bytes 3076
  627.0 4.5 copy-start.12
  627.0 4.5 copy-start.13
  627.0 4.5 copy-start.24
  627.0 6.7 %copy-start.6 = (f32[8,3,32,256]{3,2,1,0:T(8,128)S(1)}, f32[8,3,32,256]{3,2,1,0:T(8,128)}, u32[]{:S(2)}) copy-start(f32[8,3,32,256]{3,2,1,0:T(8,128)} %fusion.3) | copy-start | bytes 2359300
  627.1 6.7 %copy-start.10 = (f32[256,256]{1,0:T(8,128)S(1)}, f32[256,256]{1,0:T(8,128)}, u32[]{:S(2)}) copy-start(f32[256,256]{1,0:T(8,128)} %get-tuple-element.13) | copy-start | bytes 786436
  627.1 6.7 %copy-start.11 = (f32[256,256]{1,0:T(8,128)S(1)}, f32[256,256]{1,0:T(8,128)}, u32[]{:S(2)}) copy-start(f32[256,256]{1,0:T(8,128)} %get-tuple-element.14) | copy-start | bytes 786436
  627.1 29.9 %copy-start.26 = (s32[1,8,1]{1,2,0:T(1,128)S(1)}, s32[1,8,1]{1,2,0:T(1,128)}, u32[]{:S(2)}) copy-start(s32[1,8,1]{1,2,0:T(1,128)} %param.11) | copy-start | bytes 100
  637.0 20.0 %all-to-all-start.1 = ((bf16[8,1,1,3,8192]{4,3,2,1,0:T(4,128)(2,1)}), bf16[8,1,1,3,8192]{4,3,2,1,0:T(4,128)(2,1)S(1)}, u32[]{:S(2)}, u32[]{:S(2)}) async-start(bf16[8,1,1,3,8192]{4,3,2,1,0:T(4,128)(2,1)} %bitcast.61), calls=%async_computation.1 | async-start | bytes 1048576 | tf_op jit(solution)/shard_map/all_to_all | solution.py:151
Sparse Core Ops, SparseCore 0:
  210.9 41.0 all-reduce.4
where the time goes:
time: 670 us; the launch traced here: 666 us
  matrix products  444 us (66%)
  local copies, waits for them, and re-layouts  96.7 us (14%)
  waiting for transfers between devices  56.3 us (8%)
  other arithmetic  42.8 us (6%)
  between operations  15.1 us (2%)
  starting transfers between devices  11 us (2%)
    dot_general x5, matrix products, second_terms(): return jnp.einsum('pwakf,pabf->pwbkf', data, source, precision=highest)  156 us
    dot_general x4, matrix products, first_terms(): return jnp.einsum('pabf,pwbkf->pwakf', source, data, precision=highest)  142 us
    dot_general x4, matrix products, cross_terms(): return jnp.einsum('pwakf,pwbkf->pabf', left, right, precision=highest)  123 us
    another operation x11, local copies, waits for them, and re-layouts  57.7 us
    psum x1, waiting for transfers between devices, shards(): summed = lax.psum(partial_corr, 'win')  35.3 us
    another operation x4, other arithmetic  30.2 us
    all_to_all x1, waiting for transfers between devices, shards(): lax.all_to_all(slot_adjoint, 'stn', split_axis=0, concat_axis=0, tiled=True)  13.9 us
  transfers between devices with their start and end apart: 3, of which 3 were waited for; matrix products, arithmetic and copies ran while one was open for 2% of the time, Pallas kernels for 0%

commit v1 on v0

v1 whole, which is shorter than its diff:
```python
import functools
import math

import jax
import jax.numpy as jnp
from jax import lax
from jax.experimental import pallas as pl
from jax.experimental.pallas import tpu as pltpu
from jax.sharding import PartitionSpec as P

LAGS = 256
HALF = LAGS // 2
LANES = 128
PHASES = 16
SPAN = LAGS + PHASES
CHANS = 3
WINDOW = 3 * LANES
DEPTH = 7 * LANES
TAIL = DEPTH - CHANS * SPAN


def pack_kernel(rows_ref, rec_ref, out_ref, scratch):
    stations = rec_ref.shape[1]
    chunks = rec_ref.shape[2] // LANES
    for r in range(chunks):
        piece = rec_ref[0, :, r * LANES:(r + 1) * LANES]
        scratch[r * stations:(r + 1) * stations, :] = piece.astype(jnp.float32)
    for d in range(out_ref.shape[0]):
        picked = scratch[pl.ds(rows_ref[d], chunks, stride=stations), :]
        out_ref[d, 0] = picked.astype(jnp.bfloat16)


def unpack_kernel(rows_ref, ret_ref, out_ref, scratch):
    stations = out_ref.shape[1]
    chunks = out_ref.shape[2] // LANES
    scratch[...] = jnp.zeros_like(scratch)
    for d in range(ret_ref.shape[0]):
        where = pl.ds(rows_ref[d], chunks, stride=stations)
        scratch[where, :] = scratch[where, :] + ret_ref[d, 0].astype(jnp.float32)
    for r in range(chunks):
        piece = scratch[r * stations:(r + 1) * stations, :]
        out_ref[0, :, r * LANES:(r + 1) * LANES] = piece.astype(jnp.bfloat16)


def build_phases(slot_ref, fan_ref):
    chunks = slot_ref.shape[1]
    rows = fan_ref.shape[1]
    lane = lax.broadcasted_iota(jnp.int32, (LANES, LANES), 1)
    full_lane = lax.broadcasted_iota(jnp.int32, (rows, LANES), 1)

    def step(g, carry):
        pair = slot_ref[pl.ds(2 * g, 2)].astype(jnp.float32).reshape(2 * chunks, LANES)
        middle = pair.T
        before = jnp.where(lane % chunks == 0, 0.0, pltpu.roll(middle, 1, 1))
        after = jnp.where(lane % chunks == chunks - 1, 0.0, pltpu.roll(middle, LANES - 1, 1))
        wide = jnp.concatenate([before, middle, after], axis=0)
        swapped = pltpu.roll(wide, chunks, 1)
        left = full_lane < chunks
        fan_ref[2 * g] = jnp.where(left, wide[:rows], swapped[PHASES:]).astype(jnp.bfloat16)
        fan_ref[2 * g + 1] = jnp.where(left, swapped[:rows], wide[PHASES:]).astype(jnp.bfloat16)
        return carry

    lax.fori_loop(0, slot_ref.shape[0] // 2, step, 0)


def shifted_rows(fan_ref, slot):
    columns = []
    for m in range(4):
        first = 2 * PHASES * m
        parts = [fan_ref[CHANS * slot + b, first:first + SPAN, :] for b in range(CHANS)]
        parts.append(fan_ref[CHANS * slot, first:first + TAIL, :])
        columns.append(jnp.concatenate(parts, axis=0))
    return jnp.concatenate(columns, axis=1)


def corr_kernel(first_ref, second_ref, slot_ref, corr_ref, fan_ref, heads):
    build_phases(slot_ref, fan_ref)
    height = CHANS * PHASES
    row = lax.broadcasted_iota(jnp.int32, (height, height), 0)
    column = lax.broadcasted_iota(jnp.int32, (height, height), 1)
    same = row // PHASES == column // PHASES
    flip = (same & (row % PHASES + column % PHASES == PHASES - 1)).astype(jnp.bfloat16)

    def head(q, carry):
        rows = []
        for a in range(CHANS):
            pieces = []
            for m in range(4):
                start = HALF + 2 * PHASES * m
                pieces.append(fan_ref[CHANS * q + a, start:start + PHASES, :])
            rows.append(jnp.concatenate(pieces, axis=1))
        natural = jnp.concatenate(rows, axis=0)
        heads[q] = jnp.dot(flip, natural, preferred_element_type=jnp.float32).astype(jnp.bfloat16)
        return carry

    lax.fori_loop(0, heads.shape[0], head, 0)

    def step(p, carry):
        right = shifted_rows(fan_ref, second_ref[p])
        products = lax.dot_general(
            heads[first_ref[p]], right, (((1,), (1,)), ((), ())),
            preferred_element_type=jnp.float32,
        )
        for a in range(CHANS):
            for b in range(CHANS):
                block = products[PHASES * a:PHASES * (a + 1), LAGS * b:LAGS * b + WINDOW]
                shift = WINDOW - PHASES * b - (PHASES - 1)
                turned = pltpu.roll(block, shift, 1, stride=1, stride_axis=0)
                corr_ref[CHANS * a + b, pl.ds(p, 1), :] = jnp.sum(
                    turned[:, :LAGS], axis=0, keepdims=True
                )
        return carry

    lax.fori_loop(0, corr_ref.shape[1], step, 0)


def spread(lag_rows, base, stride_rows):
    turned = []
    for c in range(CHANS):
        row = lag_rows[pl.ds(base + stride_rows * c, 1), :]
        block = jnp.broadcast_to(row, (PHASES, WINDOW))
        turned.append(pltpu.roll(block, PHASES * c, 1, stride=1, stride_axis=0))
    w0, w1, w2 = turned
    return jnp.concatenate(
        [
            w0[:, :LAGS],
            w0[:, LAGS:] + w1[:, :LANES],
            w1[:, LANES:LAGS],
            w1[:, LAGS:] + w2[:, :LANES],
            w2[:, LANES:],
        ],
        axis=1,
    ).astype(jnp.bfloat16)


def adjoint_kernel(
    corr_scale, adj_scale, first_ref, second_ref, offset_ref,
    parts_ref, observed_ref, low_ref, high_ref, fan_ref,
    out_ref, share_ref, resid, forward, backward, bands, total,
):
    pairs = observed_ref.shape[1]
    combos = observed_ref.shape[0]
    slots = bands.shape[0]
    lag = lax.broadcasted_iota(jnp.int32, (pairs, LAGS), 1)
    inside = (lag >= low_ref[...]) & (lag < high_ref[...])
    flip = (
        lax.broadcasted_iota(jnp.int32, (LAGS, WINDOW), 0)
        + lax.broadcasted_iota(jnp.int32, (LAGS, WINDOW), 1)
        == LAGS
    ).astype(jnp.bfloat16)
    forward[...] = jnp.zeros_like(forward)
    for i in range(combos):
        summed = parts_ref[0, i]
        for w in range(1, parts_ref.shape[0]):
            summed = summed + parts_ref[w, i]
        value = jnp.where(inside, summed * corr_scale - observed_ref[i], 0.0)
        resid[i] = value
        rounded = value.astype(jnp.bfloat16)
        forward[i * pairs:(i + 1) * pairs, :LAGS] = rounded.astype(jnp.float32)
        backward[i * pairs:(i + 1) * pairs, :] = jnp.dot(
            rounded, flip, preferred_element_type=jnp.float32
        )
        for j in range(share_ref.shape[1]):
            share_ref[i, j:j + 1, :] = resid[i, pl.ds(offset_ref[0] + j, 1), :]

    bands[...] = jnp.zeros_like(bands)
    height = CHANS * PHASES

    def fill(p, carry):
        qf = first_ref[p]
        qs = second_ref[p]
        for c in range(CHANS):
            start = pl.multiple_of(height * qf + PHASES * c, PHASES)
            bands[qs, pl.ds(start, PHASES), :] = spread(forward, CHANS * pairs * c + p, pairs)
            start = pl.multiple_of(height * qs + PHASES * c, PHASES)
            bands[qf, pl.ds(start, PHASES), :] = spread(backward, pairs * c + p, CHANS * pairs)
        return carry

    lax.fori_loop(0, pairs, fill, 0)
    total[...] = jnp.zeros_like(total)

    def accumulate(r, carry):
        right = shifted_rows(fan_ref, r)
        total[...] += jnp.dot(bands[r], right, preferred_element_type=jnp.float32)
        return carry

    lax.fori_loop(0, slots, accumulate, 0)
    chunks = out_ref.shape[1]
    left = lax.broadcasted_iota(jnp.int32, (PHASES, LANES), 1) < chunks

    def store(g, carry):
        base = pl.multiple_of(2 * PHASES * g, 2 * PHASES)
        pieces = []
        for m in range(4):
            one = total[pl.ds(base, PHASES), m * LANES:(m + 1) * LANES]
            two = total[pl.ds(base + PHASES, PHASES), m * LANES:(m + 1) * LANES]
            pieces.append(jnp.where(left, one, pltpu.roll(two, chunks, 1)))
            pieces.append(jnp.where(left, pltpu.roll(one, chunks, 1), two))
        tile = jnp.concatenate(pieces, axis=0).T * adj_scale
        out_ref[pl.ds(2 * g, 2)] = tile.reshape(2, chunks, LANES).astype(jnp.bfloat16)
        return carry

    lax.fori_loop(0, out_ref.shape[0] // 2, store, 0)


def smem():
    return pl.BlockSpec(memory_space=pltpu.SMEM)


def vmem():
    return pl.BlockSpec(memory_space=pltpu.VMEM)


def shards(records, observed, lag_lo, lag_hi, send_table, pair_first, pair_second):
    owner_count = lax.axis_size("stn")
    window_groups = lax.axis_size("win")
    stations, local_windows, _, samples = records.shape
    send_rows = send_table.reshape(-1)
    slots = send_rows.shape[0]
    chunks = samples // LANES
    pairs = observed.shape[0]
    combos = CHANS * CHANS
    share = pairs // window_groups
    corr_scale = 1.0 / math.sqrt(samples * local_windows * window_groups)
    adj_scale = 1.0 / math.sqrt(CHANS * LAGS)

    planes = jnp.transpose(records, (1, 2, 0, 3)).reshape(CHANS, stations, samples)
    outgoing = pl.pallas_call(
        pack_kernel,
        grid_spec=pltpu.PrefetchScalarGridSpec(
            num_scalar_prefetch=1,
            grid=(CHANS,),
            in_specs=[pl.BlockSpec((1, stations, samples), lambda c, rows: (c, 0, 0))],
            out_specs=pl.BlockSpec((slots, 1, chunks, LANES), lambda c, rows: (0, c, 0, 0)),
            scratch_shapes=[pltpu.VMEM((chunks * stations, LANES), jnp.float32)],
        ),
        out_shape=jax.ShapeDtypeStruct((slots, CHANS, chunks, LANES), jnp.bfloat16),
        name="pack",
    )(send_rows, planes)
    arrived = lax.all_to_all(outgoing, "stn", split_axis=0, concat_axis=0, tiled=True)

    rows = 3 * LANES - PHASES
    corr, fan = pl.pallas_call(
        corr_kernel,
        in_specs=[smem(), smem(), vmem()],
        out_specs=[vmem(), vmem()],
        out_shape=[
            jax.ShapeDtypeStruct((combos, pairs, LAGS), jnp.float32),
            jax.ShapeDtypeStruct((slots * CHANS, rows, LANES), jnp.bfloat16),
        ],
        scratch_shapes=[pltpu.VMEM((slots, CHANS * PHASES, 4 * LANES), jnp.bfloat16)],
        name="corr",
    )(pair_first, pair_second, arrived.reshape(slots * CHANS, chunks, LANES))
    parts = lax.all_gather(corr, "win")

    seen = jnp.transpose(observed, (1, 2, 0, 3)).reshape(combos, pairs, LAGS)
    offset = (lax.axis_index("win") * share).astype(jnp.int32).reshape(1)
    slot_adjoint, residual = pl.pallas_call(
        functools.partial(adjoint_kernel, corr_scale, adj_scale),
        in_specs=[smem(), smem(), smem(), vmem(), vmem(), vmem(), vmem(), vmem()],
        out_specs=[vmem(), vmem()],
        out_shape=[
            jax.ShapeDtypeStruct((slots * CHANS, chunks, LANES), jnp.bfloat16),
            jax.ShapeDtypeStruct((combos, share, LAGS), jnp.float32),
        ],
        scratch_shapes=[
            pltpu.VMEM((combos, pairs, LAGS), jnp.float32),
            pltpu.VMEM((combos * pairs, WINDOW), jnp.float32),
            pltpu.VMEM((combos * pairs, WINDOW), jnp.float32),
            pltpu.VMEM((slots, slots * CHANS * PHASES, DEPTH), jnp.bfloat16),
            pltpu.VMEM((slots * CHANS * PHASES, 4 * LANES), jnp.float32),
        ],
        compiler_params=pltpu.CompilerParams(vmem_limit_bytes=44 * 2**20),
        name="adjoint",
    )(
        pair_first, pair_second, offset, parts, seen,
        lag_lo.reshape(pairs, 1), lag_hi.reshape(pairs, 1), fan,
    )
    returned = lax.all_to_all(
        slot_adjoint.reshape(slots, CHANS, chunks, LANES),
        "stn", split_axis=0, concat_axis=0, tiled=True,
    )
    stacked = pl.pallas_call(
        unpack_kernel,
        grid_spec=pltpu.PrefetchScalarGridSpec(
            num_scalar_prefetch=1,
            grid=(CHANS,),
            in_specs=[pl.BlockSpec((slots, 1, chunks, LANES), lambda c, rows: (0, c, 0, 0))],
            out_specs=pl.BlockSpec((1, stations, samples), lambda c, rows: (c, 0, 0)),
            scratch_shapes=[pltpu.VMEM((chunks * stations, LANES), jnp.float32)],
        ),
        out_shape=jax.ShapeDtypeStruct((CHANS, stations, samples), jnp.bfloat16),
        name="unpack",
    )(send_rows, returned)
    station_adjoint = jnp.transpose(stacked.reshape(1, CHANS, stations, samples), (2, 0, 1, 3))
    residual = jnp.transpose(residual.reshape(CHANS, CHANS, share, LAGS), (2, 0, 1, 3))
    return (station_adjoint, residual)


def solution(mesh):
    placed = (
        P("stn", "win", None, None),
        P("stn", None, None, None),
        P("stn"),
        P("stn"),
        P("stn", None, None),
        P("stn"),
        P("stn"),
    )
    return jax.shard_map(
        shards,
        mesh=mesh,
        in_specs=placed,
        out_specs=(P("stn", "win", None, None), P(("stn", "win"), None, None, None)),
        check_vma=False,
    )
```

time: 670 us -> 81.6 us (0.12)
  matrix products: 444 us -> 0 us
  local copies, waits for them, and re-layouts: 96.7 us -> 3.85 us
  waiting for transfers between devices: 56.3 us -> 11.1 us
  other arithmetic: 42.8 us -> 0 us
  Pallas kernels: 0 us -> 32.9 us
  blocking collectives: 0 us -> 26.3 us
  between operations: 15.1 us -> 0.69 us
    dot_general x26 -> x0, matrix products: 444 us -> none  [the longest x5 156 us: second_terms(): return jnp.einsum('pwakf,pabf->pwbkf', data, source, precision=highest)]
    another operation x11 -> x0, local copies, waits for them, and re-layouts: 57.7 us -> none
    psum x1 -> x0, waiting for transfers between devices: 35.3 us -> none  [shards(): summed = lax.psum(partial_corr, 'win')]
    pallas_call x0 -> x4, Pallas kernels: none -> 32.9 us  [the longest x1 14.1 us: shards(): pl.pallas_call(corr_kernel, in_specs=[smem(), smem(), vmem()], out_specs=...]
    another operation x4 -> x0, other arithmetic: 30.2 us -> none
    all_to_all x0 -> x1, blocking collectives: none -> 15.6 us  [shards(): lax.all_to_all(slot_adjoint.reshape(slots, CHANS, chunks, LANES), 'stn',...]
    mul x3 -> x0, local copies, waits for them, and re-layouts: 13.9 us -> none  [the longest x1 4.67 us: shards(): src_cos_other = src_cos * other_cols]
    all_to_all x1 -> x0, waiting for transfers between devices: 13.9 us -> none  [shards(): lax.all_to_all(slot_adjoint, 'stn', split_axis=0, concat_axis=0, tiled=True)]
  transfers between devices with their start and end apart: 3 -> 1, of which waited for: 3 -> 1; matrix products, arithmetic and copies ran while one was open for 2% -> 2% of each run, Pallas kernels for 0% -> 0%
where the time goes in v1:
time: 81.6 us; the launch traced here: 81.1 us
  Pallas kernels  32.9 us (40%)
  blocking collectives  26.3 us (32%)
  waiting for transfers between devices  11.1 us (14%)
  starting transfers between devices  6.33 us (8%)
  local copies, waits for them, and re-layouts  3.85 us (5%)
    all_to_all x1, blocking collectives, shards(): lax.all_to_all(slot_adjoint.reshape(slots, CHANS, chunks, LANES), 'stn',...  15.6 us
    pallas_call x1, Pallas kernels, shards(): pl.pallas_call(corr_kernel, in_specs=[smem(), smem(), vmem()], out_specs=...  14.1 us
    pallas_call x1, Pallas kernels, shards(): pl.pallas_call(functools.partial(adjoint_kernel, corr_scale, adj_scale),...  11.3 us
    all_to_all x1, waiting for transfers between devices, shards(): lax.all_to_all(outgoing, 'stn', split_axis=0, concat_axis=0, tiled=True)  11.1 us
    all_gather x1, blocking collectives, shards(): parts = lax.all_gather(corr, 'win')  10.7 us
    all_to_all x1, starting transfers between devices, shards(): lax.all_to_all(outgoing, 'stn', split_axis=0, concat_axis=0, tiled=True)  6.33 us
    pallas_call x1, Pallas kernels, shards(): pl.pallas_call(unpack_kernel, grid_spec=pltpu.PrefetchScalarGridSpec(num_...  3.8 us
    pallas_call x1, Pallas kernels, shards(): pl.pallas_call(pack_kernel, grid_spec=pltpu.PrefetchScalarGridSpec(num_sc...  3.77 us
  transfers between devices with their start and end apart: 1, of which 1 were waited for; matrix products, arithmetic and copies ran while one was open for 2% of the time, Pallas kernels for 0%

profile of v1, /device:TPU:0, one launch (start us, length us, event | category | flops | bytes accessed | tf_op | source)
XLA Modules:
  0.0 81.1 jit_solution(9819120825587558285)
XLA Ops:
  0.6 0.0 copy-start.3
  0.6 0.0 copy-start.2
  0.7 0.0 copy-start.1
  0.7 3.8 %pack.1 = bf16[8,3,64,128]{3,2,1,0:T(8,128)(2,1)} custom-call(s32[8]{0:T(128)} %bitcast.25, bf16[3,16,8192]{2,1,0:T(8,128)(2,1)} %bitcast.23), custom_call_target="tpu_custom_call" | custom-call | tf_op jit(solution)/shard_map/pack/pallas_call | solution.py:228
  4.4 6.3 %all-to-all-start = ((bf16[8,3,64,128]{3,2,1,0:T(8,128)(2,1)}), bf16[8,3,64,128]{3,2,1,0:T(8,128)(2,1)S(1)}, u32[]{:S(2)}, u32[]{:S(2)}) async-start(bf16[8,3,64,128]{3,2,1,0:T(8,128)(2,1)} %pack.1), calls=%async_computation | async-start | bytes 786432 | tf_op jit(solution)/shard_map/all_to_all | solution.py:240
  10.8 0.7 copy.11.low_ref
  11.5 0.7 copy.12.high_ref
  12.2 11.1 %all-to-all-done = bf16[8,3,64,128]{3,2,1,0:T(8,128)(2,1)S(1)} async-done(((bf16[8,3,64,128]{3,2,1,0:T(8,128)(2,1)}), bf16[8,3,64,128]{3,2,1,0:T(8,128)(2,1)S(1)}, u32[]{:S(2)}, u32[]{:S(2)}) %all-to-all-start) | async-done | bytes 393248 | tf_op jit(solution)/shard_map/all_to_all | solution.py:240
  23.3 0.0 copy-start.4
  23.3 0.7 copy-done.4
  24.1 14.1 %corr.1 = (f32[9,16,256]{2,1,0:T(8,128)}, bf16[24,368,128]{2,1,0:T(8,128)(2,1)}) custom-call(s32[16]{0:T(128)} %first_ref.3, s32[16]{0:T(128)} %second_ref.3, bf16[24,64,128]{2,1,0:T(8,128)(2,1)} %bitcast.22), custom_call_target="tpu_custom_call" | custom-call | tf_op jit(solution)/shard_map/corr/pallas_call | solution.py:243
  38.1 10.7 %all-gather = f32[36,16,256]{2,1,0:T(8,128)S(1)} all-gather(f32[9,16,256]{2,1,0:T(8,128)} %get-tuple-element.6), channel_id=2, replica_groups=mesh['stn'=8,'win'=4] {'win'}, dimensions={0}, use_global_device_ids=true | all-gather | bytes 737280 | tf_op jit(solution)/shard_map/all_gather | solution.py:254
  48.8 0.0 copy-done.3
  48.8 0.0 copy-done.2
  48.8 0.0 copy-done.1
  48.8 0.0 copy-start
  48.8 1.6 %copy-done = bf16[24,368,128]{2,1,0:T(8,128)(2,1)S(1)} copy-done((bf16[24,368,128]{2,1,0:T(8,128)(2,1)S(1)}, bf16[24,368,128]{2,1,0:T(8,128)(2,1)}, u32[]{:S(2)}) %copy-start) | copy-done | bytes 2261016
  50.4 11.3 %adjoint.1 = (bf16[24,64,128]{2,1,0:T(8,128)(2,1)S(1)}, f32[9,4,256]{2,1,0:T(4,128)}) custom-call(s32[16]{0:T(128)S(1)} %copy-done.2, s32[16]{0:T(128)S(1)} %copy-done.3, s32[1]{0:T(128)} %bitcast.1.offset_ref, f32[4,9,16,256]{3,2,1,0:T(8,128)S(1)} %bitcast.19, f32[9,16,256]{2,1,0:T(8,128)S(1)} %bitcast.21, s32[16,1]{1,0:T(8,128)S(1)} %copy.11.low_ref, ...), custom_call_target="tpu_custom_call" | custom-call | tf_op jit(solution)/shard_map/adjoint/pallas_call | solution.py:258
  61.7 15.6 %all_to_all.10.ret_ref = bf16[8,3,64,128]{3,2,1,0:T(8,128)(2,1)} all-to-all(bf16[8,3,64,128]{3,2,1,0:T(8,128)(2,1)S(1)} %bitcast.20), channel_id=1, replica_groups=mesh['stn'=8,'win'=4] {'stn'}, dimensions={0} | all-to-all | bytes 786432 | tf_op jit(solution)/shard_map/all_to_all | solution.py:279
  77.3 3.8 %unpack.1 = bf16[3,16,8192]{2,1,0:T(8,128)(2,1)} custom-call(s32[8]{0:T(128)} %bitcast.26, bf16[8,3,64,128]{3,2,1,0:T(8,128)(2,1)} %all_to_all.10.ret_ref), custom_call_target="tpu_custom_call" | custom-call | tf_op jit(solution)/shard_map/unpack/pallas_call | solution.py:283
Async XLA Ops:
  0.6 48.1 %copy-start.3 = (s32[16]{0:T(128)S(1)}, s32[16]{0:T(128)}, u32[]{:S(2)}) copy-start(s32[16]{0:T(128)} %second_ref.3) | copy-start | bytes 196
  0.6 48.1 %copy-start.2 = (s32[16]{0:T(128)S(1)}, s32[16]{0:T(128)}, u32[]{:S(2)}) copy-start(s32[16]{0:T(128)} %first_ref.3) | copy-start | bytes 196
  0.7 48.1 %copy-start.1 = (f32[16,3,3,256]{3,0,2,1:T(8,128)S(1)}, f32[16,3,3,256]{3,0,2,1:T(8,128)}, u32[]{:S(2)}) copy-start(f32[16,3,3,256]{3,0,2,1:T(8,128)} %param.8) | copy-start | bytes 442372
  4.4 18.9 %all-to-all-start = ((bf16[8,3,64,128]{3,2,1,0:T(8,128)(2,1)}), bf16[8,3,64,128]{3,2,1,0:T(8,128)(2,1)S(1)}, u32[]{:S(2)}, u32[]{:S(2)}) async-start(bf16[8,3,64,128]{3,2,1,0:T(8,128)(2,1)} %pack.1), calls=%async_computation | async-start | bytes 786432 | tf_op jit(solution)/shard_map/all_to_all | solution.py:240
  23.3 0.7 copy-start.4
  48.8 1.6 %copy-start = (bf16[24,368,128]{2,1,0:T(8,128)(2,1)S(1)}, bf16[24,368,128]{2,1,0:T(8,128)(2,1)}, u32[]{:S(2)}) copy-start(bf16[24,368,128]{2,1,0:T(8,128)(2,1)} %get-tuple-element.7.fan_ref) | copy-start | bytes 6782980

commit v2 on v1

v2 whole, which is shorter than its diff:
```python
import functools
import math

import jax
import jax.numpy as jnp
from jax import lax
from jax.experimental import pallas as pl
from jax.experimental.pallas import tpu as pltpu
from jax.sharding import PartitionSpec as P

LAGS = 256
HALF = LAGS // 2
LANES = 128
HALF_TILE = LANES // 2
PHASES = 16
WIDE = 32
CHANS = 3
WINDOW = 3 * LANES
DEPTH = 7 * LANES


def pack_kernel(rows_ref, rec_ref, swap_ref, *refs):
    keep_refs = refs[:-3]
    buffer, scratch, sems = refs[-3:]
    me = lax.axis_index("stn")
    stations = rec_ref.shape[1]
    chunks = rec_ref.shape[2] // LANES
    copies = [
        pltpu.make_async_copy(rec_ref.at[c], buffer.at[c], sems.at[c]) for c in range(CHANS)
    ]
    for copy in copies:
        copy.start()
    for c in range(CHANS):
        copies[c].wait()
        for r in range(chunks):
            piece = buffer[c, :, r * LANES:(r + 1) * LANES]
            scratch[c, r * stations:(r + 1) * stations, :] = piece.astype(jnp.float32)
        for j, keep_ref in enumerate(keep_refs):
            for i, ref in enumerate((keep_ref, swap_ref.at[j])):
                station = rows_ref[me ^ (2 * j + i)]
                picked = scratch[c, pl.ds(station, chunks, stride=stations), :]
                ref[c] = picked.astype(jnp.bfloat16)


def unpack_kernel(order, rows_ref, *refs):
    returned = refs[:-4]
    out_ref, buffer, scratch, sems = refs[-4:]
    me = lax.axis_index("stn")
    stations = out_ref.shape[1]
    chunks = out_ref.shape[2] // LANES
    copies = []
    for c in range(CHANS):
        scratch[c] = jnp.zeros_like(scratch[c])
        pieces = [(2 * j + i, ref.at[i]) for j, ref in zip(order, returned[:-2]) for i in range(2)]
        for j, ref in pieces + [(0, returned[-2]), (1, returned[-1])]:
            where = pl.ds(rows_ref[me ^ j], chunks, stride=stations)
            scratch[c, where, :] = scratch[c, where, :] + ref[c].astype(jnp.float32)
        for r in range(chunks):
            piece = scratch[c, r * stations:(r + 1) * stations, :]
            buffer[c, :, r * LANES:(r + 1) * LANES] = piece.astype(jnp.bfloat16)
        copies.append(pltpu.make_async_copy(buffer.at[c], out_ref.at[c], sems.at[c]))
        copies[c].start()
    for copy in copies:
        copy.wait()


def build_phases(slot_refs, fan_ref):
    chunks = slot_refs[0].shape[1]
    rows = fan_ref.shape[1]
    lane = lax.broadcasted_iota(jnp.int32, (LANES, LANES), 1)
    left = lax.broadcasted_iota(jnp.int32, (rows, LANES), 1) < chunks
    for place in range(0, CHANS * len(slot_refs), 2):
        pair = [slot_refs[e // CHANS][e % CHANS] for e in (place, place + 1)]
        middle = jnp.concatenate(pair, axis=0).astype(jnp.float32).T
        before = jnp.where(lane % chunks == 0, 0.0, pltpu.roll(middle, 1, 1))
        after = jnp.where(lane % chunks == chunks - 1, 0.0, pltpu.roll(middle, LANES - 1, 1))
        wide = jnp.concatenate([before, middle, after], axis=0)
        swapped = pltpu.roll(wide, chunks, 1)
        one = jnp.where(left, wide[:rows], swapped[HALF_TILE:])
        two = jnp.where(left, swapped[:rows], wide[HALF_TILE:])
        fan_ref[place] = one.astype(jnp.bfloat16)
        fan_ref[place + 1] = two.astype(jnp.bfloat16)


def shifted_rows(fan_ref, slot, phases):
    span = LAGS + phases
    tail = DEPTH - CHANS * span
    columns = []
    for first in range(0, HALF_TILE, phases):
        parts = [fan_ref[CHANS * slot + b, first:first + span, :] for b in range(CHANS)]
        parts.append(fan_ref[CHANS * slot, first:first + tail, :])
        columns.append(jnp.concatenate(parts, axis=0))
    return jnp.concatenate(columns, axis=1)


def fetch(sources, targets, sems):
    copies = [pltpu.make_async_copy(s, t, sems.at[k]) for k, (s, t) in enumerate(zip(sources, targets))]
    for copy in copies:
        copy.start()
    return copies


def corr_kernel(order, first_in, second_in, *refs):
    given = refs[:-6]
    corr_ref, fan_ref, heads, first_ref, second_ref, sems = refs[-6:]
    copies = fetch((first_in, second_in), (first_ref, second_ref), sems)
    me = lax.axis_index("stn")
    slot_refs = [None] * (2 * len(given) - 2)
    for j, ref in zip(order, given[:-2]):
        slot_refs[2 * j:2 * j + 2] = [ref.at[0], ref.at[1]]
    slot_refs[:2] = given[-2:]
    build_phases(slot_refs, fan_ref)
    height = CHANS * WIDE
    row = lax.broadcasted_iota(jnp.int32, (height, height), 0)
    column = lax.broadcasted_iota(jnp.int32, (height, height), 1)
    same = row // WIDE == column // WIDE
    flip = (same & (row % WIDE + column % WIDE == WIDE - 1)).astype(jnp.bfloat16)

    def head(q, carry):
        rows = []
        for a in range(CHANS):
            pieces = []
            for m in range(0, HALF_TILE, WIDE):
                pieces.append(fan_ref[CHANS * q + a, HALF + m:HALF + m + WIDE, :])
            rows.append(jnp.concatenate(pieces, axis=1))
        natural = jnp.concatenate(rows, axis=0)
        heads[q] = jnp.dot(flip, natural, preferred_element_type=jnp.float32).astype(jnp.bfloat16)
        return carry

    lax.fori_loop(0, heads.shape[0], head, 0, unroll=8)
    for copy in copies:
        copy.wait()

    def step(p, carry):
        right = shifted_rows(fan_ref, second_ref[p] ^ me, WIDE)
        products = lax.dot_general(
            heads[first_ref[p] ^ me], right, (((1,), (1,)), ((), ())),
            preferred_element_type=jnp.float32,
        )
        for a in range(CHANS):
            for b in range(CHANS):
                block = products[WIDE * a:WIDE * (a + 1), LAGS * b:LAGS * b + WINDOW]
                shift = WINDOW - WIDE * b - (WIDE - 1)
                turned = pltpu.roll(block, shift, 1, stride=1, stride_axis=0)
                corr_ref[CHANS * a + b, pl.ds(p, 1), :] = jnp.sum(
                    turned[:, :LAGS], axis=0, keepdims=True
                )
        return carry

    lax.fori_loop(0, corr_ref.shape[1], step, 0, unroll=8)


def spread(lag_rows, base, stride_rows):
    turned = []
    for c in range(CHANS):
        row = lag_rows[pl.ds(base + stride_rows * c, 1), :]
        block = jnp.broadcast_to(row, (PHASES, WINDOW))
        turned.append(pltpu.roll(block, PHASES * c, 1, stride=1, stride_axis=0))
    w0, w1, w2 = turned
    return jnp.concatenate(
        [
            w0[:, :LAGS],
            w0[:, LAGS:] + w1[:, :LANES],
            w1[:, LANES:LAGS],
            w1[:, LAGS:] + w2[:, :LANES],
            w2[:, LANES:],
        ],
        axis=1,
    ).astype(jnp.bfloat16)


def pairwise(terms):
    while len(terms) > 1:
        terms = [sum(terms[k + 1:k + 2], terms[k]) for k in range(0, len(terms), 2)]
    return terms[0]


def adjoint_kernel(
    corr_scale, adj_scale, first_in, second_in, low_in, high_in, observed_ref, fan_ref, *refs
):
    first_ref, second_ref, low_ref, high_ref, sems = refs[-5:]
    refs = refs[:-5]
    copies = fetch(
        (first_in, second_in, low_in, high_in), (first_ref, second_ref, low_ref, high_ref), sems
    )
    me = lax.axis_index("stn")
    chips = fan_ref.shape[0] // (2 * CHANS)
    part_refs = refs[:-chips - 7]
    keep_refs = refs[-chips - 7:-7]
    swap_ref, share_ref, resid, forward, backward, bands, total = refs[-7:]
    pairs = observed_ref.shape[1]
    combos = observed_ref.shape[0]
    slots = bands.shape[0]
    lag = lax.broadcasted_iota(jnp.int32, (pairs, LAGS), 1)
    bands[...] = jnp.zeros_like(bands)
    for copy in copies:
        copy.wait()
    row = lax.broadcasted_iota(jnp.int32, (pairs, LAGS), 0)
    low = jnp.zeros_like(row)
    high = jnp.zeros_like(row)
    for p in range(pairs):
        low = jnp.where(row == p, low_ref[p], low)
        high = jnp.where(row == p, high_ref[p], high)
    inside = (lag >= low) & (lag < high)
    offset = lax.axis_index("win") * share_ref.shape[1]
    flip = (
        lax.broadcasted_iota(jnp.int32, (LAGS, WINDOW), 0)
        + lax.broadcasted_iota(jnp.int32, (LAGS, WINDOW), 1)
        == LAGS
    ).astype(jnp.bfloat16)
    forward[...] = jnp.zeros_like(forward)
    for i in range(combos):
        summed = pairwise([ref[i] for ref in part_refs])
        value = jnp.where(inside, summed * corr_scale - observed_ref[i], 0.0)
        resid[i] = value
        rounded = value.astype(jnp.bfloat16)
        forward[i * pairs:(i + 1) * pairs, :LAGS] = rounded.astype(jnp.float32)
        backward[i * pairs:(i + 1) * pairs, :] = jnp.dot(
            rounded, flip, preferred_element_type=jnp.float32
        )
        for j in range(share_ref.shape[1]):
            share_ref[i, j:j + 1, :] = resid[i, pl.ds(offset + j, 1), :]

    height = CHANS * PHASES

    def row_place(q):
        return q // 2 + (slots // 2) * (1 - q % 2)

    def fill(p, carry):
        qf = first_ref[p] ^ me
        qs = second_ref[p] ^ me
        for c in range(CHANS):
            start = pl.multiple_of(height * row_place(qf) + PHASES * c, PHASES)
            bands[qs, pl.ds(start, PHASES), :] = spread(forward, CHANS * pairs * c + p, pairs)
            start = pl.multiple_of(height * row_place(qs) + PHASES * c, PHASES)
            bands[qf, pl.ds(start, PHASES), :] = spread(backward, pairs * c + p, CHANS * pairs)
        return carry

    lax.fori_loop(0, pairs, fill, 0, unroll=8)
    total[...] = jnp.zeros_like(total)

    def accumulate(r, carry):
        right = shifted_rows(fan_ref, r, PHASES)
        total[...] += jnp.dot(bands[r], right, preferred_element_type=jnp.float32)
        return carry

    lax.fori_loop(0, slots, accumulate, 0, unroll=8)
    chunks = swap_ref.shape[2]
    left = lax.broadcasted_iota(jnp.int32, (PHASES, LANES), 1) < chunks
    outs = [swap_ref.at[j] for j in range(chips)] + list(keep_refs)
    for place in range(0, CHANS * slots, 2):
        upper = []
        lower = []
        for m in range(4):
            columns = slice(m * LANES, (m + 1) * LANES)
            one = total[place * PHASES:(place + 1) * PHASES, columns]
            two = total[(place + 1) * PHASES:(place + 2) * PHASES, columns]
            upper.append(jnp.where(left, one, pltpu.roll(two, chunks, 1)))
            lower.append(jnp.where(left, pltpu.roll(one, chunks, 1), two))
        tile = (jnp.concatenate(upper + lower, axis=0).T * adj_scale).astype(jnp.bfloat16)
        for k in range(2):
            e = place + k
            outs[e // CHANS][e % CHANS] = tile[k * chunks:(k + 1) * chunks]


def smem():
    return pl.BlockSpec(memory_space=pltpu.SMEM)


def vmem():
    return pl.BlockSpec(memory_space=pltpu.VMEM)


def flipped(x, axis, bits):
    count = lax.axis_size(axis)
    return lax.ppermute(x, axis, [(k, k ^ bits) for k in range(count)])


def across(swap, keep):
    chips = len(keep)
    got = flipped(swap, "stn", 1)
    order = []
    blocks = []
    for j in range(chips - 1, 0, -1):
        moved = flipped(jnp.stack([keep[j], got[j]]), "stn", 2 * j)
        order.append(j)
        blocks.append(moved)
    return order + [0, 0], blocks + [keep[0], got[0]]


def window_parts(corr):
    groups = lax.axis_size("win")
    if groups > 4:
        gathered = lax.all_gather(corr, "win")
        return [gathered[w] for w in range(groups)]
    return [corr] + [flipped(corr, "win", w) for w in range(1, groups)]


def shards(records, observed, lag_lo, lag_hi, send_table, pair_first, pair_second):
    owner_count = lax.axis_size("stn")
    window_groups = lax.axis_size("win")
    stations, local_windows, _, samples = records.shape
    send_rows = send_table.reshape(-1)
    slots = send_rows.shape[0]
    chunks = samples // LANES
    pairs = observed.shape[0]
    combos = CHANS * CHANS
    share = pairs // window_groups
    corr_scale = 1.0 / math.sqrt(samples * local_windows * window_groups)
    adj_scale = 1.0 / math.sqrt(CHANS * LAGS)

    chips = slots // 2
    block = jax.ShapeDtypeStruct((CHANS, chunks, LANES), jnp.bfloat16)
    blocks = jax.ShapeDtypeStruct((chips, CHANS, chunks, LANES), jnp.bfloat16)
    any_space = pl.BlockSpec(memory_space=pltpu.HBM)
    planes = jnp.transpose(records, (1, 2, 0, 3)).reshape(CHANS, stations, samples)
    planes = pltpu.with_memory_space_constraint(planes, pltpu.HBM)
    send_rows, pair_first, pair_second, lag_lo, lag_hi = [
        pltpu.with_memory_space_constraint(x, pltpu.HBM)
        for x in (send_rows, pair_first, pair_second, lag_lo, lag_hi)
    ]
    swap, *keep = pl.pallas_call(
        pack_kernel,
        in_specs=[smem(), any_space],
        out_specs=[vmem()] * (1 + chips),
        out_shape=[blocks] + [block] * chips,
        scratch_shapes=[
            pltpu.VMEM((CHANS, stations, samples), jnp.bfloat16),
            pltpu.VMEM((CHANS, chunks * stations, LANES), jnp.float32),
            pltpu.SemaphoreType.DMA((CHANS,)),
        ],
        compiler_params=pltpu.CompilerParams(vmem_limit_bytes=8 * 2**20),
        name="pack",
    )(send_rows, planes)
    order, arrived = across(swap, keep)

    rows = 3 * LANES - HALF_TILE
    corr, fan = pl.pallas_call(
        functools.partial(corr_kernel, order),
        in_specs=[any_space] * 2 + [vmem()] * (chips + 1),
        out_specs=[vmem(), vmem()],
        out_shape=[
            jax.ShapeDtypeStruct((combos, pairs, LAGS), jnp.float32),
            jax.ShapeDtypeStruct((slots * CHANS, rows, LANES), jnp.bfloat16),
        ],
        scratch_shapes=[
            pltpu.VMEM((slots, CHANS * WIDE, HALF_TILE // WIDE * LANES), jnp.bfloat16),
            pltpu.SMEM((pairs,), jnp.int32),
            pltpu.SMEM((pairs,), jnp.int32),
            pltpu.SemaphoreType.DMA((2,)),
        ],
        compiler_params=pltpu.CompilerParams(vmem_limit_bytes=16 * 2**20),
        name="corr",
    )(pair_first, pair_second, *arrived)
    parts = window_parts(corr)

    seen = jnp.transpose(observed, (1, 2, 0, 3)).reshape(combos, pairs, LAGS)
    *keep, swap, residual = pl.pallas_call(
        functools.partial(adjoint_kernel, corr_scale, adj_scale),
        in_specs=[any_space] * 4 + [vmem()] * (2 + len(parts)),
        out_specs=[vmem()] * (chips + 2),
        out_shape=[block] * chips
        + [blocks, jax.ShapeDtypeStruct((combos, share, LAGS), jnp.float32)],
        scratch_shapes=[
            pltpu.VMEM((combos, pairs, LAGS), jnp.float32),
            pltpu.VMEM((combos * pairs, WINDOW), jnp.float32),
            pltpu.VMEM((combos * pairs, WINDOW), jnp.float32),
            pltpu.VMEM((slots, slots * CHANS * PHASES, DEPTH), jnp.bfloat16),
            pltpu.VMEM((slots * CHANS * PHASES, 4 * LANES), jnp.float32),
            pltpu.SMEM((pairs,), jnp.int32),
            pltpu.SMEM((pairs,), jnp.int32),
            pltpu.SMEM((pairs,), jnp.int32),
            pltpu.SMEM((pairs,), jnp.int32),
            pltpu.SemaphoreType.DMA((4,)),
        ],
        compiler_params=pltpu.CompilerParams(vmem_limit_bytes=44 * 2**20),
        name="adjoint",
    )(
        pair_first, pair_second, lag_lo, lag_hi, seen, fan, *parts,
    )
    order, returned = across(swap, keep)
    stacked = pl.pallas_call(
        functools.partial(unpack_kernel, order),
        in_specs=[smem()] + [vmem()] * (chips + 1),
        out_specs=any_space,
        out_shape=jax.ShapeDtypeStruct((CHANS, stations, samples), jnp.bfloat16),
        scratch_shapes=[
            pltpu.VMEM((CHANS, stations, samples), jnp.bfloat16),
            pltpu.VMEM((CHANS, chunks * stations, LANES), jnp.float32),
            pltpu.SemaphoreType.DMA((CHANS,)),
        ],
        compiler_params=pltpu.CompilerParams(vmem_limit_bytes=8 * 2**20),
        name="unpack",
    )(send_rows, *returned)
    station_adjoint = jnp.transpose(stacked.reshape(1, CHANS, stations, samples), (2, 0, 1, 3))
    residual = jnp.transpose(residual.reshape(CHANS, CHANS, share, LAGS), (2, 0, 1, 3))
    return (station_adjoint, residual)


def solution(mesh):
    placed = (
        P("stn", "win", None, None),
        P("stn", None, None, None),
        P("stn"),
        P("stn"),
        P("stn", None, None),
        P("stn"),
        P("stn"),
    )
    return jax.shard_map(
        shards,
        mesh=mesh,
        in_specs=placed,
        out_specs=(P("stn", "win", None, None), P(("stn", "win"), None, None, None)),
        check_vma=False,
    )
```

time: 81.6 us -> 53.8 us (0.66)
  blocking collectives: 26.3 us -> 0 us
  Pallas kernels: 32.9 us -> 15.7 us
  waiting for transfers between devices: 11.1 us -> 22.6 us
  starting transfers between devices: 6.33 us -> 14.4 us
  local copies, waits for them, and re-layouts: 3.85 us -> 0.03 us
    ppermute x0 -> x11, waiting for transfers between devices: none -> 22.6 us  [flipped(): return lax.ppermute(x, axis, [(k, k ^ bits) for k in range(count)])]
    all_to_all x1 -> x0, blocking collectives: 15.6 us -> none  [shards(): lax.all_to_all(slot_adjoint.reshape(slots, CHANS, chunks, LANES), 'stn',...]
    ppermute x0 -> x11, starting transfers between devices: none -> 14.4 us  [flipped(): return lax.ppermute(x, axis, [(k, k ^ bits) for k in range(count)])]
    pallas_call x3, Pallas kernels: 21.6 us -> 9.05 us  [the longest x1 4.61 us: shards(): pl.pallas_call(functools.partial(corr_kernel, order), in_specs=[any_space...]
    all_to_all x1 -> x0, waiting for transfers between devices: 11.1 us -> none  [shards(): lax.all_to_all(outgoing, 'stn', split_axis=0, concat_axis=0, tiled=True)]
    all_gather x1 -> x0, blocking collectives: 10.7 us -> none  [shards(): parts = lax.all_gather(corr, 'win')]
    all_to_all x1 -> x0, starting transfers between devices: 6.33 us -> none  [shards(): lax.all_to_all(outgoing, 'stn', split_axis=0, concat_axis=0, tiled=True)]
    pallas_call x1, Pallas kernels: 11.3 us -> 6.66 us  [shards(): pl.pallas_call(functools.partial(adjoint_kernel, corr_scale, adj_scale),...]
  transfers between devices with their start and end apart: 1 -> 11, of which waited for: 1 -> 9; matrix products, arithmetic and copies ran while one was open for 2% -> 0% of each run, Pallas kernels for 0% -> 0%
where the time goes in v2:
time: 53.8 us; the launch traced here: 53.6 us
  waiting for transfers between devices  22.6 us (42%)
  Pallas kernels  15.7 us (29%)
  starting transfers between devices  14.4 us (27%)
  between operations  0.74 us (1%)
    ppermute x11, waiting for transfers between devices, flipped(): return lax.ppermute(x, axis, [(k, k ^ bits) for k in range(count)])  22.6 us
    ppermute x11, starting transfers between devices, flipped(): return lax.ppermute(x, axis, [(k, k ^ bits) for k in range(count)])  14.4 us
    pallas_call x1, Pallas kernels, shards(): pl.pallas_call(functools.partial(adjoint_kernel, corr_scale, adj_scale),...  6.66 us
    pallas_call x1, Pallas kernels, shards(): pl.pallas_call(functools.partial(corr_kernel, order), in_specs=[any_space...  4.61 us
    pallas_call x1, Pallas kernels, shards(): pl.pallas_call(pack_kernel, in_specs=[smem(), any_space], out_specs=[vmem...  2.3 us
    pallas_call x1, Pallas kernels, shards(): pl.pallas_call(functools.partial(unpack_kernel, order), in_specs=[smem()]...  2.14 us
  transfers between devices with their start and end apart: 11, of which 9 were waited for; matrix products, arithmetic and copies ran while one was open for 0% of the time, Pallas kernels for 0%

profile of v2, /device:TPU:0, one launch (start us, length us, event | category | flops | bytes accessed | tf_op | source)
XLA Modules:
  0.0 53.6 jit_solution(250593955172659979)
XLA Ops:
  0.6 0.0 copy-start
  0.6 2.3 %pack.1 = (bf16[4,3,64,128]{3,2,1,0:T(8,128)(2,1)S(1)}, bf16[3,64,128]{2,1,0:T(8,128)(2,1)S(1)}, bf16[3,64,128]{2,1,0:T(8,128)(2,1)S(1)}, bf16[3,64,128]{2,1,0:T(8,128)(2,1)S(1)}, bf16[3,64,128]{2,1,0:T(8,128)(2,1)S(1)}) custom-call(s32[8]{0:T(128)} %bitcast.32, bf16[3,16,8192]{2,1,0:T(8,128)(2,1)} %bitcast.30), custom_call_target="tpu_custom_call" | custom-call | tf_op jit(solution)/shard_map/pack/pallas_call | solution.py:322
  2.9 0.5 collective-permute-start
  3.5 1.1 %collective-permute-done = bf16[4,3,64,128]{3,2,1,0:T(8,128)(2,1)S(1)} collective-permute-done((bf16[4,3,64,128]{3,2,1,0:T(8,128)(2,1)S(1)}, bf16[4,3,64,128]{3,2,1,0:T(8,128)(2,1)S(1)}, u32[]{:S(2)}, u32[]{:S(2)}) %collective-permute-start) | collective-permute-done | bytes 196640 | tf_op jit(solution)/shard_map/ppermute | solution.py:276
  4.6 5.0 %collective-permute-start.1 = (bf16[2,3,64,128]{3,2,1,0:T(8,128)(2,1)S(1)}, bf16[2,3,64,128]{3,2,1,0:T(8,128)(2,1)S(1)}, u32[]{:S(2)}, u32[]{:S(2)}) collective-permute-start(bf16[2,3,64,128]{3,2,1,0:T(8,128)(2,1)S(1)} %pad_maximum_fusion), channel_id=1, source_target_pairs={{0,24},{4,28},{8,16},{12,20},{16,8},{20,12},{24,0},{28,4},{1,25},{... | collective-permute-start | bytes 294920 | tf_op jit(solution)/shard_map/ppermute | solution.py:276
  9.6 0.1 collective-permute-start.2
  9.7 0.6 %collective-permute-start.3 = (bf16[2,3,64,128]{3,2,1,0:T(8,128)(2,1)S(1)}, bf16[2,3,64,128]{3,2,1,0:T(8,128)(2,1)S(1)}, u32[]{:S(2)}, u32[]{:S(2)}) collective-permute-start(bf16[2,3,64,128]{3,2,1,0:T(8,128)(2,1)S(1)} %pad_maximum_fusion.2), channel_id=1, source_target_pairs={{0,8},{4,12},{8,0},{12,4},{16,24},{20,28},{24,16},{28,20},{1,9},{5... | collective-permute-start | bytes 294920 | tf_op jit(solution)/shard_map/ppermute | solution.py:276
  10.3 2.9 %collective-permute-done.1.refs_0_ = bf16[2,3,64,128]{3,2,1,0:T(8,128)(2,1)S(1)} collective-permute-done((bf16[2,3,64,128]{3,2,1,0:T(8,128)(2,1)S(1)}, bf16[2,3,64,128]{3,2,1,0:T(8,128)(2,1)S(1)}, u32[]{:S(2)}, u32[]{:S(2)}) %collective-permute-start.1) | collective-permute-done | bytes 98336 | tf_op jit(solution)/shard_map/ppermute | solution.py:276
  13.3 4.9 %collective-permute-done.2.refs_1_ = bf16[2,3,64,128]{3,2,1,0:T(8,128)(2,1)S(1)} collective-permute-done((bf16[2,3,64,128]{3,2,1,0:T(8,128)(2,1)S(1)}, bf16[2,3,64,128]{3,2,1,0:T(8,128)(2,1)S(1)}, u32[]{:S(2)}, u32[]{:S(2)}) %collective-permute-start.2) | collective-permute-done | bytes 98336 | tf_op jit(solution)/shard_map/ppermute | solution.py:276
  18.2 0.0 collective-permute-done.3.refs_2_
  18.2 4.6 %corr.1 = (f32[9,16,256]{2,1,0:T(8,128)S(1)}, bf16[24,320,128]{2,1,0:T(8,128)(2,1)S(1)}) custom-call(s32[16]{0:T(128)} %first_in.3, s32[16]{0:T(128)} %second_in.3, bf16[2,3,64,128]{3,2,1,0:T(8,128)(2,1)S(1)} %collective-permute-done.1.refs_0_, bf16[2,3,64,128]{3,2,1,0:T(8,128)(2,1)S(1)} %collective-permute-done.2.refs_1_, ...), custom_call_target="tpu_custom_call" | custom-call | tf_op jit(solution)/shard_map/corr/pallas_call | solution.py:338
  22.8 2.5 %collective-permute-start.6 = (f32[9,16,256]{2,1,0:T(8,128)S(1)}, f32[9,16,256]{2,1,0:T(8,128)S(1)}, u32[]{:S(2)}, u32[]{:S(2)}) collective-permute-start(f32[9,16,256]{2,1,0:T(8,128)S(1)} %get-tuple-element.21.refs_0_), channel_id=1, source_target_pairs={{0,3},{1,2},{2,1},{3,0},{4,7},{5,6},{6,5},{7,4},{8,11},{9,10},{10,... | collective-permute-start | bytes 442376 | tf_op jit(solution)/shard_map/ppermute | solution.py:276
  25.3 0.5 collective-permute-start.5
  25.8 0.5 %collective-permute-start.4 = (f32[9,16,256]{2,1,0:T(8,128)S(1)}, f32[9,16,256]{2,1,0:T(8,128)S(1)}, u32[]{:S(2)}, u32[]{:S(2)}) collective-permute-start(f32[9,16,256]{2,1,0:T(8,128)S(1)} %get-tuple-element.21.refs_0_), channel_id=1, source_target_pairs={{0,1},{1,0},{2,3},{3,2},{4,5},{5,4},{6,7},{7,6},{8,9},{9,8},{10,11... | collective-permute-start | bytes 442376 | tf_op jit(solution)/shard_map/ppermute | solution.py:276
  26.4 3.4 %collective-permute-done.6.refs_3_ = f32[9,16,256]{2,1,0:T(8,128)S(1)} collective-permute-done((f32[9,16,256]{2,1,0:T(8,128)S(1)}, f32[9,16,256]{2,1,0:T(8,128)S(1)}, u32[]{:S(2)}, u32[]{:S(2)}) %collective-permute-start.6) | collective-permute-done | bytes 147488 | tf_op jit(solution)/shard_map/ppermute | solution.py:276
  29.7 2.2 %collective-permute-done.5.refs_2_ = f32[9,16,256]{2,1,0:T(8,128)S(1)} collective-permute-done((f32[9,16,256]{2,1,0:T(8,128)S(1)}, f32[9,16,256]{2,1,0:T(8,128)S(1)}, u32[]{:S(2)}, u32[]{:S(2)}) %collective-permute-start.5) | collective-permute-done | bytes 147488 | tf_op jit(solution)/shard_map/ppermute | solution.py:276
  32.0 0.1 collective-permute-done.4.refs_1_
  32.0 0.0 copy-done
  32.0 6.7 %adjoint.1 = (bf16[3,64,128]{2,1,0:T(8,128)(2,1)S(1)}, bf16[3,64,128]{2,1,0:T(8,128)(2,1)S(1)}, bf16[3,64,128]{2,1,0:T(8,128)(2,1)S(1)}, bf16[3,64,128]{2,1,0:T(...) custom-call(s32[16]{0:T(128)} %first_in.3, s32[16]{0:T(128)} %second_in.3, s32[16]{0:T(128)} %low_in.1, ...), custom_call_target="tpu_custom_call" | custom-call | tf_op jit(solution)/shard_map/adjoint/pallas_call | solution.py:358
  38.7 0.1 collective-permute-start.7
  38.8 1.4 %collective-permute-done.7 = bf16[4,3,64,128]{3,2,1,0:T(8,128)(2,1)S(1)} collective-permute-done((bf16[4,3,64,128]{3,2,1,0:T(8,128)(2,1)S(1)}, bf16[4,3,64,128]{3,2,1,0:T(8,128)(2,1)S(1)}, u32[]{:S(2)}, u32[]{:S(2)}) %collective-permute-start.7) | collective-permute-done | bytes 196640 | tf_op jit(solution)/shard_map/ppermute | solution.py:276
  40.3 2.5 %collective-permute-start.8 = (bf16[2,3,64,128]{3,2,1,0:T(8,128)(2,1)S(1)}, bf16[2,3,64,128]{3,2,1,0:T(8,128)(2,1)S(1)}, u32[]{:S(2)}, u32[]{:S(2)}) collective-permute-start(bf16[2,3,64,128]{3,2,1,0:T(8,128)(2,1)S(1)} %pad_maximum_fusion.3), channel_id=1, source_target_pairs={{0,24},{4,28},{8,16},{12,20},{16,8},{20,12},{24,0},{28,4},{1,25},{... | collective-permute-start | bytes 294920 | tf_op jit(solution)/shard_map/ppermute | solution.py:276
  42.8 0.1 collective-permute-start.9
  42.9 2.0 %collective-permute-start.10 = (bf16[2,3,64,128]{3,2,1,0:T(8,128)(2,1)S(1)}, bf16[2,3,64,128]{3,2,1,0:T(8,128)(2,1)S(1)}, u32[]{:S(2)}, u32[]{:S(2)}) collective-permute-start(bf16[2,3,64,128]{3,2,1,0:T(8,128)(2,1)S(1)} %pad_maximum_fusion.5), channel_id=1, source_target_pairs={{0,8},{4,12},{8,0},{12,4},{16,24},{20,28},{24,16},{28,20},{1,9},{5... | collective-permute-start | bytes 294920 | tf_op jit(solution)/shard_map/ppermute | solution.py:276
  44.9 3.0 %collective-permute-done.8.refs_0_ = bf16[2,3,64,128]{3,2,1,0:T(8,128)(2,1)S(1)} collective-permute-done((bf16[2,3,64,128]{3,2,1,0:T(8,128)(2,1)S(1)}, bf16[2,3,64,128]{3,2,1,0:T(8,128)(2,1)S(1)}, u32[]{:S(2)}, u32[]{:S(2)}) %collective-permute-start.8) | collective-permute-done | bytes 98336 | tf_op jit(solution)/shard_map/ppermute | solution.py:276
  47.9 3.6 %collective-permute-done.9.refs_1_ = bf16[2,3,64,128]{3,2,1,0:T(8,128)(2,1)S(1)} collective-permute-done((bf16[2,3,64,128]{3,2,1,0:T(8,128)(2,1)S(1)}, bf16[2,3,64,128]{3,2,1,0:T(8,128)(2,1)S(1)}, u32[]{:S(2)}, u32[]{:S(2)}) %collective-permute-start.9) | collective-permute-done | bytes 98336 | tf_op jit(solution)/shard_map/ppermute | solution.py:276
  51.4 0.0 collective-permute-done.10.refs_2_
  51.4 2.1 %unpack.1 = bf16[3,16,8192]{2,1,0:T(8,128)(2,1)} custom-call(s32[8]{0:T(128)} %bitcast.33, bf16[2,3,64,128]{3,2,1,0:T(8,128)(2,1)S(1)} %collective-permute-done.8.refs_0_, bf16[2,3,64,128]{3,2,1,0:T(8,128)(2,1)S(1)} %collective-permute-done.9.refs_1_, bf16[2,3,64,128]{3,2,1,0:T(8,128)(2,1)S(1)} %collective-permute-done.10.refs_2_, ...), custom_call_target="tpu_custom_call" | custom-call | tf_op jit(solution)/shard_map/unpack/pallas_call | solution.py:382
  (8 shorter events, 0.1 us)
Async XLA Ops:
  0.6 31.4 %copy-start = (f32[16,3,3,256]{3,0,2,1:T(8,128)S(1)}, f32[16,3,3,256]{3,0,2,1:T(8,128)}, u32[]{:S(2)}) copy-start(f32[16,3,3,256]{3,0,2,1:T(8,128)} %param.8) | copy-start | bytes 442372
  2.9 1.6 %collective-permute-start = (bf16[4,3,64,128]{3,2,1,0:T(8,128)(2,1)S(1)}, bf16[4,3,64,128]{3,2,1,0:T(8,128)(2,1)S(1)}, u32[]{:S(2)}, u32[]{:S(2)}) collective-permute-start(bf16[4,3,64,128]{3,2,1,0:T(8,128)(2,1)S(1)} %get-tuple-element.16), channel_id=1, source_target_pairs={{0,4},{4,0},{8,12},{12,8},{16,20},{20,16},{24,28},{28,24},{1,5},{5... | collective-permute-start | bytes 589832 | tf_op jit(solution)/shard_map/ppermute | solution.py:276
  4.6 8.7 %collective-permute-start.1 = (bf16[2,3,64,128]{3,2,1,0:T(8,128)(2,1)S(1)}, bf16[2,3,64,128]{3,2,1,0:T(8,128)(2,1)S(1)}, u32[]{:S(2)}, u32[]{:S(2)}) collective-permute-start(bf16[2,3,64,128]{3,2,1,0:T(8,128)(2,1)S(1)} %pad_maximum_fusion), channel_id=1, source_target_pairs={{0,24},{4,28},{8,16},{12,20},{16,8},{20,12},{24,0},{28,4},{1,25},{... | collective-permute-start | bytes 294920 | tf_op jit(solution)/shard_map/ppermute | solution.py:276
  9.6 8.6 %collective-permute-start.2 = (bf16[2,3,64,128]{3,2,1,0:T(8,128)(2,1)S(1)}, bf16[2,3,64,128]{3,2,1,0:T(8,128)(2,1)S(1)}, u32[]{:S(2)}, u32[]{:S(2)}) collective-permute-start(bf16[2,3,64,128]{3,2,1,0:T(8,128)(2,1)S(1)} %pad_maximum_fusion.1), channel_id=1, source_target_pairs={{0,16},{4,20},{8,24},{12,28},{16,0},{20,4},{24,8},{28,12},{1,17},{... | collective-permute-start | bytes 294920 | tf_op jit(solution)/shard_map/ppermute | solution.py:276
  9.7 8.5 %collective-permute-start.3 = (bf16[2,3,64,128]{3,2,1,0:T(8,128)(2,1)S(1)}, bf16[2,3,64,128]{3,2,1,0:T(8,128)(2,1)S(1)}, u32[]{:S(2)}, u32[]{:S(2)}) collective-permute-start(bf16[2,3,64,128]{3,2,1,0:T(8,128)(2,1)S(1)} %pad_maximum_fusion.2), channel_id=1, source_target_pairs={{0,8},{4,12},{8,0},{12,4},{16,24},{20,28},{24,16},{28,20},{1,9},{5... | collective-permute-start | bytes 294920 | tf_op jit(solution)/shard_map/ppermute | solution.py:276
  22.8 6.9 %collective-permute-start.6 = (f32[9,16,256]{2,1,0:T(8,128)S(1)}, f32[9,16,256]{2,1,0:T(8,128)S(1)}, u32[]{:S(2)}, u32[]{:S(2)}) collective-permute-start(f32[9,16,256]{2,1,0:T(8,128)S(1)} %get-tuple-element.21.refs_0_), channel_id=1, source_target_pairs={{0,3},{1,2},{2,1},{3,0},{4,7},{5,6},{6,5},{7,4},{8,11},{9,10},{10,... | collective-permute-start | bytes 442376 | tf_op jit(solution)/shard_map/ppermute | solution.py:276
  25.3 6.7 %collective-permute-start.5 = (f32[9,16,256]{2,1,0:T(8,128)S(1)}, f32[9,16,256]{2,1,0:T(8,128)S(1)}, u32[]{:S(2)}, u32[]{:S(2)}) collective-permute-start(f32[9,16,256]{2,1,0:T(8,128)S(1)} %get-tuple-element.21.refs_0_), channel_id=1, source_target_pairs={{0,2},{1,3},{2,0},{3,1},{4,6},{5,7},{6,4},{7,5},{8,10},{9,11},{10,... | collective-permute-start | bytes 442376 | tf_op jit(solution)/shard_map/ppermute | solution.py:276
  25.8 6.2 %collective-permute-start.4 = (f32[9,16,256]{2,1,0:T(8,128)S(1)}, f32[9,16,256]{2,1,0:T(8,128)S(1)}, u32[]{:S(2)}, u32[]{:S(2)}) collective-permute-start(f32[9,16,256]{2,1,0:T(8,128)S(1)} %get-tuple-element.21.refs_0_), channel_id=1, source_target_pairs={{0,1},{1,0},{2,3},{3,2},{4,5},{5,4},{6,7},{7,6},{8,9},{9,8},{10,11... | collective-permute-start | bytes 442376 | tf_op jit(solution)/shard_map/ppermute | solution.py:276
  38.7 1.5 %collective-permute-start.7 = (bf16[4,3,64,128]{3,2,1,0:T(8,128)(2,1)S(1)}, bf16[4,3,64,128]{3,2,1,0:T(8,128)(2,1)S(1)}, u32[]{:S(2)}, u32[]{:S(2)}) collective-permute-start(bf16[4,3,64,128]{3,2,1,0:T(8,128)(2,1)S(1)} %get-tuple-element.23), channel_id=1, source_target_pairs={{0,4},{4,0},{8,12},{12,8},{16,20},{20,16},{24,28},{28,24},{1,5},{5... | collective-permute-start | bytes 589832 | tf_op jit(solution)/shard_map/ppermute | solution.py:276
  40.3 7.6 %collective-permute-start.8 = (bf16[2,3,64,128]{3,2,1,0:T(8,128)(2,1)S(1)}, bf16[2,3,64,128]{3,2,1,0:T(8,128)(2,1)S(1)}, u32[]{:S(2)}, u32[]{:S(2)}) collective-permute-start(bf16[2,3,64,128]{3,2,1,0:T(8,128)(2,1)S(1)} %pad_maximum_fusion.3), channel_id=1, source_target_pairs={{0,24},{4,28},{8,16},{12,20},{16,8},{20,12},{24,0},{28,4},{1,25},{... | collective-permute-start | bytes 294920 | tf_op jit(solution)/shard_map/ppermute | solution.py:276
  42.8 8.6 %collective-permute-start.9 = (bf16[2,3,64,128]{3,2,1,0:T(8,128)(2,1)S(1)}, bf16[2,3,64,128]{3,2,1,0:T(8,128)(2,1)S(1)}, u32[]{:S(2)}, u32[]{:S(2)}) collective-permute-start(bf16[2,3,64,128]{3,2,1,0:T(8,128)(2,1)S(1)} %pad_maximum_fusion.4), channel_id=1, source_target_pairs={{0,16},{4,20},{8,24},{12,28},{16,0},{20,4},{24,8},{28,12},{1,17},{... | collective-permute-start | bytes 294920 | tf_op jit(solution)/shard_map/ppermute | solution.py:276
  42.9 8.5 %collective-permute-start.10 = (bf16[2,3,64,128]{3,2,1,0:T(8,128)(2,1)S(1)}, bf16[2,3,64,128]{3,2,1,0:T(8,128)(2,1)S(1)}, u32[]{:S(2)}, u32[]{:S(2)}) collective-permute-start(bf16[2,3,64,128]{3,2,1,0:T(8,128)(2,1)S(1)} %pad_maximum_fusion.5), channel_id=1, source_target_pairs={{0,8},{4,12},{8,0},{12,4},{16,24},{20,28},{24,16},{28,20},{1,9},{5... | collective-permute-start | bytes 294920 | tf_op jit(solution)/shard_map/ppermute | solution.py:276

commit v3 on v2

v3 whole, which is shorter than its diff:
```python
import functools
import math

import jax
import jax.numpy as jnp
from jax import lax
from jax.experimental import pallas as pl
from jax.experimental.pallas import tpu as pltpu
from jax.sharding import PartitionSpec as P

LAGS = 256
HALF = LAGS // 2
LANES = 128
HALF_TILE = LANES // 2
PHASES = 16
WIDE = 32
EARLY = 12
CHANS = 3
WINDOW = 3 * LANES
DEPTH = 7 * LANES


def fetch(sources, targets, sems):
    copies = [pltpu.make_async_copy(s, t, sems.at[k]) for k, (s, t) in enumerate(zip(sources, targets))]
    for copy in copies:
        copy.start()
    return copies


def pack_kernel(rows_in, rec_ref, swap_ref, *refs):
    keep_refs = refs[:-4]
    buffer, scratch, rows_ref, sems = refs[-4:]
    me = lax.axis_index("stn")
    stations = rec_ref.shape[1]
    chunks = rec_ref.shape[2] // LANES
    copies = fetch(
        [rows_in] + [rec_ref.at[c] for c in range(CHANS)],
        [rows_ref] + [buffer.at[c] for c in range(CHANS)],
        sems,
    )
    copies[0].wait()
    for c in range(CHANS):
        copies[c + 1].wait()
        for r in range(chunks):
            piece = buffer[c, :, r * LANES:(r + 1) * LANES]
            scratch[c, r * stations:(r + 1) * stations, :] = piece.astype(jnp.float32)
        for j, keep_ref in enumerate(keep_refs):
            for i, ref in enumerate((keep_ref, swap_ref.at[j])):
                station = rows_ref[me ^ (2 * j + i)]
                picked = scratch[c, pl.ds(station, chunks, stride=stations), :]
                ref[c] = picked.astype(jnp.bfloat16)


def unpack_kernel(order, rows_in, *refs):
    returned = refs[:-5]
    out_ref, buffer, scratch, rows_ref, sems = refs[-5:]
    rows_copy = pltpu.make_async_copy(rows_in, rows_ref, sems.at[CHANS])
    rows_copy.start()
    scratch[...] = jnp.zeros_like(scratch)
    rows_copy.wait()
    me = lax.axis_index("stn")
    stations = out_ref.shape[1]
    chunks = out_ref.shape[2] // LANES
    copies = []
    for c in range(CHANS):
        pieces = [(2 * j + i, ref.at[i]) for j, ref in zip(order, returned[:-2]) for i in range(2)]
        for j, ref in pieces + [(0, returned[-2]), (1, returned[-1])]:
            where = pl.ds(rows_ref[me ^ j], chunks, stride=stations)
            scratch[c, where, :] = scratch[c, where, :] + ref[c].astype(jnp.float32)
        for r in range(chunks):
            piece = scratch[c, r * stations:(r + 1) * stations, :]
            buffer[c, :, r * LANES:(r + 1) * LANES] = piece.astype(jnp.bfloat16)
        copies.append(pltpu.make_async_copy(buffer.at[c], out_ref.at[c], sems.at[c]))
        copies[c].start()
    for copy in copies:
        copy.wait()


def build_phases(slot_refs, fan_ref):
    chunks = slot_refs[0].shape[1]
    rows = fan_ref.shape[1]
    lane = lax.broadcasted_iota(jnp.int32, (LANES, LANES), 1)
    left = lax.broadcasted_iota(jnp.int32, (rows, LANES), 1) < chunks
    for place in range(0, CHANS * len(slot_refs), 2):
        pair = [slot_refs[e // CHANS][e % CHANS] for e in (place, place + 1)]
        middle = jnp.concatenate(pair, axis=0).astype(jnp.float32).T
        before = jnp.where(lane % chunks == 0, 0.0, pltpu.roll(middle, 1, 1))
        after = jnp.where(lane % chunks == chunks - 1, 0.0, pltpu.roll(middle, LANES - 1, 1))
        wide = jnp.concatenate([before, middle, after], axis=0)
        swapped = pltpu.roll(wide, chunks, 1)
        one = jnp.where(left, wide[:rows], swapped[HALF_TILE:])
        two = jnp.where(left, swapped[:rows], wide[HALF_TILE:])
        fan_ref[place] = one.astype(jnp.bfloat16)
        fan_ref[place + 1] = two.astype(jnp.bfloat16)


def shifted_rows(fan_ref, slot, phases):
    span = LAGS + phases
    tail = DEPTH - CHANS * span
    columns = []
    for first in range(0, HALF_TILE, phases):
        parts = [fan_ref[CHANS * slot + b, first:first + span, :] for b in range(CHANS)]
        parts.append(fan_ref[CHANS * slot, first:first + tail, :])
        columns.append(jnp.concatenate(parts, axis=0))
    return jnp.concatenate(columns, axis=1)


def prep_kernel(
    token, first_in, second_in, rows_in, low_in, high_in, observed_in,
    bands, first_out, second_out, rows_out, inside, seen, seen_later,
    staged, low_ref, high_ref, sems,
):
    copies = fetch(
        (low_in, high_in, observed_in, first_in, second_in, rows_in),
        (low_ref, high_ref, staged, first_out, second_out, rows_out),
        sems,
    )
    bands[...] = jnp.zeros_like(bands)
    for copy in copies:
        copy.wait()
    pairs = inside.shape[0]
    early = seen.shape[1]
    row = lax.broadcasted_iota(jnp.int32, (pairs, LAGS), 0)
    lag = lax.broadcasted_iota(jnp.int32, (pairs, LAGS), 1)
    low = jnp.zeros_like(row)
    high = jnp.zeros_like(row)
    for p in range(pairs):
        low = jnp.where(row == p, low_ref[p], low)
        high = jnp.where(row == p, high_ref[p], high)
    inside[...] = ((lag >= low) & (lag < high)).astype(jnp.int32)
    for i in range(seen.shape[0]):
        seen[i] = staged[i, :early]
        seen_later[i] = staged[i, early:]


def correlate(start, first_ref, second_ref, fan_ref, heads, corr_ref):
    me = lax.axis_index("stn")

    def step(p, carry):
        right = shifted_rows(fan_ref, second_ref[start + p] ^ me, WIDE)
        products = lax.dot_general(
            heads[first_ref[start + p] ^ me], right, (((1,), (1,)), ((), ())),
            preferred_element_type=jnp.float32,
        )
        for a in range(CHANS):
            for b in range(CHANS):
                block = products[WIDE * a:WIDE * (a + 1), LAGS * b:LAGS * b + WINDOW]
                shift = WINDOW - WIDE * b - (WIDE - 1)
                turned = pltpu.roll(block, shift, 1, stride=1, stride_axis=0)
                corr_ref[CHANS * a + b, pl.ds(p, 1), :] = jnp.sum(
                    turned[:, :LAGS], axis=0, keepdims=True
                )
        return carry

    count = corr_ref.shape[1]
    lax.fori_loop(0, count, step, 0, unroll=min(count, 16))


def corr_first_kernel(order, first_in, second_in, *refs):
    given = refs[:-6]
    corr_ref, fan_ref, heads, first_ref, second_ref, sems = refs[-6:]
    copies = fetch((first_in, second_in), (first_ref, second_ref), sems)
    slot_refs = [None] * (2 * len(given) - 2)
    for j, ref in zip(order, given[:-2]):
        slot_refs[2 * j:2 * j + 2] = [ref.at[0], ref.at[1]]
    slot_refs[:2] = given[-2:]
    build_phases(slot_refs, fan_ref)
    height = CHANS * WIDE
    row = lax.broadcasted_iota(jnp.int32, (height, height), 0)
    column = lax.broadcasted_iota(jnp.int32, (height, height), 1)
    same = row // WIDE == column // WIDE
    flip = (same & (row % WIDE + column % WIDE == WIDE - 1)).astype(jnp.bfloat16)

    def head(q, carry):
        rows = []
        for a in range(CHANS):
            pieces = []
            for m in range(0, HALF_TILE, WIDE):
                pieces.append(fan_ref[CHANS * q + a, HALF + m:HALF + m + WIDE, :])
            rows.append(jnp.concatenate(pieces, axis=1))
        natural = jnp.concatenate(rows, axis=0)
        heads[q] = jnp.dot(flip, natural, preferred_element_type=jnp.float32).astype(jnp.bfloat16)
        return carry

    lax.fori_loop(0, heads.shape[0], head, 0, unroll=8)
    for copy in copies:
        copy.wait()
    correlate(0, first_ref, second_ref, fan_ref, heads, corr_ref)


def corr_second_kernel(start, first_ref, second_ref, fan_ref, heads, corr_ref):
    correlate(start, first_ref, second_ref, fan_ref, heads, corr_ref)


def spread(lag_rows, combos, p):
    turned = []
    for c, combo in enumerate(combos):
        block = jnp.broadcast_to(lag_rows[combo, pl.ds(p, 1), :], (PHASES, WINDOW))
        turned.append(pltpu.roll(block, PHASES * c, 1, stride=1, stride_axis=0))
    w0, w1, w2 = turned
    return jnp.concatenate(
        [
            w0[:, :LAGS],
            w0[:, LAGS:] + w1[:, :LANES],
            w1[:, LANES:LAGS],
            w1[:, LAGS:] + w2[:, :LANES],
            w2[:, LANES:],
        ],
        axis=1,
    ).astype(jnp.bfloat16)


def pairwise(terms):
    while len(terms) > 1:
        terms = [sum(terms[k + 1:k + 2], terms[k]) for k in range(0, len(terms), 2)]
    return terms[0]


def residuals(corr_scale, part_refs, observed_ref, inside, resid, forward, backward):
    combos, pairs, _ = resid.shape
    flip = (
        lax.broadcasted_iota(jnp.int32, (LAGS, WINDOW), 0)
        + lax.broadcasted_iota(jnp.int32, (LAGS, WINDOW), 1)
        == LAGS
    ).astype(jnp.bfloat16)
    forward[:, :, LAGS:] = jnp.zeros((combos, pairs, WINDOW - LAGS), jnp.float32)
    for i in range(combos):
        summed = pairwise([ref[i] for ref in part_refs])
        value = jnp.where(inside, summed * corr_scale - observed_ref[i], 0.0)
        resid[i] = value
        rounded = value.astype(jnp.bfloat16)
        forward[i, :, :LAGS] = rounded.astype(jnp.float32)
        backward[i] = jnp.dot(rounded, flip, preferred_element_type=jnp.float32)


def fill_bands(start, first_ref, second_ref, forward, backward, bands):
    me = lax.axis_index("stn")
    slots = bands.shape[0]
    pairs = forward.shape[1]
    height = CHANS * PHASES

    def row_place(q):
        return q // 2 + (slots // 2) * (1 - q % 2)

    def fill(p, carry):
        qf = first_ref[start + p] ^ me
        qs = second_ref[start + p] ^ me
        for c in range(CHANS):
            at = pl.multiple_of(height * row_place(qf) + PHASES * c, PHASES)
            bands[qs, pl.ds(at, PHASES), :] = spread(
                forward, [CHANS * c + b for b in range(CHANS)], p
            )
            at = pl.multiple_of(height * row_place(qs) + PHASES * c, PHASES)
            bands[qf, pl.ds(at, PHASES), :] = spread(
                backward, [CHANS * a + c for a in range(CHANS)], p
            )
        return carry

    lax.fori_loop(0, pairs, fill, 0, unroll=min(pairs, 16))


def contract(adj_scale, first_row, bands, fan_ref, total, outs):
    rows = total.shape[0]
    total[...] = jnp.zeros_like(total)

    def accumulate(r, carry):
        right = shifted_rows(fan_ref, r, PHASES)
        left = bands[r, first_row:first_row + rows, :]
        total[...] += jnp.dot(left, right, preferred_element_type=jnp.float32)
        return carry

    lax.fori_loop(0, bands.shape[0], accumulate, 0, unroll=8)
    chunks = outs[0].shape[1]
    near = lax.broadcasted_iota(jnp.int32, (PHASES, LANES), 1) < chunks
    for place in range(0, rows // PHASES, 2):
        upper = []
        lower = []
        for m in range(4):
            columns = slice(m * LANES, (m + 1) * LANES)
            one = total[place * PHASES:(place + 1) * PHASES, columns]
            two = total[(place + 1) * PHASES:(place + 2) * PHASES, columns]
            upper.append(jnp.where(near, one, pltpu.roll(two, chunks, 1)))
            lower.append(jnp.where(near, pltpu.roll(one, chunks, 1), two))
        tile = (jnp.concatenate(upper + lower, axis=0).T * adj_scale).astype(jnp.bfloat16)
        for k in range(2):
            e = place + k
            outs[e // CHANS][e % CHANS] = tile[k * chunks:(k + 1) * chunks]


def bands_kernel(corr_scale, first_in, second_in, inside_ref, seen_ref, bands_in, *refs):
    part_refs = refs[:-7]
    bands, resid, forward, backward, first_ref, second_ref, sems = refs[-7:]
    copies = fetch((first_in, second_in), (first_ref, second_ref), sems)
    inside = inside_ref[:resid.shape[1], :] > 0
    residuals(corr_scale, part_refs, seen_ref, inside, resid, forward, backward)
    for copy in copies:
        copy.wait()
    fill_bands(0, first_ref, second_ref, forward, backward, bands)


def adjoint_kernel(
    corr_scale, adj_scale, first_in, second_in, inside_ref, seen_ref, bands_in, fan_ref,
    earlier, *refs
):
    (bands, swap_ref, share_ref, resid, forward, backward, total,
     first_ref, second_ref, sems) = refs[-10:]
    part_refs = refs[:-10]
    copies = fetch((first_in, second_in), (first_ref, second_ref), sems)
    half = earlier.shape[1]
    inside = inside_ref[half:, :] > 0
    residuals(corr_scale, part_refs, seen_ref, inside, resid, forward, backward)
    offset = lax.axis_index("win") * share_ref.shape[1]
    for j in range(share_ref.shape[1]):
        p = offset + j
        for i in range(resid.shape[0]):
            one = earlier[i, pl.ds(jnp.minimum(p, half - 1), 1), :]
            two = resid[i, pl.ds(jnp.maximum(p - half, 0), 1), :]
            share_ref[i, j:j + 1, :] = jnp.where(p < half, one, two)
    for copy in copies:
        copy.wait()
    fill_bands(half, first_ref, second_ref, forward, backward, bands)
    outs = [swap_ref.at[j] for j in range(swap_ref.shape[0])]
    contract(adj_scale, 0, bands, fan_ref, total, outs)


def keep_kernel(adj_scale, bands, fan_ref, *refs):
    outs = refs[:-1]
    total = refs[-1]
    contract(adj_scale, total.shape[0], bands, fan_ref, total, outs)


def smem():
    return pl.BlockSpec(memory_space=pltpu.SMEM)


def vmem():
    return pl.BlockSpec(memory_space=pltpu.VMEM)


def flipped(x, axis, bits):
    count = lax.axis_size(axis)
    return lax.ppermute(x, axis, [(k, k ^ bits) for k in range(count)])


def across(swap, keep):
    chips = len(keep)
    got = flipped(swap, "stn", 1)
    order = []
    blocks = []
    for j in range(chips - 1, 0, -1):
        moved = flipped(jnp.stack([keep[j], got[j]]), "stn", 2 * j)
        order.append(j)
        blocks.append(moved)
    return order + [0, 0], blocks + [keep[0], got[0]]


def window_parts(corr):
    groups = lax.axis_size("win")
    if groups > 4:
        gathered = lax.all_gather(corr, "win")
        return [gathered[w] for w in range(groups)]
    return [corr] + [flipped(corr, "win", w) for w in range(1, groups)]


def shards(records, observed, lag_lo, lag_hi, send_table, pair_first, pair_second):
    owner_count = lax.axis_size("stn")
    window_groups = lax.axis_size("win")
    stations, local_windows, _, samples = records.shape
    send_rows = send_table.reshape(-1)
    slots = send_rows.shape[0]
    chunks = samples // LANES
    pairs = observed.shape[0]
    combos = CHANS * CHANS
    share = pairs // window_groups
    corr_scale = 1.0 / math.sqrt(samples * local_windows * window_groups)
    adj_scale = 1.0 / math.sqrt(CHANS * LAGS)

    chips = slots // 2
    block = jax.ShapeDtypeStruct((CHANS, chunks, LANES), jnp.bfloat16)
    blocks = jax.ShapeDtypeStruct((chips, CHANS, chunks, LANES), jnp.bfloat16)
    any_space = pl.BlockSpec(memory_space=pltpu.HBM)
    planes = jnp.transpose(records, (1, 2, 0, 3)).reshape(CHANS, stations, samples)
    planes = pltpu.with_memory_space_constraint(planes, pltpu.HBM)
    send_rows, pair_first, pair_second, lag_lo, lag_hi = [
        pltpu.with_memory_space_constraint(x, pltpu.HBM)
        for x in (send_rows, pair_first, pair_second, lag_lo, lag_hi)
    ]
    swap, *keep = pl.pallas_call(
        pack_kernel,
        in_specs=[any_space, any_space],
        out_specs=[vmem()] * (1 + chips),
        out_shape=[blocks] + [block] * chips,
        scratch_shapes=[
            pltpu.VMEM((CHANS, stations, samples), jnp.bfloat16),
            pltpu.VMEM((CHANS, chunks * stations, LANES), jnp.float32),
            pltpu.SMEM((slots,), jnp.int32),
            pltpu.SemaphoreType.DMA((CHANS + 1,)),
        ],
        compiler_params=pltpu.CompilerParams(vmem_limit_bytes=8 * 2**20),
        name="pack",
    )(send_rows, planes)
    rows = 3 * LANES - HALF_TILE
    early = pairs * EARLY // 16
    fan_shape = jax.ShapeDtypeStruct((slots * CHANS, rows, LANES), jnp.bfloat16)
    corr_shape = jax.ShapeDtypeStruct((combos, early, LAGS), jnp.float32)
    late_shape = jax.ShapeDtypeStruct((combos, pairs - early, LAGS), jnp.float32)
    index_shape = jax.ShapeDtypeStruct((pairs,), jnp.int32)
    height = slots * CHANS * PHASES
    bands_shape = jax.ShapeDtypeStruct((slots, height, DEPTH), jnp.bfloat16)
    index_scratch = pltpu.SMEM((pairs,), jnp.int32)
    small = pltpu.CompilerParams(vmem_limit_bytes=16 * 2**20)
    cost = pl.CostEstimate(flops=2 * 10**9, bytes_accessed=2**22, transcendentals=0)
    seen = jnp.transpose(observed, (1, 2, 0, 3)).reshape(combos, pairs, LAGS)
    seen = pltpu.with_memory_space_constraint(seen, pltpu.HBM)
    bands, firsts, seconds, rows_copy, inside, seen, seen_later = pl.pallas_call(
        prep_kernel,
        in_specs=[pl.BlockSpec(memory_space=pl.ANY)] + [any_space] * 6,
        out_specs=[vmem()] * 7,
        out_shape=[
            bands_shape,
            index_shape,
            index_shape,
            jax.ShapeDtypeStruct((slots,), jnp.int32),
            jax.ShapeDtypeStruct((pairs, LAGS), jnp.int32),
            corr_shape,
            late_shape,
        ],
        scratch_shapes=[
            pltpu.VMEM((combos, pairs, LAGS), jnp.float32),
            index_scratch,
            index_scratch,
            pltpu.SemaphoreType.DMA((6,)),
        ],
        compiler_params=small,
        cost_estimate=cost,
        name="prep",
    )(swap, pair_first, pair_second, send_rows, lag_lo, lag_hi, seen)
    order, arrived = across(swap, keep)

    corr, fan, heads = pl.pallas_call(
        functools.partial(corr_first_kernel, order),
        in_specs=[vmem()] * (chips + 3),
        out_specs=[vmem()] * 3,
        out_shape=[
            corr_shape,
            fan_shape,
            jax.ShapeDtypeStruct(
                (slots, CHANS * WIDE, HALF_TILE // WIDE * LANES), jnp.bfloat16
            ),
        ],
        scratch_shapes=[index_scratch, index_scratch, pltpu.SemaphoreType.DMA((2,))],
        compiler_params=small,
        cost_estimate=cost,
        name="corr_first",
    )(firsts, seconds, *arrived)
    parts = window_parts(corr)
    later = pl.pallas_call(
        functools.partial(corr_second_kernel, early),
        in_specs=[smem(), smem(), vmem(), vmem()],
        out_specs=vmem(),
        out_shape=late_shape,
        compiler_params=small,
        cost_estimate=cost,
        name="corr_second",
    )(firsts, seconds, fan, heads)
    later_parts = window_parts(later)

    lag_rows = pltpu.VMEM((combos, early, WINDOW), jnp.float32)
    bands, resid = pl.pallas_call(
        functools.partial(bands_kernel, corr_scale),
        in_specs=[vmem()] * (5 + len(parts)),
        out_specs=[vmem()] * 2,
        out_shape=[bands_shape, corr_shape],
        scratch_shapes=[
            lag_rows, lag_rows, index_scratch, index_scratch, pltpu.SemaphoreType.DMA((2,))
        ],
        input_output_aliases={4: 0},
        compiler_params=small,
        cost_estimate=cost,
        name="bands",
    )(firsts, seconds, inside, seen, bands, *parts)
    total = pltpu.VMEM((height // 2, 4 * LANES), jnp.float32)
    lag_rows = pltpu.VMEM((combos, pairs - early, WINDOW), jnp.float32)
    bands, swap, residual = pl.pallas_call(
        functools.partial(adjoint_kernel, corr_scale, adj_scale),
        in_specs=[vmem()] * (7 + len(later_parts)),
        out_specs=[vmem()] * 3,
        out_shape=[bands_shape, blocks, jax.ShapeDtypeStruct((combos, share, LAGS), jnp.float32)],
        scratch_shapes=[
            pltpu.VMEM((combos, pairs - early, LAGS), jnp.float32),
            lag_rows,
            lag_rows,
            total,
            index_scratch,
            index_scratch,
            pltpu.SemaphoreType.DMA((2,)),
        ],
        input_output_aliases={4: 0},
        compiler_params=small,
        cost_estimate=cost,
        name="adjoint",
    )(firsts, seconds, inside, seen_later, bands, fan, resid, *later_parts)
    keep = pl.pallas_call(
        functools.partial(keep_kernel, adj_scale),
        in_specs=[vmem()] * 2,
        out_specs=[vmem()] * chips,
        out_shape=[block] * chips,
        scratch_shapes=[total],
        compiler_params=small,
        cost_estimate=cost,
        name="keep",
    )(bands, fan)
    order, returned = across(swap, keep)
    stacked = pl.pallas_call(
        functools.partial(unpack_kernel, order),
        in_specs=[vmem()] * (chips + 2),
        out_specs=any_space,
        out_shape=jax.ShapeDtypeStruct((CHANS, stations, samples), jnp.bfloat16),
        scratch_shapes=[
            pltpu.VMEM((CHANS, stations, samples), jnp.bfloat16),
            pltpu.VMEM((CHANS, chunks * stations, LANES), jnp.float32),
            pltpu.SMEM((slots,), jnp.int32),
            pltpu.SemaphoreType.DMA((CHANS + 1,)),
        ],
        compiler_params=pltpu.CompilerParams(vmem_limit_bytes=8 * 2**20),
        name="unpack",
    )(rows_copy, *returned)
    station_adjoint = jnp.transpose(stacked.reshape(1, CHANS, stations, samples), (2, 0, 1, 3))
    residual = jnp.transpose(residual.reshape(CHANS, CHANS, share, LAGS), (2, 0, 1, 3))
    return (station_adjoint, residual)


def solution(mesh):
    placed = (
        P("stn", "win", None, None),
        P("stn", None, None, None),
        P("stn"),
        P("stn"),
        P("stn", None, None),
        P("stn"),
        P("stn"),
    )
    return jax.shard_map(
        shards,
        mesh=mesh,
        in_specs=placed,
        out_specs=(P("stn", "win", None, None), P(("stn", "win"), None, None, None)),
        check_vma=False,
    )
```

time: 53.8 us -> 51.7 us (0.961)
  waiting for transfers between devices: 22.6 us -> 15.6 us
  starting transfers between devices: 14.4 us -> 18.8 us
    ppermute x11 -> x14, waiting for transfers between devices: 22.6 us -> 15.6 us  [flipped(): return lax.ppermute(x, axis, [(k, k ^ bits) for k in range(count)])]
    ppermute x11 -> x14, starting transfers between devices: 14.4 us -> 18.8 us  [flipped(): return lax.ppermute(x, axis, [(k, k ^ bits) for k in range(count)])]
    pallas_call x3 -> x7, Pallas kernels: 9.05 us -> 13 us  [the longest x1 3.28 us: shards(): pl.pallas_call(functools.partial(corr_first_kernel, order), in_specs=[vme...]
    pallas_call x1, Pallas kernels: 6.66 us -> 3.22 us  [shards(): pl.pallas_call(functools.partial(adjoint_kernel, corr_scale, adj_scale),...]
  transfers between devices with their start and end apart: 11 -> 14, of which waited for: 9 -> 6; matrix products, arithmetic and copies ran while one was open for 0% -> 0% of each run, Pallas kernels for 0% -> 12%
where the time goes in v3:
time: 51.7 us; the launch traced here: 51.5 us
  starting transfers between devices  18.8 us (36%)
  Pallas kernels  16.2 us (31%)
  waiting for transfers between devices  15.6 us (30%)
  between operations  0.79 us (2%)
    ppermute x14, starting transfers between devices, flipped(): return lax.ppermute(x, axis, [(k, k ^ bits) for k in range(count)])  18.8 us
    ppermute x14, waiting for transfers between devices, flipped(): return lax.ppermute(x, axis, [(k, k ^ bits) for k in range(count)])  15.6 us
    pallas_call x1, Pallas kernels, shards(): pl.pallas_call(functools.partial(corr_first_kernel, order), in_specs=[vme...  3.28 us
    pallas_call x1, Pallas kernels, shards(): pl.pallas_call(functools.partial(adjoint_kernel, corr_scale, adj_scale),...  3.22 us
    pallas_call x1, Pallas kernels, shards(): pl.pallas_call(functools.partial(keep_kernel, adj_scale), in_specs=[vmem(...  2.05 us
    pallas_call x1, Pallas kernels, shards(): pl.pallas_call(functools.partial(unpack_kernel, order), in_specs=[vmem()]...  1.94 us
    pallas_call x1, Pallas kernels, shards(): pl.pallas_call(functools.partial(bands_kernel, corr_scale), in_specs=[vme...  1.86 us
    pallas_call x1, Pallas kernels, shards(): pl.pallas_call(pack_kernel, in_specs=[any_space, any_space], out_specs=[v...  1.51 us
  transfers between devices with their start and end apart: 14, of which 6 were waited for; matrix products, arithmetic and copies ran while one was open for 0% of the time, Pallas kernels for 12%

profile of v3, /device:TPU:0, one launch (start us, length us, event | category | flops | bytes accessed | tf_op | source)
XLA Modules:
  0.0 51.5 jit_solution(17752300409539714309)
XLA Ops:
  0.6 1.5 %pack.1 = (bf16[4,3,64,128]{3,2,1,0:T(8,128)(2,1)S(1)}, bf16[3,64,128]{2,1,0:T(8,128)(2,1)S(1)}, bf16[3,64,128]{2,1,0:T(8,128)(2,1)S(1)}, bf16[3,64,128]{2,1,0:T(8,128)(2,1)S(1)}, bf16[3,64,128]{2,1,0:T(8,128)(2,1)S(1)}) custom-call(s32[8]{0:T(128)} %bitcast.31, bf16[3,16,8192]{2,1,0:T(8,128)(2,1)} %bitcast.29), custom_call_target="tpu_custom_call" | custom-call | tf_op jit(solution)/shard_map/pack/pallas_call | solution.py:388
  2.1 0.5 %collective-permute-start = (bf16[4,3,64,128]{3,2,1,0:T(8,128)(2,1)S(1)}, bf16[4,3,64,128]{3,2,1,0:T(8,128)(2,1)S(1)}, u32[]{:S(2)}, u32[]{:S(2)}) collective-permute-start(bf16[4,3,64,128]{3,2,1,0:T(8,128)(2,1)S(1)} %get-tuple-element.26.token), channel_id=1, source_target_pairs={{0,4},{4,0},{8,12},{12,8},{16,20},{20,16},{24,28},{28,24},{1,5},{5... | collective-permute-start | bytes 589832 | tf_op jit(solution)/shard_map/ppermute | solution.py:342
  2.7 1.1 %collective-permute-done = bf16[4,3,64,128]{3,2,1,0:T(8,128)(2,1)S(1)} collective-permute-done((bf16[4,3,64,128]{3,2,1,0:T(8,128)(2,1)S(1)}, bf16[4,3,64,128]{3,2,1,0:T(8,128)(2,1)S(1)}, u32[]{:S(2)}, u32[]{:S(2)}) %collective-permute-start) | collective-permute-done | bytes 196640 | tf_op jit(solution)/shard_map/ppermute | solution.py:342
  3.8 5.0 %collective-permute-start.1 = (bf16[2,3,64,128]{3,2,1,0:T(8,128)(2,1)S(1)}, bf16[2,3,64,128]{3,2,1,0:T(8,128)(2,1)S(1)}, u32[]{:S(2)}, u32[]{:S(2)}) collective-permute-start(bf16[2,3,64,128]{3,2,1,0:T(8,128)(2,1)S(1)} %pad_maximum_fusion), channel_id=1, source_target_pairs={{0,24},{4,28},{8,16},{12,20},{16,8},{20,12},{24,0},{28,4},{1,25},{... | collective-permute-start | bytes 294920 | tf_op jit(solution)/shard_map/ppermute | solution.py:342
  8.8 0.1 collective-permute-start.2
  8.9 0.6 %collective-permute-start.3 = (bf16[2,3,64,128]{3,2,1,0:T(8,128)(2,1)S(1)}, bf16[2,3,64,128]{3,2,1,0:T(8,128)(2,1)S(1)}, u32[]{:S(2)}, u32[]{:S(2)}) collective-permute-start(bf16[2,3,64,128]{3,2,1,0:T(8,128)(2,1)S(1)} %pad_maximum_fusion.2), channel_id=1, source_target_pairs={{0,8},{4,12},{8,0},{12,4},{16,24},{20,28},{24,16},{28,20},{1,9},{5... | collective-permute-start | bytes 294920 | tf_op jit(solution)/shard_map/ppermute | solution.py:342
  9.6 1.0 %prep.1 = (bf16[8,384,896]{2,1,0:T(8,128)(2,1)S(1)}, s32[16]{0:T(128)S(1)}, s32[16]{0:T(128)S(1)}, s32[8]{0:T(128)S(1)}, s32[16,256]{1,0:T(8,128)S(1)}, /*index=...) custom-call(bf16[4,3,64,128]{3,2,1,0:T(8,128)(2,1)S(1)} %get-tuple-element.26.token, s32[16]{0:T(128)} %first_in.1, ...), custom_call_target="tpu_custom_call" | custom-call | flops 2000000000 | bytes 4194304 | tf_op jit(solution)/shard_map/prep/pallas_call | solution.py:415
  10.5 1.9 %collective-permute-done.1.refs_0_ = bf16[2,3,64,128]{3,2,1,0:T(8,128)(2,1)S(1)} collective-permute-done((bf16[2,3,64,128]{3,2,1,0:T(8,128)(2,1)S(1)}, bf16[2,3,64,128]{3,2,1,0:T(8,128)(2,1)S(1)}, u32[]{:S(2)}, u32[]{:S(2)}) %collective-permute-start.1) | collective-permute-done | bytes 98336 | tf_op jit(solution)/shard_map/ppermute | solution.py:342
  12.5 4.9 %collective-permute-done.2.refs_1_ = bf16[2,3,64,128]{3,2,1,0:T(8,128)(2,1)S(1)} collective-permute-done((bf16[2,3,64,128]{3,2,1,0:T(8,128)(2,1)S(1)}, bf16[2,3,64,128]{3,2,1,0:T(8,128)(2,1)S(1)}, u32[]{:S(2)}, u32[]{:S(2)}) %collective-permute-start.2) | collective-permute-done | bytes 98336 | tf_op jit(solution)/shard_map/ppermute | solution.py:342
  17.4 0.0 collective-permute-done.3.refs_2_
  17.4 3.3 %corr_first.1 = (f32[9,12,256]{2,1,0:T(8,128)S(1)}, bf16[24,320,128]{2,1,0:T(8,128)(2,1)S(1)}, bf16[8,96,256]{2,1,0:T(8,128)(2,1)S(1)}) custom-call(s32[16]{0:T(128)S(1)} %get-tuple-element.28.first_in.first_ref, s32[16]{0:T(128)S(1)} %get-tuple-element.29.second_in.second_ref, bf16[2,3,64,128]{3,2,1,0:T(8,128)(2,1)S(1)} %collective-permute-done.1.refs_0_, ...), custom_call_target="tpu_custom_call" | custom-call | flops 2000000000 | bytes 4194304 | tf_op jit(solution)/shard_map/corr_first/pallas_call | solution.py:440
  20.7 2.5 %collective-permute-start.6 = (f32[9,12,256]{2,1,0:T(8,128)S(1)}, f32[9,12,256]{2,1,0:T(8,128)S(1)}, u32[]{:S(2)}, u32[]{:S(2)}) collective-permute-start(f32[9,12,256]{2,1,0:T(8,128)S(1)} %get-tuple-element.38.refs_0_), channel_id=1, source_target_pairs={{0,3},{1,2},{2,1},{3,0},{4,7},{5,6},{6,5},{7,4},{8,11},{9,10},{10,... | collective-permute-start | bytes 331784 | tf_op jit(solution)/shard_map/ppermute | solution.py:342
  23.2 0.5 collective-permute-start.5
  23.7 0.5 %collective-permute-start.4 = (f32[9,12,256]{2,1,0:T(8,128)S(1)}, f32[9,12,256]{2,1,0:T(8,128)S(1)}, u32[]{:S(2)}, u32[]{:S(2)}) collective-permute-start(f32[9,12,256]{2,1,0:T(8,128)S(1)} %get-tuple-element.38.refs_0_), channel_id=1, source_target_pairs={{0,1},{1,0},{2,3},{3,2},{4,5},{5,4},{6,7},{7,6},{8,9},{9,8},{10,11... | collective-permute-start | bytes 331784 | tf_op jit(solution)/shard_map/ppermute | solution.py:342
  24.2 1.3 %corr_second.1.refs_0_ = f32[9,4,256]{2,1,0:T(4,128)S(1)} custom-call(s32[16]{0:T(128)S(1)} %get-tuple-element.28.first_in.first_ref, s32[16]{0:T(128)S(1)} %get-tuple-element.29.second_in.second_ref, bf16[24,320,128]{2,1,0:T(8,128)(2,1)S(1)} %get-tuple-element.40.fan_ref, bf16[8,96,256]{2,1,0:T(8,128)(2,1)S(1)} %get-tuple-element.42.heads), custom_call_target="tpu_custom_call" | custom-call | flops 2000000000 | bytes 4194304 | tf_op jit(solution)/shard_map/corr_second/pallas_call | solution.py:457
  25.5 2.5 %collective-permute-start.9 = (f32[9,4,256]{2,1,0:T(4,128)S(1)}, f32[9,4,256]{2,1,0:T(4,128)S(1)}, u32[]{:S(2)}, u32[]{:S(2)}) collective-permute-start(f32[9,4,256]{2,1,0:T(4,128)S(1)} %corr_second.1.refs_0_), channel_id=1, source_target_pairs={{0,3},{1,2},{2,1},{3,0},{4,7},{5,6},{6,5},{7,4},{8,11},{9,10},{10,... | collective-permute-start | bytes 110600 | tf_op jit(solution)/shard_map/ppermute | solution.py:342
  28.1 0.5 collective-permute-start.8
  28.6 0.0 collective-permute-done.6.refs_3_
  28.6 1.4 %collective-permute-start.7 = (f32[9,4,256]{2,1,0:T(4,128)S(1)}, f32[9,4,256]{2,1,0:T(4,128)S(1)}, u32[]{:S(2)}, u32[]{:S(2)}) collective-permute-start(f32[9,4,256]{2,1,0:T(4,128)S(1)} %corr_second.1.refs_0_), channel_id=1, source_target_pairs={{0,1},{1,0},{2,3},{3,2},{4,5},{5,4},{6,7},{7,6},{8,9},{9,8},{10,11... | collective-permute-start | bytes 110600 | tf_op jit(solution)/shard_map/ppermute | solution.py:342
  29.9 0.8 %collective-permute-done.5.refs_2_ = f32[9,12,256]{2,1,0:T(8,128)S(1)} collective-permute-done((f32[9,12,256]{2,1,0:T(8,128)S(1)}, f32[9,12,256]{2,1,0:T(8,128)S(1)}, u32[]{:S(2)}, u32[]{:S(2)}) %collective-permute-start.5) | collective-permute-done | bytes 110624 | tf_op jit(solution)/shard_map/ppermute | solution.py:342
  30.7 0.0 collective-permute-done.4.refs_1_
  30.7 1.9 %bands.1 = (bf16[8,384,896]{2,1,0:T(8,128)(2,1)S(1)}, f32[9,12,256]{2,1,0:T(8,128)S(1)}) custom-call(s32[16]{0:T(128)S(1)} %get-tuple-element.28.first_in.first_ref, s32[16]{0:T(128)S(1)} %get-tuple-element.29.second_in.second_ref, s32[16,256]{1,0:T(8,128)S(1)} %get-tuple-element.30.inside_ref, ...), custom_call_target="tpu_custom_call", output_to_operand_aliasing={{0}: (4, {})} | custom-call | flops 2000000000 | bytes 4194304 | tf_op jit(solution)/shard_map/bands/pallas_call | solution.py:469
  32.6 0.0 collective-permute-done.9.refs_3_
  32.6 0.0 collective-permute-done.8.refs_2_
  32.6 0.0 collective-permute-done.7.refs_1_
  32.6 3.2 %adjoint.1 = (bf16[8,384,896]{2,1,0:T(8,128)(2,1)S(1)}, bf16[4,3,64,128]{3,2,1,0:T(8,128)(2,1)S(1)}, f32[9,4,256]{2,1,0:T(4,128)}) custom-call(s32[16]{0:T(128)S(1)} %get-tuple-element.28.first_in.first_ref, s32[16]{0:T(128)S(1)} %get-tuple-element.29.second_in.second_ref, ...), custom_call_target="tpu_custom_call", output_to_operand_aliasing={{0}: (4, {})} | custom-call | flops 2000000000 | bytes 4194304 | tf_op jit(solution)/shard_map/adjoint/pallas_call | solution.py:484
  35.8 0.1 collective-permute-start.10
  35.9 2.1 %keep.1 = (bf16[3,64,128]{2,1,0:T(8,128)(2,1)S(1)}, bf16[3,64,128]{2,1,0:T(8,128)(2,1)S(1)}, bf16[3,64,128]{2,1,0:T(8,128)(2,1)S(1)}, bf16[3,64,128]{2,1,0:T(8,128)(2,1)S(1)}) custom-call(bf16[8,384,896]{2,1,0:T(8,128)(2,1)S(1)} %get-tuple-element.43.bands, bf16[24,320,128]{2,1,0:T(8,128)(2,1)S(1)} %get-tuple-element.40.fan_ref), custom_call_target="tpu_custom_call" | custom-call | flops 2000000000 | bytes 4194304 | tf_op jit(solution)/shard_map/keep/pallas_call | solution.py:503
  38.0 0.0 collective-permute-done.10
  38.0 2.5 %collective-permute-start.11 = (bf16[2,3,64,128]{3,2,1,0:T(8,128)(2,1)S(1)}, bf16[2,3,64,128]{3,2,1,0:T(8,128)(2,1)S(1)}, u32[]{:S(2)}, u32[]{:S(2)}) collective-permute-start(bf16[2,3,64,128]{3,2,1,0:T(8,128)(2,1)S(1)} %pad_maximum_fusion.3), channel_id=1, source_target_pairs={{0,24},{4,28},{8,16},{12,20},{16,8},{20,12},{24,0},{28,4},{1,25},{... | collective-permute-start | bytes 294920 | tf_op jit(solution)/shard_map/ppermute | solution.py:342
  40.6 0.1 collective-permute-start.12
  40.7 2.0 %collective-permute-start.13 = (bf16[2,3,64,128]{3,2,1,0:T(8,128)(2,1)S(1)}, bf16[2,3,64,128]{3,2,1,0:T(8,128)(2,1)S(1)}, u32[]{:S(2)}, u32[]{:S(2)}) collective-permute-start(bf16[2,3,64,128]{3,2,1,0:T(8,128)(2,1)S(1)} %pad_maximum_fusion.5), channel_id=1, source_target_pairs={{0,8},{4,12},{8,0},{12,4},{16,24},{20,28},{24,16},{28,20},{1,9},{5... | collective-permute-start | bytes 294920 | tf_op jit(solution)/shard_map/ppermute | solution.py:342
  42.6 2.9 %collective-permute-done.11.refs_0_ = bf16[2,3,64,128]{3,2,1,0:T(8,128)(2,1)S(1)} collective-permute-done((bf16[2,3,64,128]{3,2,1,0:T(8,128)(2,1)S(1)}, bf16[2,3,64,128]{3,2,1,0:T(8,128)(2,1)S(1)}, u32[]{:S(2)}, u32[]{:S(2)}) %collective-permute-start.11) | collective-permute-done | bytes 98336 | tf_op jit(solution)/shard_map/ppermute | solution.py:342
  45.6 4.0 %collective-permute-done.12.refs_1_ = bf16[2,3,64,128]{3,2,1,0:T(8,128)(2,1)S(1)} collective-permute-done((bf16[2,3,64,128]{3,2,1,0:T(8,128)(2,1)S(1)}, bf16[2,3,64,128]{3,2,1,0:T(8,128)(2,1)S(1)}, u32[]{:S(2)}, u32[]{:S(2)}) %collective-permute-start.12) | collective-permute-done | bytes 98336 | tf_op jit(solution)/shard_map/ppermute | solution.py:342
  49.6 0.0 collective-permute-done.13.refs_2_
  49.6 1.9 %unpack.1 = bf16[3,16,8192]{2,1,0:T(8,128)(2,1)} custom-call(s32[8]{0:T(128)S(1)} %get-tuple-element.27.rows_in, bf16[2,3,64,128]{3,2,1,0:T(8,128)(2,1)S(1)} %collective-permute-done.11.refs_0_, bf16[2,3,64,128]{3,2,1,0:T(8,128)(2,1)S(1)} %collective-permute-done.12.refs_1_, bf16[2,3,64,128]{3,2,1,0:T(8,128)(2,1)S(1)} %collective-permute-done.13.refs_2_, ...), custom_call_target="tpu_custom_call" | custom-call | tf_op jit(solution)/shard_map/unpack/pallas_call | solution.py:514
  (8 shorter events, 0.1 us)
Async XLA Ops:
  2.1 1.6 %collective-permute-start = (bf16[4,3,64,128]{3,2,1,0:T(8,128)(2,1)S(1)}, bf16[4,3,64,128]{3,2,1,0:T(8,128)(2,1)S(1)}, u32[]{:S(2)}, u32[]{:S(2)}) collective-permute-start(bf16[4,3,64,128]{3,2,1,0:T(8,128)(2,1)S(1)} %get-tuple-element.26.token), channel_id=1, source_target_pairs={{0,4},{4,0},{8,12},{12,8},{16,20},{20,16},{24,28},{28,24},{1,5},{5... | collective-permute-start | bytes 589832 | tf_op jit(solution)/shard_map/ppermute | solution.py:342
  3.8 8.7 %collective-permute-start.1 = (bf16[2,3,64,128]{3,2,1,0:T(8,128)(2,1)S(1)}, bf16[2,3,64,128]{3,2,1,0:T(8,128)(2,1)S(1)}, u32[]{:S(2)}, u32[]{:S(2)}) collective-permute-start(bf16[2,3,64,128]{3,2,1,0:T(8,128)(2,1)S(1)} %pad_maximum_fusion), channel_id=1, source_target_pairs={{0,24},{4,28},{8,16},{12,20},{16,8},{20,12},{24,0},{28,4},{1,25},{... | collective-permute-start | bytes 294920 | tf_op jit(solution)/shard_map/ppermute | solution.py:342
  8.8 8.6 %collective-permute-start.2 = (bf16[2,3,64,128]{3,2,1,0:T(8,128)(2,1)S(1)}, bf16[2,3,64,128]{3,2,1,0:T(8,128)(2,1)S(1)}, u32[]{:S(2)}, u32[]{:S(2)}) collective-permute-start(bf16[2,3,64,128]{3,2,1,0:T(8,128)(2,1)S(1)} %pad_maximum_fusion.1), channel_id=1, source_target_pairs={{0,16},{4,20},{8,24},{12,28},{16,0},{20,4},{24,8},{28,12},{1,17},{... | collective-permute-start | bytes 294920 | tf_op jit(solution)/shard_map/ppermute | solution.py:342
  8.9 8.5 %collective-permute-start.3 = (bf16[2,3,64,128]{3,2,1,0:T(8,128)(2,1)S(1)}, bf16[2,3,64,128]{3,2,1,0:T(8,128)(2,1)S(1)}, u32[]{:S(2)}, u32[]{:S(2)}) collective-permute-start(bf16[2,3,64,128]{3,2,1,0:T(8,128)(2,1)S(1)} %pad_maximum_fusion.2), channel_id=1, source_target_pairs={{0,8},{4,12},{8,0},{12,4},{16,24},{20,28},{24,16},{28,20},{1,9},{5... | collective-permute-start | bytes 294920 | tf_op jit(solution)/shard_map/ppermute | solution.py:342
  20.7 7.9 %collective-permute-start.6 = (f32[9,12,256]{2,1,0:T(8,128)S(1)}, f32[9,12,256]{2,1,0:T(8,128)S(1)}, u32[]{:S(2)}, u32[]{:S(2)}) collective-permute-start(f32[9,12,256]{2,1,0:T(8,128)S(1)} %get-tuple-element.38.refs_0_), channel_id=1, source_target_pairs={{0,3},{1,2},{2,1},{3,0},{4,7},{5,6},{6,5},{7,4},{8,11},{9,10},{10,... | collective-permute-start | bytes 331784 | tf_op jit(solution)/shard_map/ppermute | solution.py:342
  23.2 7.5 %collective-permute-start.5 = (f32[9,12,256]{2,1,0:T(8,128)S(1)}, f32[9,12,256]{2,1,0:T(8,128)S(1)}, u32[]{:S(2)}, u32[]{:S(2)}) collective-permute-start(f32[9,12,256]{2,1,0:T(8,128)S(1)} %get-tuple-element.38.refs_0_), channel_id=1, source_target_pairs={{0,2},{1,3},{2,0},{3,1},{4,6},{5,7},{6,4},{7,5},{8,10},{9,11},{10,... | collective-permute-start | bytes 331784 | tf_op jit(solution)/shard_map/ppermute | solution.py:342
  23.7 7.0 %collective-permute-start.4 = (f32[9,12,256]{2,1,0:T(8,128)S(1)}, f32[9,12,256]{2,1,0:T(8,128)S(1)}, u32[]{:S(2)}, u32[]{:S(2)}) collective-permute-start(f32[9,12,256]{2,1,0:T(8,128)S(1)} %get-tuple-element.38.refs_0_), channel_id=1, source_target_pairs={{0,1},{1,0},{2,3},{3,2},{4,5},{5,4},{6,7},{7,6},{8,9},{9,8},{10,11... | collective-permute-start | bytes 331784 | tf_op jit(solution)/shard_map/ppermute | solution.py:342
  25.5 7.0 %collective-permute-start.9 = (f32[9,4,256]{2,1,0:T(4,128)S(1)}, f32[9,4,256]{2,1,0:T(4,128)S(1)}, u32[]{:S(2)}, u32[]{:S(2)}) collective-permute-start(f32[9,4,256]{2,1,0:T(4,128)S(1)} %corr_second.1.refs_0_), channel_id=1, source_target_pairs={{0,3},{1,2},{2,1},{3,0},{4,7},{5,6},{6,5},{7,4},{8,11},{9,10},{10,... | collective-permute-start | bytes 110600 | tf_op jit(solution)/shard_map/ppermute | solution.py:342
  28.1 4.5 %collective-permute-start.8 = (f32[9,4,256]{2,1,0:T(4,128)S(1)}, f32[9,4,256]{2,1,0:T(4,128)S(1)}, u32[]{:S(2)}, u32[]{:S(2)}) collective-permute-start(f32[9,4,256]{2,1,0:T(4,128)S(1)} %corr_second.1.refs_0_), channel_id=1, source_target_pairs={{0,2},{1,3},{2,0},{3,1},{4,6},{5,7},{6,4},{7,5},{8,10},{9,11},{10,... | collective-permute-start | bytes 110600 | tf_op jit(solution)/shard_map/ppermute | solution.py:342
  28.6 4.0 %collective-permute-start.7 = (f32[9,4,256]{2,1,0:T(4,128)S(1)}, f32[9,4,256]{2,1,0:T(4,128)S(1)}, u32[]{:S(2)}, u32[]{:S(2)}) collective-permute-start(f32[9,4,256]{2,1,0:T(4,128)S(1)} %corr_second.1.refs_0_), channel_id=1, source_target_pairs={{0,1},{1,0},{2,3},{3,2},{4,5},{5,4},{6,7},{7,6},{8,9},{9,8},{10,11... | collective-permute-start | bytes 110600 | tf_op jit(solution)/shard_map/ppermute | solution.py:342
  35.8 2.1 %collective-permute-start.10 = (bf16[4,3,64,128]{3,2,1,0:T(8,128)(2,1)S(1)}, bf16[4,3,64,128]{3,2,1,0:T(8,128)(2,1)S(1)}, u32[]{:S(2)}, u32[]{:S(2)}) collective-permute-start(bf16[4,3,64,128]{3,2,1,0:T(8,128)(2,1)S(1)} %get-tuple-element.45), channel_id=1, source_target_pairs={{0,4},{4,0},{8,12},{12,8},{16,20},{20,16},{24,28},{28,24},{1,5},{5... | collective-permute-start | bytes 589832 | tf_op jit(solution)/shard_map/ppermute | solution.py:342
  38.0 7.6 %collective-permute-start.11 = (bf16[2,3,64,128]{3,2,1,0:T(8,128)(2,1)S(1)}, bf16[2,3,64,128]{3,2,1,0:T(8,128)(2,1)S(1)}, u32[]{:S(2)}, u32[]{:S(2)}) collective-permute-start(bf16[2,3,64,128]{3,2,1,0:T(8,128)(2,1)S(1)} %pad_maximum_fusion.3), channel_id=1, source_target_pairs={{0,24},{4,28},{8,16},{12,20},{16,8},{20,12},{24,0},{28,4},{1,25},{... | collective-permute-start | bytes 294920 | tf_op jit(solution)/shard_map/ppermute | solution.py:342
  40.6 9.0 %collective-permute-start.12 = (bf16[2,3,64,128]{3,2,1,0:T(8,128)(2,1)S(1)}, bf16[2,3,64,128]{3,2,1,0:T(8,128)(2,1)S(1)}, u32[]{:S(2)}, u32[]{:S(2)}) collective-permute-start(bf16[2,3,64,128]{3,2,1,0:T(8,128)(2,1)S(1)} %pad_maximum_fusion.4), channel_id=1, source_target_pairs={{0,16},{4,20},{8,24},{12,28},{16,0},{20,4},{24,8},{28,12},{1,17},{... | collective-permute-start | bytes 294920 | tf_op jit(solution)/shard_map/ppermute | solution.py:342
  40.7 8.9 %collective-permute-start.13 = (bf16[2,3,64,128]{3,2,1,0:T(8,128)(2,1)S(1)}, bf16[2,3,64,128]{3,2,1,0:T(8,128)(2,1)S(1)}, u32[]{:S(2)}, u32[]{:S(2)}) collective-permute-start(bf16[2,3,64,128]{3,2,1,0:T(8,128)(2,1)S(1)} %pad_maximum_fusion.5), channel_id=1, source_target_pairs={{0,8},{4,12},{8,0},{12,4},{16,24},{20,28},{24,16},{28,20},{1,9},{5... | collective-permute-start | bytes 294920 | tf_op jit(solution)/shard_map/ppermute | solution.py:342

commit v4 on v3

--- a/solution.py
+++ b/solution.py
@@ -14,10 +14,18 @@
 HALF_TILE = LANES // 2
 PHASES = 16
 WIDE = 32
-EARLY = 12
+EARLY = 14
 CHANS = 3
 WINDOW = 3 * LANES
 DEPTH = 7 * LANES
+
+
+def member(me, chips, step, other):
+    return 2 * ((me // 2 + step) & (chips - 1)) + ((me & 1) ^ other)
+
+
+def near_slot(q, me, chips):
+    return 2 * ((me // 2 - q // 2) & (chips - 1)) + ((q ^ me) & 1)
 
 
 def fetch(sources, targets, sems):
@@ -46,7 +54,7 @@
             scratch[c, r * stations:(r + 1) * stations, :] = piece.astype(jnp.float32)
         for j, keep_ref in enumerate(keep_refs):
             for i, ref in enumerate((keep_ref, swap_ref.at[j])):
-                station = rows_ref[me ^ (2 * j + i)]
+                station = rows_ref[member(me, len(keep_refs), j, i)]
                 picked = scratch[c, pl.ds(station, chunks, stride=stations), :]
                 ref[c] = picked.astype(jnp.bfloat16)
 
@@ -65,7 +73,8 @@
     for c in range(CHANS):
         pieces = [(2 * j + i, ref.at[i]) for j, ref in zip(order, returned[:-2]) for i in range(2)]
         for j, ref in pieces + [(0, returned[-2]), (1, returned[-1])]:
-            where = pl.ds(rows_ref[me ^ j], chunks, stride=stations)
+            station = rows_ref[member(me, len(order) - 1, j // 2, j % 2)]
+            where = pl.ds(station, chunks, stride=stations)
             scratch[c, where, :] = scratch[c, where, :] + ref[c].astype(jnp.float32)
         for r in range(chunks):
             piece = scratch[c, r * stations:(r + 1) * stations, :]
@@ -135,11 +144,12 @@
 
 def correlate(start, first_ref, second_ref, fan_ref, heads, corr_ref):
     me = lax.axis_index("stn")
+    chips = heads.shape[0] // 2
 
     def step(p, carry):
-        right = shifted_rows(fan_ref, second_ref[start + p] ^ me, WIDE)
+        right = shifted_rows(fan_ref, near_slot(second_ref[start + p], me, chips), WIDE)
         products = lax.dot_general(
-            heads[first_ref[start + p] ^ me], right, (((1,), (1,)), ((), ())),
+            heads[near_slot(first_ref[start + p], me, chips)], right, (((1,), (1,)), ((), ())),
             preferred_element_type=jnp.float32,
         )
         for a in range(CHANS):
@@ -243,8 +253,8 @@
         return q // 2 + (slots // 2) * (1 - q % 2)
 
     def fill(p, carry):
-        qf = first_ref[start + p] ^ me
-        qs = second_ref[start + p] ^ me
+        qf = near_slot(first_ref[start + p], me, slots // 2)
+        qs = near_slot(second_ref[start + p], me, slots // 2)
         for c in range(CHANS):
             at = pl.multiple_of(height * row_place(qf) + PHASES * c, PHASES)
             bands[qs, pl.ds(at, PHASES), :] = spread(
@@ -342,15 +352,14 @@
     return lax.ppermute(x, axis, [(k, k ^ bits) for k in range(count)])
 
 
-def across(swap, keep):
+def across(swap, keep, sign, first):
     chips = len(keep)
     got = flipped(swap, "stn", 1)
-    order = []
+    order = first(chips)
     blocks = []
-    for j in range(chips - 1, 0, -1):
-        moved = flipped(jnp.stack([keep[j], got[j]]), "stn", 2 * j)
-        order.append(j)
-        blocks.append(moved)
+    for j in order:
+        pairs = [(k, (k + 2 * sign * j) % (2 * chips)) for k in range(2 * chips)]
+        blocks.append(lax.ppermute(jnp.stack([keep[j], got[j]]), "stn", pairs))
     return order + [0, 0], blocks + [keep[0], got[0]]
 
 
@@ -435,7 +444,7 @@
         cost_estimate=cost,
         name="prep",
     )(swap, pair_first, pair_second, send_rows, lag_lo, lag_hi, seen)
-    order, arrived = across(swap, keep)
+    order, arrived = across(swap, keep, 1, lambda n: list(range(1,n)))
 
     corr, fan, heads = pl.pallas_call(
         functools.partial(corr_first_kernel, order),
@@ -510,7 +519,7 @@
         cost_estimate=cost,
         name="keep",
     )(bands, fan)
-    order, returned = across(swap, keep)
+    order, returned = across(swap, keep, -1, lambda n: list(range(n-1,0,-1)))
     stacked = pl.pallas_call(
         functools.partial(unpack_kernel, order),
         in_specs=[vmem()] * (chips + 2),

time: 51.7 us -> 50.9 us (0.985)
  waiting for transfers between devices: 15.6 us -> 12.5 us
  starting transfers between devices: 18.8 us -> 21.1 us
    ppermute x14 -> x8, waiting for transfers between devices: 15.6 us -> 2.08 us  [flipped(): return lax.ppermute(x, axis, [(k, k ^ bits) for k in range(count)])]
    ppermute x0 -> x6, starting transfers between devices: none -> 12.3 us  [across(): blocks.append(lax.ppermute(jnp.stack([keep[j], got[j]]), 'stn', pairs))]
    ppermute x0 -> x6, waiting for transfers between devices: none -> 10.5 us  [across(): blocks.append(lax.ppermute(jnp.stack([keep[j], got[j]]), 'stn', pairs))]
    ppermute x14 -> x8, starting transfers between devices: 18.8 us -> 8.81 us  [flipped(): return lax.ppermute(x, axis, [(k, k ^ bits) for k in range(count)])]
  transfers between devices with their start and end apart: 14 -> 14, of which waited for: 6 -> 7; matrix products, arithmetic and copies ran while one was open for 0% -> 0% of each run, Pallas kernels for 12% -> 12%
where the time goes in v4:
time: 50.9 us; the launch traced here: 50.7 us
  starting transfers between devices  21.1 us (41%)
  Pallas kernels  16.2 us (32%)
  waiting for transfers between devices  12.5 us (25%)
  between operations  0.77 us (2%)
    ppermute x6, starting transfers between devices, across(): blocks.append(lax.ppermute(jnp.stack([keep[j], got[j]]), 'stn', pairs))  12.3 us
    ppermute x6, waiting for transfers between devices, across(): blocks.append(lax.ppermute(jnp.stack([keep[j], got[j]]), 'stn', pairs))  10.5 us
    ppermute x8, starting transfers between devices, flipped(): return lax.ppermute(x, axis, [(k, k ^ bits) for k in range(count)])  8.81 us
    pallas_call x1, Pallas kernels, shards(): pl.pallas_call(functools.partial(corr_first_kernel, order), in_specs=[vme...  3.56 us
    pallas_call x1, Pallas kernels, shards(): pl.pallas_call(functools.partial(adjoint_kernel, corr_scale, adj_scale),...  3.02 us
    pallas_call x1, Pallas kernels, shards(): pl.pallas_call(functools.partial(bands_kernel, corr_scale), in_specs=[vme...  2.09 us
    ppermute x8, waiting for transfers between devices, flipped(): return lax.ppermute(x, axis, [(k, k ^ bits) for k in range(count)])  2.08 us
    pallas_call x1, Pallas kernels, shards(): pl.pallas_call(functools.partial(keep_kernel, adj_scale), in_specs=[vmem(...  2.05 us
  transfers between devices with their start and end apart: 14, of which 7 were waited for; matrix products, arithmetic and copies ran while one was open for 0% of the time, Pallas kernels for 12%

profile of v4, /device:TPU:0, one launch (start us, length us, event | category | flops | bytes accessed | tf_op | source)
XLA Modules:
  0.0 50.7 jit_solution(16043717305815149647)
XLA Ops:
  0.6 1.5 %pack.1 = (bf16[4,3,64,128]{3,2,1,0:T(8,128)(2,1)S(1)}, bf16[3,64,128]{2,1,0:T(8,128)(2,1)S(1)}, bf16[3,64,128]{2,1,0:T(8,128)(2,1)S(1)}, bf16[3,64,128]{2,1,0:T(8,128)(2,1)S(1)}, bf16[3,64,128]{2,1,0:T(8,128)(2,1)S(1)}) custom-call(s32[8]{0:T(128)} %bitcast.31, bf16[3,16,8192]{2,1,0:T(8,128)(2,1)} %bitcast.29), custom_call_target="tpu_custom_call" | custom-call | tf_op jit(solution)/shard_map/pack/pallas_call | solution.py:397
  2.1 0.5 %collective-permute-start = (bf16[4,3,64,128]{3,2,1,0:T(8,128)(2,1)S(1)}, bf16[4,3,64,128]{3,2,1,0:T(8,128)(2,1)S(1)}, u32[]{:S(2)}, u32[]{:S(2)}) collective-permute-start(bf16[4,3,64,128]{3,2,1,0:T(8,128)(2,1)S(1)} %get-tuple-element.26.token), channel_id=1, source_target_pairs={{0,4},{4,0},{8,12},{12,8},{16,20},{20,16},{24,28},{28,24},{1,5},{5... | collective-permute-start | bytes 589832 | tf_op jit(solution)/shard_map/ppermute | solution.py:352
  2.7 1.1 %collective-permute-done = bf16[4,3,64,128]{3,2,1,0:T(8,128)(2,1)S(1)} collective-permute-done((bf16[4,3,64,128]{3,2,1,0:T(8,128)(2,1)S(1)}, bf16[4,3,64,128]{3,2,1,0:T(8,128)(2,1)S(1)}, u32[]{:S(2)}, u32[]{:S(2)}) %collective-permute-start) | collective-permute-done | bytes 196640 | tf_op jit(solution)/shard_map/ppermute | solution.py:352
  3.8 3.0 %collective-permute-start.1 = (bf16[2,3,64,128]{3,2,1,0:T(8,128)(2,1)S(1)}, bf16[2,3,64,128]{3,2,1,0:T(8,128)(2,1)S(1)}, u32[]{:S(2)}, u32[]{:S(2)}) collective-permute-start(bf16[2,3,64,128]{3,2,1,0:T(8,128)(2,1)S(1)} %pad_maximum_fusion), channel_id=1, source_target_pairs={{0,8},{4,12},{8,16},{12,20},{16,24},{20,28},{24,0},{28,4},{1,9},{5... | collective-permute-start | bytes 294920 | tf_op jit(solution)/shard_map/ppermute | solution.py:362
  6.8 2.7 %collective-permute-start.2 = (bf16[2,3,64,128]{3,2,1,0:T(8,128)(2,1)S(1)}, bf16[2,3,64,128]{3,2,1,0:T(8,128)(2,1)S(1)}, u32[]{:S(2)}, u32[]{:S(2)}) collective-permute-start(bf16[2,3,64,128]{3,2,1,0:T(8,128)(2,1)S(1)} %pad_maximum_fusion.1), channel_id=1, source_target_pairs={{0,16},{4,20},{8,24},{12,28},{16,0},{20,4},{24,8},{28,12},{1,17},{... | collective-permute-start | bytes 294920 | tf_op jit(solution)/shard_map/ppermute | solution.py:362
  9.5 1.4 %collective-permute-start.3 = (bf16[2,3,64,128]{3,2,1,0:T(8,128)(2,1)S(1)}, bf16[2,3,64,128]{3,2,1,0:T(8,128)(2,1)S(1)}, u32[]{:S(2)}, u32[]{:S(2)}) collective-permute-start(bf16[2,3,64,128]{3,2,1,0:T(8,128)(2,1)S(1)} %pad_maximum_fusion.2), channel_id=1, source_target_pairs={{0,24},{4,28},{8,0},{12,4},{16,8},{20,12},{24,16},{28,20},{1,25},{... | collective-permute-start | bytes 294920 | tf_op jit(solution)/shard_map/ppermute | solution.py:362
  10.9 1.0 %prep.1 = (bf16[8,384,896]{2,1,0:T(8,128)(2,1)S(1)}, s32[16]{0:T(128)S(1)}, s32[16]{0:T(128)S(1)}, s32[8]{0:T(128)S(1)}, s32[16,256]{1,0:T(8,128)S(1)}, /*index=...) custom-call(bf16[4,3,64,128]{3,2,1,0:T(8,128)(2,1)S(1)} %get-tuple-element.26.token, s32[16]{0:T(128)} %first_in.1, ...), custom_call_target="tpu_custom_call" | custom-call | flops 2000000000 | bytes 4194304 | tf_op jit(solution)/shard_map/prep/pallas_call | solution.py:424
  11.9 0.6 %collective-permute-done.1.refs_0_ = bf16[2,3,64,128]{3,2,1,0:T(8,128)(2,1)S(1)} collective-permute-done((bf16[2,3,64,128]{3,2,1,0:T(8,128)(2,1)S(1)}, bf16[2,3,64,128]{3,2,1,0:T(8,128)(2,1)S(1)}, u32[]{:S(2)}, u32[]{:S(2)}) %collective-permute-start.1) | collective-permute-done | bytes 98336 | tf_op jit(solution)/shard_map/ppermute | solution.py:362
  12.5 3.8 %collective-permute-done.2.refs_1_ = bf16[2,3,64,128]{3,2,1,0:T(8,128)(2,1)S(1)} collective-permute-done((bf16[2,3,64,128]{3,2,1,0:T(8,128)(2,1)S(1)}, bf16[2,3,64,128]{3,2,1,0:T(8,128)(2,1)S(1)}, u32[]{:S(2)}, u32[]{:S(2)}) %collective-permute-start.2) | collective-permute-done | bytes 98336 | tf_op jit(solution)/shard_map/ppermute | solution.py:362
  16.2 0.0 collective-permute-done.3.refs_2_
  16.2 3.6 %corr_first.1 = (f32[9,14,256]{2,1,0:T(8,128)S(1)}, bf16[24,320,128]{2,1,0:T(8,128)(2,1)S(1)}, bf16[8,96,256]{2,1,0:T(8,128)(2,1)S(1)}) custom-call(s32[16]{0:T(128)S(1)} %get-tuple-element.28.first_in.first_ref, s32[16]{0:T(128)S(1)} %get-tuple-element.29.second_in.second_ref, bf16[2,3,64,128]{3,2,1,0:T(8,128)(2,1)S(1)} %collective-permute-done.1.refs_0_, ...), custom_call_target="tpu_custom_call" | custom-call | flops 2000000000 | bytes 4194304 | tf_op jit(solution)/shard_map/corr_first/pallas_call | solution.py:449
  19.8 2.6 %collective-permute-start.6 = (f32[9,14,256]{2,1,0:T(8,128)S(1)}, f32[9,14,256]{2,1,0:T(8,128)S(1)}, u32[]{:S(2)}, u32[]{:S(2)}) collective-permute-start(f32[9,14,256]{2,1,0:T(8,128)S(1)} %get-tuple-element.38.refs_0_), channel_id=1, source_target_pairs={{0,3},{1,2},{2,1},{3,0},{4,7},{5,6},{6,5},{7,4},{8,11},{9,10},{10,... | collective-permute-start | bytes 387080 | tf_op jit(solution)/shard_map/ppermute | solution.py:352
  22.4 0.5 collective-permute-start.5
  22.9 0.5 collective-permute-start.4
  23.4 1.1 %corr_second.1.refs_0_ = f32[9,2,256]{2,1,0:T(2,128)S(1)} custom-call(s32[16]{0:T(128)S(1)} %get-tuple-element.28.first_in.first_ref, s32[16]{0:T(128)S(1)} %get-tuple-element.29.second_in.second_ref, bf16[24,320,128]{2,1,0:T(8,128)(2,1)S(1)} %get-tuple-element.40.fan_ref, bf16[8,96,256]{2,1,0:T(8,128)(2,1)S(1)} %get-tuple-element.42.heads), custom_call_target="tpu_custom_call" | custom-call | flops 2000000000 | bytes 4194304 | tf_op jit(solution)/shard_map/corr_second/pallas_call | solution.py:466
  24.4 2.6 %collective-permute-start.9 = (f32[9,2,256]{2,1,0:T(2,128)S(1)}, f32[9,2,256]{2,1,0:T(2,128)S(1)}, u32[]{:S(2)}, u32[]{:S(2)}) collective-permute-start(f32[9,2,256]{2,1,0:T(2,128)S(1)} %corr_second.1.refs_0_), channel_id=1, source_target_pairs={{0,3},{1,2},{2,1},{3,0},{4,7},{5,6},{6,5},{7,4},{8,11},{9,10},{10,... | collective-permute-start | bytes 55304 | tf_op jit(solution)/shard_map/ppermute | solution.py:352
  27.0 0.5 collective-permute-start.8
  27.5 0.0 collective-permute-done.6.refs_3_
  27.5 1.6 %collective-permute-start.7 = (f32[9,2,256]{2,1,0:T(2,128)S(1)}, f32[9,2,256]{2,1,0:T(2,128)S(1)}, u32[]{:S(2)}, u32[]{:S(2)}) collective-permute-start(f32[9,2,256]{2,1,0:T(2,128)S(1)} %corr_second.1.refs_0_), channel_id=1, source_target_pairs={{0,1},{1,0},{2,3},{3,2},{4,5},{5,4},{6,7},{7,6},{8,9},{9,8},{10,11... | collective-permute-start | bytes 55304 | tf_op jit(solution)/shard_map/ppermute | solution.py:352
  29.1 0.8 %collective-permute-done.5.refs_2_ = f32[9,14,256]{2,1,0:T(8,128)S(1)} collective-permute-done((f32[9,14,256]{2,1,0:T(8,128)S(1)}, f32[9,14,256]{2,1,0:T(8,128)S(1)}, u32[]{:S(2)}, u32[]{:S(2)}) %collective-permute-start.5) | collective-permute-done | bytes 129056 | tf_op jit(solution)/shard_map/ppermute | solution.py:352
  29.9 0.2 collective-permute-done.4.refs_1_
  30.1 2.1 %bands.1 = (bf16[8,384,896]{2,1,0:T(8,128)(2,1)S(1)}, f32[9,14,256]{2,1,0:T(8,128)S(1)}) custom-call(s32[16]{0:T(128)S(1)} %get-tuple-element.28.first_in.first_ref, s32[16]{0:T(128)S(1)} %get-tuple-element.29.second_in.second_ref, s32[16,256]{1,0:T(8,128)S(1)} %get-tuple-element.30.inside_ref, ...), custom_call_target="tpu_custom_call", output_to_operand_aliasing={{0}: (4, {})} | custom-call | flops 2000000000 | bytes 4194304 | tf_op jit(solution)/shard_map/bands/pallas_call | solution.py:478
  32.2 0.0 collective-permute-done.9.refs_3_
  32.2 0.0 collective-permute-done.8.refs_2_
  32.2 0.0 collective-permute-done.7.refs_1_
  32.2 3.0 %adjoint.1 = (bf16[8,384,896]{2,1,0:T(8,128)(2,1)S(1)}, bf16[4,3,64,128]{3,2,1,0:T(8,128)(2,1)S(1)}, f32[9,4,256]{2,1,0:T(4,128)}) custom-call(s32[16]{0:T(128)S(1)} %get-tuple-element.28.first_in.first_ref, s32[16]{0:T(128)S(1)} %get-tuple-element.29.second_in.second_ref, ...), custom_call_target="tpu_custom_call", output_to_operand_aliasing={{0}: (4, {})} | custom-call | flops 2000000000 | bytes 4194304 | tf_op jit(solution)/shard_map/adjoint/pallas_call | solution.py:493
  35.3 0.1 collective-permute-start.10
  35.3 2.1 %keep.1 = (bf16[3,64,128]{2,1,0:T(8,128)(2,1)S(1)}, bf16[3,64,128]{2,1,0:T(8,128)(2,1)S(1)}, bf16[3,64,128]{2,1,0:T(8,128)(2,1)S(1)}, bf16[3,64,128]{2,1,0:T(8,128)(2,1)S(1)}) custom-call(bf16[8,384,896]{2,1,0:T(8,128)(2,1)S(1)} %get-tuple-element.43.bands, bf16[24,320,128]{2,1,0:T(8,128)(2,1)S(1)} %get-tuple-element.40.fan_ref), custom_call_target="tpu_custom_call" | custom-call | flops 2000000000 | bytes 4194304 | tf_op jit(solution)/shard_map/keep/pallas_call | solution.py:512
  37.4 0.0 collective-permute-done.10
  37.5 2.7 %collective-permute-start.11 = (bf16[2,3,64,128]{3,2,1,0:T(8,128)(2,1)S(1)}, bf16[2,3,64,128]{3,2,1,0:T(8,128)(2,1)S(1)}, u32[]{:S(2)}, u32[]{:S(2)}) collective-permute-start(bf16[2,3,64,128]{3,2,1,0:T(8,128)(2,1)S(1)} %pad_maximum_fusion.3), channel_id=1, source_target_pairs={{0,8},{4,12},{8,16},{12,20},{16,24},{20,28},{24,0},{28,4},{1,9},{5... | collective-permute-start | bytes 294920 | tf_op jit(solution)/shard_map/ppermute | solution.py:362
  40.2 0.9 %collective-permute-start.12 = (bf16[2,3,64,128]{3,2,1,0:T(8,128)(2,1)S(1)}, bf16[2,3,64,128]{3,2,1,0:T(8,128)(2,1)S(1)}, u32[]{:S(2)}, u32[]{:S(2)}) collective-permute-start(bf16[2,3,64,128]{3,2,1,0:T(8,128)(2,1)S(1)} %pad_maximum_fusion.4), channel_id=1, source_target_pairs={{0,16},{4,20},{8,24},{12,28},{16,0},{20,4},{24,8},{28,12},{1,17},{... | collective-permute-start | bytes 294920 | tf_op jit(solution)/shard_map/ppermute | solution.py:362
  41.1 1.6 %collective-permute-start.13 = (bf16[2,3,64,128]{3,2,1,0:T(8,128)(2,1)S(1)}, bf16[2,3,64,128]{3,2,1,0:T(8,128)(2,1)S(1)}, u32[]{:S(2)}, u32[]{:S(2)}) collective-permute-start(bf16[2,3,64,128]{3,2,1,0:T(8,128)(2,1)S(1)} %pad_maximum_fusion.5), channel_id=1, source_target_pairs={{0,24},{4,28},{8,0},{12,4},{16,8},{20,12},{24,16},{28,20},{1,25},{... | collective-permute-start | bytes 294920 | tf_op jit(solution)/shard_map/ppermute | solution.py:362
  42.7 2.3 %collective-permute-done.11.refs_0_ = bf16[2,3,64,128]{3,2,1,0:T(8,128)(2,1)S(1)} collective-permute-done((bf16[2,3,64,128]{3,2,1,0:T(8,128)(2,1)S(1)}, bf16[2,3,64,128]{3,2,1,0:T(8,128)(2,1)S(1)}, u32[]{:S(2)}, u32[]{:S(2)}) %collective-permute-start.11) | collective-permute-done | bytes 98336 | tf_op jit(solution)/shard_map/ppermute | solution.py:362
  45.0 3.8 %collective-permute-done.12.refs_1_ = bf16[2,3,64,128]{3,2,1,0:T(8,128)(2,1)S(1)} collective-permute-done((bf16[2,3,64,128]{3,2,1,0:T(8,128)(2,1)S(1)}, bf16[2,3,64,128]{3,2,1,0:T(8,128)(2,1)S(1)}, u32[]{:S(2)}, u32[]{:S(2)}) %collective-permute-start.12) | collective-permute-done | bytes 98336 | tf_op jit(solution)/shard_map/ppermute | solution.py:362
  48.8 0.0 collective-permute-done.13.refs_2_
  48.8 2.0 %unpack.1 = bf16[3,16,8192]{2,1,0:T(8,128)(2,1)} custom-call(s32[8]{0:T(128)S(1)} %get-tuple-element.27.rows_in, bf16[2,3,64,128]{3,2,1,0:T(8,128)(2,1)S(1)} %collective-permute-done.11.refs_0_, bf16[2,3,64,128]{3,2,1,0:T(8,128)(2,1)S(1)} %collective-permute-done.12.refs_1_, bf16[2,3,64,128]{3,2,1,0:T(8,128)(2,1)S(1)} %collective-permute-done.13.refs_2_, ...), custom_call_target="tpu_custom_call" | custom-call | tf_op jit(solution)/shard_map/unpack/pallas_call | solution.py:523
  (8 shorter events, 0.1 us)
Async XLA Ops:
  2.1 1.6 %collective-permute-start = (bf16[4,3,64,128]{3,2,1,0:T(8,128)(2,1)S(1)}, bf16[4,3,64,128]{3,2,1,0:T(8,128)(2,1)S(1)}, u32[]{:S(2)}, u32[]{:S(2)}) collective-permute-start(bf16[4,3,64,128]{3,2,1,0:T(8,128)(2,1)S(1)} %get-tuple-element.26.token), channel_id=1, source_target_pairs={{0,4},{4,0},{8,12},{12,8},{16,20},{20,16},{24,28},{28,24},{1,5},{5... | collective-permute-start | bytes 589832 | tf_op jit(solution)/shard_map/ppermute | solution.py:352
  3.8 8.7 %collective-permute-start.1 = (bf16[2,3,64,128]{3,2,1,0:T(8,128)(2,1)S(1)}, bf16[2,3,64,128]{3,2,1,0:T(8,128)(2,1)S(1)}, u32[]{:S(2)}, u32[]{:S(2)}) collective-permute-start(bf16[2,3,64,128]{3,2,1,0:T(8,128)(2,1)S(1)} %pad_maximum_fusion), channel_id=1, source_target_pairs={{0,8},{4,12},{8,16},{12,20},{16,24},{20,28},{24,0},{28,4},{1,9},{5... | collective-permute-start | bytes 294920 | tf_op jit(solution)/shard_map/ppermute | solution.py:362
  6.8 9.4 %collective-permute-start.2 = (bf16[2,3,64,128]{3,2,1,0:T(8,128)(2,1)S(1)}, bf16[2,3,64,128]{3,2,1,0:T(8,128)(2,1)S(1)}, u32[]{:S(2)}, u32[]{:S(2)}) collective-permute-start(bf16[2,3,64,128]{3,2,1,0:T(8,128)(2,1)S(1)} %pad_maximum_fusion.1), channel_id=1, source_target_pairs={{0,16},{4,20},{8,24},{12,28},{16,0},{20,4},{24,8},{28,12},{1,17},{... | collective-permute-start | bytes 294920 | tf_op jit(solution)/shard_map/ppermute | solution.py:362
  9.5 6.8 %collective-permute-start.3 = (bf16[2,3,64,128]{3,2,1,0:T(8,128)(2,1)S(1)}, bf16[2,3,64,128]{3,2,1,0:T(8,128)(2,1)S(1)}, u32[]{:S(2)}, u32[]{:S(2)}) collective-permute-start(bf16[2,3,64,128]{3,2,1,0:T(8,128)(2,1)S(1)} %pad_maximum_fusion.2), channel_id=1, source_target_pairs={{0,24},{4,28},{8,0},{12,4},{16,8},{20,12},{24,16},{28,20},{1,25},{... | collective-permute-start | bytes 294920 | tf_op jit(solution)/shard_map/ppermute | solution.py:362
  19.8 7.7 %collective-permute-start.6 = (f32[9,14,256]{2,1,0:T(8,128)S(1)}, f32[9,14,256]{2,1,0:T(8,128)S(1)}, u32[]{:S(2)}, u32[]{:S(2)}) collective-permute-start(f32[9,14,256]{2,1,0:T(8,128)S(1)} %get-tuple-element.38.refs_0_), channel_id=1, source_target_pairs={{0,3},{1,2},{2,1},{3,0},{4,7},{5,6},{6,5},{7,4},{8,11},{9,10},{10,... | collective-permute-start | bytes 387080 | tf_op jit(solution)/shard_map/ppermute | solution.py:352
  22.4 7.5 %collective-permute-start.5 = (f32[9,14,256]{2,1,0:T(8,128)S(1)}, f32[9,14,256]{2,1,0:T(8,128)S(1)}, u32[]{:S(2)}, u32[]{:S(2)}) collective-permute-start(f32[9,14,256]{2,1,0:T(8,128)S(1)} %get-tuple-element.38.refs_0_), channel_id=1, source_target_pairs={{0,2},{1,3},{2,0},{3,1},{4,6},{5,7},{6,4},{7,5},{8,10},{9,11},{10,... | collective-permute-start | bytes 387080 | tf_op jit(solution)/shard_map/ppermute | solution.py:352
  22.9 7.2 %collective-permute-start.4 = (f32[9,14,256]{2,1,0:T(8,128)S(1)}, f32[9,14,256]{2,1,0:T(8,128)S(1)}, u32[]{:S(2)}, u32[]{:S(2)}) collective-permute-start(f32[9,14,256]{2,1,0:T(8,128)S(1)} %get-tuple-element.38.refs_0_), channel_id=1, source_target_pairs={{0,1},{1,0},{2,3},{3,2},{4,5},{5,4},{6,7},{7,6},{8,9},{9,8},{10,11... | collective-permute-start | bytes 387080 | tf_op jit(solution)/shard_map/ppermute | solution.py:352
  24.4 7.8 %collective-permute-start.9 = (f32[9,2,256]{2,1,0:T(2,128)S(1)}, f32[9,2,256]{2,1,0:T(2,128)S(1)}, u32[]{:S(2)}, u32[]{:S(2)}) collective-permute-start(f32[9,2,256]{2,1,0:T(2,128)S(1)} %corr_second.1.refs_0_), channel_id=1, source_target_pairs={{0,3},{1,2},{2,1},{3,0},{4,7},{5,6},{6,5},{7,4},{8,11},{9,10},{10,... | collective-permute-start | bytes 55304 | tf_op jit(solution)/shard_map/ppermute | solution.py:352
  27.0 5.2 %collective-permute-start.8 = (f32[9,2,256]{2,1,0:T(2,128)S(1)}, f32[9,2,256]{2,1,0:T(2,128)S(1)}, u32[]{:S(2)}, u32[]{:S(2)}) collective-permute-start(f32[9,2,256]{2,1,0:T(2,128)S(1)} %corr_second.1.refs_0_), channel_id=1, source_target_pairs={{0,2},{1,3},{2,0},{3,1},{4,6},{5,7},{6,4},{7,5},{8,10},{9,11},{10,... | collective-permute-start | bytes 55304 | tf_op jit(solution)/shard_map/ppermute | solution.py:352
  27.5 4.7 %collective-permute-start.7 = (f32[9,2,256]{2,1,0:T(2,128)S(1)}, f32[9,2,256]{2,1,0:T(2,128)S(1)}, u32[]{:S(2)}, u32[]{:S(2)}) collective-permute-start(f32[9,2,256]{2,1,0:T(2,128)S(1)} %corr_second.1.refs_0_), channel_id=1, source_target_pairs={{0,1},{1,0},{2,3},{3,2},{4,5},{5,4},{6,7},{7,6},{8,9},{9,8},{10,11... | collective-permute-start | bytes 55304 | tf_op jit(solution)/shard_map/ppermute | solution.py:352
  35.3 2.1 %collective-permute-start.10 = (bf16[4,3,64,128]{3,2,1,0:T(8,128)(2,1)S(1)}, bf16[4,3,64,128]{3,2,1,0:T(8,128)(2,1)S(1)}, u32[]{:S(2)}, u32[]{:S(2)}) collective-permute-start(bf16[4,3,64,128]{3,2,1,0:T(8,128)(2,1)S(1)} %get-tuple-element.45), channel_id=1, source_target_pairs={{0,4},{4,0},{8,12},{12,8},{16,20},{20,16},{24,28},{28,24},{1,5},{5... | collective-permute-start | bytes 589832 | tf_op jit(solution)/shard_map/ppermute | solution.py:352
  37.5 7.5 %collective-permute-start.11 = (bf16[2,3,64,128]{3,2,1,0:T(8,128)(2,1)S(1)}, bf16[2,3,64,128]{3,2,1,0:T(8,128)(2,1)S(1)}, u32[]{:S(2)}, u32[]{:S(2)}) collective-permute-start(bf16[2,3,64,128]{3,2,1,0:T(8,128)(2,1)S(1)} %pad_maximum_fusion.3), channel_id=1, source_target_pairs={{0,8},{4,12},{8,16},{12,20},{16,24},{20,28},{24,0},{28,4},{1,9},{5... | collective-permute-start | bytes 294920 | tf_op jit(solution)/shard_map/ppermute | solution.py:362
  40.2 8.6 %collective-permute-start.12 = (bf16[2,3,64,128]{3,2,1,0:T(8,128)(2,1)S(1)}, bf16[2,3,64,128]{3,2,1,0:T(8,128)(2,1)S(1)}, u32[]{:S(2)}, u32[]{:S(2)}) collective-permute-start(bf16[2,3,64,128]{3,2,1,0:T(8,128)(2,1)S(1)} %pad_maximum_fusion.4), channel_id=1, source_target_pairs={{0,16},{4,20},{8,24},{12,28},{16,0},{20,4},{24,8},{28,12},{1,17},{... | collective-permute-start | bytes 294920 | tf_op jit(solution)/shard_map/ppermute | solution.py:362
  41.1 7.7 %collective-permute-start.13 = (bf16[2,3,64,128]{3,2,1,0:T(8,128)(2,1)S(1)}, bf16[2,3,64,128]{3,2,1,0:T(8,128)(2,1)S(1)}, u32[]{:S(2)}, u32[]{:S(2)}) collective-permute-start(bf16[2,3,64,128]{3,2,1,0:T(8,128)(2,1)S(1)} %pad_maximum_fusion.5), channel_id=1, source_target_pairs={{0,24},{4,28},{8,0},{12,4},{16,8},{20,12},{24,16},{28,20},{1,25},{... | collective-permute-start | bytes 294920 | tf_op jit(solution)/shard_map/ppermute | solution.py:362

commit v5 on v4

--- a/solution.py
+++ b/solution.py
@@ -271,15 +271,17 @@
 
 def contract(adj_scale, first_row, bands, fan_ref, total, outs):
     rows = total.shape[0]
-    total[...] = jnp.zeros_like(total)
-
-    def accumulate(r, carry):
-        right = shifted_rows(fan_ref, r, PHASES)
-        left = bands[r, first_row:first_row + rows, :]
-        total[...] += jnp.dot(left, right, preferred_element_type=jnp.float32)
-        return carry
-
-    lax.fori_loop(0, bands.shape[0], accumulate, 0, unroll=8)
+    slots = bands.shape[0]
+    group = 2
+    for r in range(0, slots, group):
+        right = jnp.concatenate(
+            [shifted_rows(fan_ref, q, PHASES) for q in range(r, r + group)], axis=0
+        )
+        left = jnp.concatenate(
+            [bands[q, first_row:first_row + rows, :] for q in range(r, r + group)], axis=1
+        )
+        product = jnp.dot(left, right, preferred_element_type=jnp.float32)
+        total[...] = product if r == 0 else total[...] + product
     chunks = outs[0].shape[1]
     near = lax.broadcasted_iota(jnp.int32, (PHASES, LANES), 1) < chunks
     for place in range(0, rows // PHASES, 2):

time: 50.9 us -> 50.5 us (level)
  no operation moved by 1% of the time
where the time goes in v5:
time: 50.5 us; the launch traced here: 50.3 us
  starting transfers between devices  21.1 us (42%)
  Pallas kernels  15.8 us (31%)
  waiting for transfers between devices  12.5 us (25%)
  between operations  0.77 us (2%)
    ppermute x6, starting transfers between devices, across(): blocks.append(lax.ppermute(jnp.stack([keep[j], got[j]]), 'stn', pairs))  12.3 us
    ppermute x6, waiting for transfers between devices, across(): blocks.append(lax.ppermute(jnp.stack([keep[j], got[j]]), 'stn', pairs))  10.4 us
    ppermute x8, starting transfers between devices, flipped(): return lax.ppermute(x, axis, [(k, k ^ bits) for k in range(count)])  8.81 us
    pallas_call x1, Pallas kernels, shards(): pl.pallas_call(functools.partial(corr_first_kernel, order), in_specs=[vme...  3.56 us
    pallas_call x1, Pallas kernels, shards(): pl.pallas_call(functools.partial(adjoint_kernel, corr_scale, adj_scale),...  2.82 us
    pallas_call x1, Pallas kernels, shards(): pl.pallas_call(functools.partial(bands_kernel, corr_scale), in_specs=[vme...  2.09 us
    ppermute x8, waiting for transfers between devices, flipped(): return lax.ppermute(x, axis, [(k, k ^ bits) for k in range(count)])  2.08 us
    pallas_call x1, Pallas kernels, shards(): pl.pallas_call(functools.partial(unpack_kernel, order), in_specs=[vmem()]...  1.96 us
  transfers between devices with their start and end apart: 14, of which 7 were waited for; matrix products, arithmetic and copies ran while one was open for 0% of the time, Pallas kernels for 12%

profile of v5, /device:TPU:0, one launch (start us, length us, event | category | flops | bytes accessed | tf_op | source)
XLA Modules:
  0.0 50.3 jit_solution(1279710068985161048)
XLA Ops:
  0.6 1.5 %pack.1 = (bf16[4,3,64,128]{3,2,1,0:T(8,128)(2,1)S(1)}, bf16[3,64,128]{2,1,0:T(8,128)(2,1)S(1)}, bf16[3,64,128]{2,1,0:T(8,128)(2,1)S(1)}, bf16[3,64,128]{2,1,0:T(8,128)(2,1)S(1)}, bf16[3,64,128]{2,1,0:T(8,128)(2,1)S(1)}) custom-call(s32[8]{0:T(128)} %bitcast.31, bf16[3,16,8192]{2,1,0:T(8,128)(2,1)} %bitcast.29), custom_call_target="tpu_custom_call" | custom-call | tf_op jit(solution)/shard_map/pack/pallas_call | solution.py:399
  2.1 0.5 %collective-permute-start = (bf16[4,3,64,128]{3,2,1,0:T(8,128)(2,1)S(1)}, bf16[4,3,64,128]{3,2,1,0:T(8,128)(2,1)S(1)}, u32[]{:S(2)}, u32[]{:S(2)}) collective-permute-start(bf16[4,3,64,128]{3,2,1,0:T(8,128)(2,1)S(1)} %get-tuple-element.26.token), channel_id=1, source_target_pairs={{0,4},{4,0},{8,12},{12,8},{16,20},{20,16},{24,28},{28,24},{1,5},{5... | collective-permute-start | bytes 589832 | tf_op jit(solution)/shard_map/ppermute | solution.py:354
  2.7 1.1 %collective-permute-done = bf16[4,3,64,128]{3,2,1,0:T(8,128)(2,1)S(1)} collective-permute-done((bf16[4,3,64,128]{3,2,1,0:T(8,128)(2,1)S(1)}, bf16[4,3,64,128]{3,2,1,0:T(8,128)(2,1)S(1)}, u32[]{:S(2)}, u32[]{:S(2)}) %collective-permute-start) | collective-permute-done | bytes 196640 | tf_op jit(solution)/shard_map/ppermute | solution.py:354
  3.8 3.0 %collective-permute-start.1 = (bf16[2,3,64,128]{3,2,1,0:T(8,128)(2,1)S(1)}, bf16[2,3,64,128]{3,2,1,0:T(8,128)(2,1)S(1)}, u32[]{:S(2)}, u32[]{:S(2)}) collective-permute-start(bf16[2,3,64,128]{3,2,1,0:T(8,128)(2,1)S(1)} %pad_maximum_fusion), channel_id=1, source_target_pairs={{0,8},{4,12},{8,16},{12,20},{16,24},{20,28},{24,0},{28,4},{1,9},{5... | collective-permute-start | bytes 294920 | tf_op jit(solution)/shard_map/ppermute | solution.py:364
  6.8 2.7 %collective-permute-start.2 = (bf16[2,3,64,128]{3,2,1,0:T(8,128)(2,1)S(1)}, bf16[2,3,64,128]{3,2,1,0:T(8,128)(2,1)S(1)}, u32[]{:S(2)}, u32[]{:S(2)}) collective-permute-start(bf16[2,3,64,128]{3,2,1,0:T(8,128)(2,1)S(1)} %pad_maximum_fusion.1), channel_id=1, source_target_pairs={{0,16},{4,20},{8,24},{12,28},{16,0},{20,4},{24,8},{28,12},{1,17},{... | collective-permute-start | bytes 294920 | tf_op jit(solution)/shard_map/ppermute | solution.py:364
  9.5 1.4 %collective-permute-start.3 = (bf16[2,3,64,128]{3,2,1,0:T(8,128)(2,1)S(1)}, bf16[2,3,64,128]{3,2,1,0:T(8,128)(2,1)S(1)}, u32[]{:S(2)}, u32[]{:S(2)}) collective-permute-start(bf16[2,3,64,128]{3,2,1,0:T(8,128)(2,1)S(1)} %pad_maximum_fusion.2), channel_id=1, source_target_pairs={{0,24},{4,28},{8,0},{12,4},{16,8},{20,12},{24,16},{28,20},{1,25},{... | collective-permute-start | bytes 294920 | tf_op jit(solution)/shard_map/ppermute | solution.py:364
  10.9 1.0 %prep.1 = (bf16[8,384,896]{2,1,0:T(8,128)(2,1)S(1)}, s32[16]{0:T(128)S(1)}, s32[16]{0:T(128)S(1)}, s32[8]{0:T(128)S(1)}, s32[16,256]{1,0:T(8,128)S(1)}, /*index=...) custom-call(bf16[4,3,64,128]{3,2,1,0:T(8,128)(2,1)S(1)} %get-tuple-element.26.token, s32[16]{0:T(128)} %first_in.1, ...), custom_call_target="tpu_custom_call" | custom-call | flops 2000000000 | bytes 4194304 | tf_op jit(solution)/shard_map/prep/pallas_call | solution.py:426
  11.9 0.6 %collective-permute-done.1.refs_0_ = bf16[2,3,64,128]{3,2,1,0:T(8,128)(2,1)S(1)} collective-permute-done((bf16[2,3,64,128]{3,2,1,0:T(8,128)(2,1)S(1)}, bf16[2,3,64,128]{3,2,1,0:T(8,128)(2,1)S(1)}, u32[]{:S(2)}, u32[]{:S(2)}) %collective-permute-start.1) | collective-permute-done | bytes 98336 | tf_op jit(solution)/shard_map/ppermute | solution.py:364
  12.5 3.8 %collective-permute-done.2.refs_1_ = bf16[2,3,64,128]{3,2,1,0:T(8,128)(2,1)S(1)} collective-permute-done((bf16[2,3,64,128]{3,2,1,0:T(8,128)(2,1)S(1)}, bf16[2,3,64,128]{3,2,1,0:T(8,128)(2,1)S(1)}, u32[]{:S(2)}, u32[]{:S(2)}) %collective-permute-start.2) | collective-permute-done | bytes 98336 | tf_op jit(solution)/shard_map/ppermute | solution.py:364
  16.2 0.0 collective-permute-done.3.refs_2_
  16.2 3.6 %corr_first.1 = (f32[9,14,256]{2,1,0:T(8,128)S(1)}, bf16[24,320,128]{2,1,0:T(8,128)(2,1)S(1)}, bf16[8,96,256]{2,1,0:T(8,128)(2,1)S(1)}) custom-call(s32[16]{0:T(128)S(1)} %get-tuple-element.28.first_in.first_ref, s32[16]{0:T(128)S(1)} %get-tuple-element.29.second_in.second_ref, bf16[2,3,64,128]{3,2,1,0:T(8,128)(2,1)S(1)} %collective-permute-done.1.refs_0_, ...), custom_call_target="tpu_custom_call" | custom-call | flops 2000000000 | bytes 4194304 | tf_op jit(solution)/shard_map/corr_first/pallas_call | solution.py:451
  19.8 2.6 %collective-permute-start.6 = (f32[9,14,256]{2,1,0:T(8,128)S(1)}, f32[9,14,256]{2,1,0:T(8,128)S(1)}, u32[]{:S(2)}, u32[]{:S(2)}) collective-permute-start(f32[9,14,256]{2,1,0:T(8,128)S(1)} %get-tuple-element.38.refs_0_), channel_id=1, source_target_pairs={{0,3},{1,2},{2,1},{3,0},{4,7},{5,6},{6,5},{7,4},{8,11},{9,10},{10,... | collective-permute-start | bytes 387080 | tf_op jit(solution)/shard_map/ppermute | solution.py:354
  22.4 0.5 %collective-permute-start.5 = (f32[9,14,256]{2,1,0:T(8,128)S(1)}, f32[9,14,256]{2,1,0:T(8,128)S(1)}, u32[]{:S(2)}, u32[]{:S(2)}) collective-permute-start(f32[9,14,256]{2,1,0:T(8,128)S(1)} %get-tuple-element.38.refs_0_), channel_id=1, source_target_pairs={{0,2},{1,3},{2,0},{3,1},{4,6},{5,7},{6,4},{7,5},{8,10},{9,11},{10,... | collective-permute-start | bytes 387080 | tf_op jit(solution)/shard_map/ppermute | solution.py:354
  22.9 0.5 collective-permute-start.4
  23.4 1.1 %corr_second.1.refs_0_ = f32[9,2,256]{2,1,0:T(2,128)S(1)} custom-call(s32[16]{0:T(128)S(1)} %get-tuple-element.28.first_in.first_ref, s32[16]{0:T(128)S(1)} %get-tuple-element.29.second_in.second_ref, bf16[24,320,128]{2,1,0:T(8,128)(2,1)S(1)} %get-tuple-element.40.fan_ref, bf16[8,96,256]{2,1,0:T(8,128)(2,1)S(1)} %get-tuple-element.42.heads), custom_call_target="tpu_custom_call" | custom-call | flops 2000000000 | bytes 4194304 | tf_op jit(solution)/shard_map/corr_second/pallas_call | solution.py:468
  24.4 2.6 %collective-permute-start.9 = (f32[9,2,256]{2,1,0:T(2,128)S(1)}, f32[9,2,256]{2,1,0:T(2,128)S(1)}, u32[]{:S(2)}, u32[]{:S(2)}) collective-permute-start(f32[9,2,256]{2,1,0:T(2,128)S(1)} %corr_second.1.refs_0_), channel_id=1, source_target_pairs={{0,3},{1,2},{2,1},{3,0},{4,7},{5,6},{6,5},{7,4},{8,11},{9,10},{10,... | collective-permute-start | bytes 55304 | tf_op jit(solution)/shard_map/ppermute | solution.py:354
  27.0 0.5 %collective-permute-start.8 = (f32[9,2,256]{2,1,0:T(2,128)S(1)}, f32[9,2,256]{2,1,0:T(2,128)S(1)}, u32[]{:S(2)}, u32[]{:S(2)}) collective-permute-start(f32[9,2,256]{2,1,0:T(2,128)S(1)} %corr_second.1.refs_0_), channel_id=1, source_target_pairs={{0,2},{1,3},{2,0},{3,1},{4,6},{5,7},{6,4},{7,5},{8,10},{9,11},{10,... | collective-permute-start | bytes 55304 | tf_op jit(solution)/shard_map/ppermute | solution.py:354
  27.5 0.0 collective-permute-done.6.refs_3_
  27.5 1.6 %collective-permute-start.7 = (f32[9,2,256]{2,1,0:T(2,128)S(1)}, f32[9,2,256]{2,1,0:T(2,128)S(1)}, u32[]{:S(2)}, u32[]{:S(2)}) collective-permute-start(f32[9,2,256]{2,1,0:T(2,128)S(1)} %corr_second.1.refs_0_), channel_id=1, source_target_pairs={{0,1},{1,0},{2,3},{3,2},{4,5},{5,4},{6,7},{7,6},{8,9},{9,8},{10,11... | collective-permute-start | bytes 55304 | tf_op jit(solution)/shard_map/ppermute | solution.py:354
  29.1 0.8 %collective-permute-done.5.refs_2_ = f32[9,14,256]{2,1,0:T(8,128)S(1)} collective-permute-done((f32[9,14,256]{2,1,0:T(8,128)S(1)}, f32[9,14,256]{2,1,0:T(8,128)S(1)}, u32[]{:S(2)}, u32[]{:S(2)}) %collective-permute-start.5) | collective-permute-done | bytes 129056 | tf_op jit(solution)/shard_map/ppermute | solution.py:354
  29.9 0.2 collective-permute-done.4.refs_1_
  30.1 2.1 %bands.1 = (bf16[8,384,896]{2,1,0:T(8,128)(2,1)S(1)}, f32[9,14,256]{2,1,0:T(8,128)S(1)}) custom-call(s32[16]{0:T(128)S(1)} %get-tuple-element.28.first_in.first_ref, s32[16]{0:T(128)S(1)} %get-tuple-element.29.second_in.second_ref, s32[16,256]{1,0:T(8,128)S(1)} %get-tuple-element.30.inside_ref, ...), custom_call_target="tpu_custom_call", output_to_operand_aliasing={{0}: (4, {})} | custom-call | flops 2000000000 | bytes 4194304 | tf_op jit(solution)/shard_map/bands/pallas_call | solution.py:480
  32.2 0.0 collective-permute-done.9.refs_3_
  32.2 0.0 collective-permute-done.8.refs_2_
  32.2 0.0 collective-permute-done.7.refs_1_
  32.2 2.8 %adjoint.1 = (bf16[8,384,896]{2,1,0:T(8,128)(2,1)S(1)}, bf16[4,3,64,128]{3,2,1,0:T(8,128)(2,1)S(1)}, f32[9,4,256]{2,1,0:T(4,128)}) custom-call(s32[16]{0:T(128)S(1)} %get-tuple-element.28.first_in.first_ref, s32[16]{0:T(128)S(1)} %get-tuple-element.29.second_in.second_ref, ...), custom_call_target="tpu_custom_call", output_to_operand_aliasing={{0}: (4, {})} | custom-call | flops 2000000000 | bytes 4194304 | tf_op jit(solution)/shard_map/adjoint/pallas_call | solution.py:495
  35.1 0.1 collective-permute-start.10
  35.1 1.8 %keep.1 = (bf16[3,64,128]{2,1,0:T(8,128)(2,1)S(1)}, bf16[3,64,128]{2,1,0:T(8,128)(2,1)S(1)}, bf16[3,64,128]{2,1,0:T(8,128)(2,1)S(1)}, bf16[3,64,128]{2,1,0:T(8,128)(2,1)S(1)}) custom-call(bf16[8,384,896]{2,1,0:T(8,128)(2,1)S(1)} %get-tuple-element.43.bands, bf16[24,320,128]{2,1,0:T(8,128)(2,1)S(1)} %get-tuple-element.40.fan_ref), custom_call_target="tpu_custom_call" | custom-call | flops 2000000000 | bytes 4194304 | tf_op jit(solution)/shard_map/keep/pallas_call | solution.py:514
  37.0 0.0 collective-permute-done.10
  37.0 2.7 %collective-permute-start.11 = (bf16[2,3,64,128]{3,2,1,0:T(8,128)(2,1)S(1)}, bf16[2,3,64,128]{3,2,1,0:T(8,128)(2,1)S(1)}, u32[]{:S(2)}, u32[]{:S(2)}) collective-permute-start(bf16[2,3,64,128]{3,2,1,0:T(8,128)(2,1)S(1)} %pad_maximum_fusion.3), channel_id=1, source_target_pairs={{0,8},{4,12},{8,16},{12,20},{16,24},{20,28},{24,0},{28,4},{1,9},{5... | collective-permute-start | bytes 294920 | tf_op jit(solution)/shard_map/ppermute | solution.py:364
  39.8 0.9 %collective-permute-start.12 = (bf16[2,3,64,128]{3,2,1,0:T(8,128)(2,1)S(1)}, bf16[2,3,64,128]{3,2,1,0:T(8,128)(2,1)S(1)}, u32[]{:S(2)}, u32[]{:S(2)}) collective-permute-start(bf16[2,3,64,128]{3,2,1,0:T(8,128)(2,1)S(1)} %pad_maximum_fusion.4), channel_id=1, source_target_pairs={{0,16},{4,20},{8,24},{12,28},{16,0},{20,4},{24,8},{28,12},{1,17},{... | collective-permute-start | bytes 294920 | tf_op jit(solution)/shard_map/ppermute | solution.py:364
  40.7 1.6 %collective-permute-start.13 = (bf16[2,3,64,128]{3,2,1,0:T(8,128)(2,1)S(1)}, bf16[2,3,64,128]{3,2,1,0:T(8,128)(2,1)S(1)}, u32[]{:S(2)}, u32[]{:S(2)}) collective-permute-start(bf16[2,3,64,128]{3,2,1,0:T(8,128)(2,1)S(1)} %pad_maximum_fusion.5), channel_id=1, source_target_pairs={{0,24},{4,28},{8,0},{12,4},{16,8},{20,12},{24,16},{28,20},{1,25},{... | collective-permute-start | bytes 294920 | tf_op jit(solution)/shard_map/ppermute | solution.py:364
  42.3 2.3 %collective-permute-done.11.refs_0_ = bf16[2,3,64,128]{3,2,1,0:T(8,128)(2,1)S(1)} collective-permute-done((bf16[2,3,64,128]{3,2,1,0:T(8,128)(2,1)S(1)}, bf16[2,3,64,128]{3,2,1,0:T(8,128)(2,1)S(1)}, u32[]{:S(2)}, u32[]{:S(2)}) %collective-permute-start.11) | collective-permute-done | bytes 98336 | tf_op jit(solution)/shard_map/ppermute | solution.py:364
  44.6 3.8 %collective-permute-done.12.refs_1_ = bf16[2,3,64,128]{3,2,1,0:T(8,128)(2,1)S(1)} collective-permute-done((bf16[2,3,64,128]{3,2,1,0:T(8,128)(2,1)S(1)}, bf16[2,3,64,128]{3,2,1,0:T(8,128)(2,1)S(1)}, u32[]{:S(2)}, u32[]{:S(2)}) %collective-permute-start.12) | collective-permute-done | bytes 98336 | tf_op jit(solution)/shard_map/ppermute | solution.py:364
  48.4 0.0 collective-permute-done.13.refs_2_
  48.4 2.0 %unpack.1 = bf16[3,16,8192]{2,1,0:T(8,128)(2,1)} custom-call(s32[8]{0:T(128)S(1)} %get-tuple-element.27.rows_in, bf16[2,3,64,128]{3,2,1,0:T(8,128)(2,1)S(1)} %collective-permute-done.11.refs_0_, bf16[2,3,64,128]{3,2,1,0:T(8,128)(2,1)S(1)} %collective-permute-done.12.refs_1_, bf16[2,3,64,128]{3,2,1,0:T(8,128)(2,1)S(1)} %collective-permute-done.13.refs_2_, ...), custom_call_target="tpu_custom_call" | custom-call | tf_op jit(solution)/shard_map/unpack/pallas_call | solution.py:525
  (8 shorter events, 0.1 us)
Async XLA Ops:
  2.1 1.6 %collective-permute-start = (bf16[4,3,64,128]{3,2,1,0:T(8,128)(2,1)S(1)}, bf16[4,3,64,128]{3,2,1,0:T(8,128)(2,1)S(1)}, u32[]{:S(2)}, u32[]{:S(2)}) collective-permute-start(bf16[4,3,64,128]{3,2,1,0:T(8,128)(2,1)S(1)} %get-tuple-element.26.token), channel_id=1, source_target_pairs={{0,4},{4,0},{8,12},{12,8},{16,20},{20,16},{24,28},{28,24},{1,5},{5... | collective-permute-start | bytes 589832 | tf_op jit(solution)/shard_map/ppermute | solution.py:354
  3.8 8.7 %collective-permute-start.1 = (bf16[2,3,64,128]{3,2,1,0:T(8,128)(2,1)S(1)}, bf16[2,3,64,128]{3,2,1,0:T(8,128)(2,1)S(1)}, u32[]{:S(2)}, u32[]{:S(2)}) collective-permute-start(bf16[2,3,64,128]{3,2,1,0:T(8,128)(2,1)S(1)} %pad_maximum_fusion), channel_id=1, source_target_pairs={{0,8},{4,12},{8,16},{12,20},{16,24},{20,28},{24,0},{28,4},{1,9},{5... | collective-permute-start | bytes 294920 | tf_op jit(solution)/shard_map/ppermute | solution.py:364
  6.8 9.4 %collective-permute-start.2 = (bf16[2,3,64,128]{3,2,1,0:T(8,128)(2,1)S(1)}, bf16[2,3,64,128]{3,2,1,0:T(8,128)(2,1)S(1)}, u32[]{:S(2)}, u32[]{:S(2)}) collective-permute-start(bf16[2,3,64,128]{3,2,1,0:T(8,128)(2,1)S(1)} %pad_maximum_fusion.1), channel_id=1, source_target_pairs={{0,16},{4,20},{8,24},{12,28},{16,0},{20,4},{24,8},{28,12},{1,17},{... | collective-permute-start | bytes 294920 | tf_op jit(solution)/shard_map/ppermute | solution.py:364
  9.5 6.8 %collective-permute-start.3 = (bf16[2,3,64,128]{3,2,1,0:T(8,128)(2,1)S(1)}, bf16[2,3,64,128]{3,2,1,0:T(8,128)(2,1)S(1)}, u32[]{:S(2)}, u32[]{:S(2)}) collective-permute-start(bf16[2,3,64,128]{3,2,1,0:T(8,128)(2,1)S(1)} %pad_maximum_fusion.2), channel_id=1, source_target_pairs={{0,24},{4,28},{8,0},{12,4},{16,8},{20,12},{24,16},{28,20},{1,25},{... | collective-permute-start | bytes 294920 | tf_op jit(solution)/shard_map/ppermute | solution.py:364
  19.8 7.7 %collective-permute-start.6 = (f32[9,14,256]{2,1,0:T(8,128)S(1)}, f32[9,14,256]{2,1,0:T(8,128)S(1)}, u32[]{:S(2)}, u32[]{:S(2)}) collective-permute-start(f32[9,14,256]{2,1,0:T(8,128)S(1)} %get-tuple-element.38.refs_0_), channel_id=1, source_target_pairs={{0,3},{1,2},{2,1},{3,0},{4,7},{5,6},{6,5},{7,4},{8,11},{9,10},{10,... | collective-permute-start | bytes 387080 | tf_op jit(solution)/shard_map/ppermute | solution.py:354
  22.4 7.5 %collective-permute-start.5 = (f32[9,14,256]{2,1,0:T(8,128)S(1)}, f32[9,14,256]{2,1,0:T(8,128)S(1)}, u32[]{:S(2)}, u32[]{:S(2)}) collective-permute-start(f32[9,14,256]{2,1,0:T(8,128)S(1)} %get-tuple-element.38.refs_0_), channel_id=1, source_target_pairs={{0,2},{1,3},{2,0},{3,1},{4,6},{5,7},{6,4},{7,5},{8,10},{9,11},{10,... | collective-permute-start | bytes 387080 | tf_op jit(solution)/shard_map/ppermute | solution.py:354
  22.9 7.2 %collective-permute-start.4 = (f32[9,14,256]{2,1,0:T(8,128)S(1)}, f32[9,14,256]{2,1,0:T(8,128)S(1)}, u32[]{:S(2)}, u32[]{:S(2)}) collective-permute-start(f32[9,14,256]{2,1,0:T(8,128)S(1)} %get-tuple-element.38.refs_0_), channel_id=1, source_target_pairs={{0,1},{1,0},{2,3},{3,2},{4,5},{5,4},{6,7},{7,6},{8,9},{9,8},{10,11... | collective-permute-start | bytes 387080 | tf_op jit(solution)/shard_map/ppermute | solution.py:354
  24.4 7.8 %collective-permute-start.9 = (f32[9,2,256]{2,1,0:T(2,128)S(1)}, f32[9,2,256]{2,1,0:T(2,128)S(1)}, u32[]{:S(2)}, u32[]{:S(2)}) collective-permute-start(f32[9,2,256]{2,1,0:T(2,128)S(1)} %corr_second.1.refs_0_), channel_id=1, source_target_pairs={{0,3},{1,2},{2,1},{3,0},{4,7},{5,6},{6,5},{7,4},{8,11},{9,10},{10,... | collective-permute-start | bytes 55304 | tf_op jit(solution)/shard_map/ppermute | solution.py:354
  27.0 5.2 %collective-permute-start.8 = (f32[9,2,256]{2,1,0:T(2,128)S(1)}, f32[9,2,256]{2,1,0:T(2,128)S(1)}, u32[]{:S(2)}, u32[]{:S(2)}) collective-permute-start(f32[9,2,256]{2,1,0:T(2,128)S(1)} %corr_second.1.refs_0_), channel_id=1, source_target_pairs={{0,2},{1,3},{2,0},{3,1},{4,6},{5,7},{6,4},{7,5},{8,10},{9,11},{10,... | collective-permute-start | bytes 55304 | tf_op jit(solution)/shard_map/ppermute | solution.py:354
  27.5 4.7 %collective-permute-start.7 = (f32[9,2,256]{2,1,0:T(2,128)S(1)}, f32[9,2,256]{2,1,0:T(2,128)S(1)}, u32[]{:S(2)}, u32[]{:S(2)}) collective-permute-start(f32[9,2,256]{2,1,0:T(2,128)S(1)} %corr_second.1.refs_0_), channel_id=1, source_target_pairs={{0,1},{1,0},{2,3},{3,2},{4,5},{5,4},{6,7},{7,6},{8,9},{9,8},{10,11... | collective-permute-start | bytes 55304 | tf_op jit(solution)/shard_map/ppermute | solution.py:354
  35.1 1.9 %collective-permute-start.10 = (bf16[4,3,64,128]{3,2,1,0:T(8,128)(2,1)S(1)}, bf16[4,3,64,128]{3,2,1,0:T(8,128)(2,1)S(1)}, u32[]{:S(2)}, u32[]{:S(2)}) collective-permute-start(bf16[4,3,64,128]{3,2,1,0:T(8,128)(2,1)S(1)} %get-tuple-element.45), channel_id=1, source_target_pairs={{0,4},{4,0},{8,12},{12,8},{16,20},{20,16},{24,28},{28,24},{1,5},{5... | collective-permute-start | bytes 589832 | tf_op jit(solution)/shard_map/ppermute | solution.py:354
  37.0 7.5 %collective-permute-start.11 = (bf16[2,3,64,128]{3,2,1,0:T(8,128)(2,1)S(1)}, bf16[2,3,64,128]{3,2,1,0:T(8,128)(2,1)S(1)}, u32[]{:S(2)}, u32[]{:S(2)}) collective-permute-start(bf16[2,3,64,128]{3,2,1,0:T(8,128)(2,1)S(1)} %pad_maximum_fusion.3), channel_id=1, source_target_pairs={{0,8},{4,12},{8,16},{12,20},{16,24},{20,28},{24,0},{28,4},{1,9},{5... | collective-permute-start | bytes 294920 | tf_op jit(solution)/shard_map/ppermute | solution.py:364
  39.8 8.6 %collective-permute-start.12 = (bf16[2,3,64,128]{3,2,1,0:T(8,128)(2,1)S(1)}, bf16[2,3,64,128]{3,2,1,0:T(8,128)(2,1)S(1)}, u32[]{:S(2)}, u32[]{:S(2)}) collective-permute-start(bf16[2,3,64,128]{3,2,1,0:T(8,128)(2,1)S(1)} %pad_maximum_fusion.4), channel_id=1, source_target_pairs={{0,16},{4,20},{8,24},{12,28},{16,0},{20,4},{24,8},{28,12},{1,17},{... | collective-permute-start | bytes 294920 | tf_op jit(solution)/shard_map/ppermute | solution.py:364
  40.7 7.7 %collective-permute-start.13 = (bf16[2,3,64,128]{3,2,1,0:T(8,128)(2,1)S(1)}, bf16[2,3,64,128]{3,2,1,0:T(8,128)(2,1)S(1)}, u32[]{:S(2)}, u32[]{:S(2)}) collective-permute-start(bf16[2,3,64,128]{3,2,1,0:T(8,128)(2,1)S(1)} %pad_maximum_fusion.5), channel_id=1, source_target_pairs={{0,24},{4,28},{8,0},{12,4},{16,8},{20,12},{24,16},{28,20},{1,25},{... | collective-permute-start | bytes 294920 | tf_op jit(solution)/shard_map/ppermute | solution.py:364

commit v6 on v5

--- a/solution.py
+++ b/solution.py
@@ -85,7 +85,7 @@
         copy.wait()
 
 
-def build_phases(slot_refs, fan_ref):
+def build_phases(slot_refs, fan_ref, first_slot):
     chunks = slot_refs[0].shape[1]
     rows = fan_ref.shape[1]
     lane = lax.broadcasted_iota(jnp.int32, (LANES, LANES), 1)
@@ -99,8 +99,8 @@
         swapped = pltpu.roll(wide, chunks, 1)
         one = jnp.where(left, wide[:rows], swapped[HALF_TILE:])
         two = jnp.where(left, swapped[:rows], wide[HALF_TILE:])
-        fan_ref[place] = one.astype(jnp.bfloat16)
-        fan_ref[place + 1] = two.astype(jnp.bfloat16)
+        fan_ref[CHANS * first_slot + place] = one.astype(jnp.bfloat16)
+        fan_ref[CHANS * first_slot + place + 1] = two.astype(jnp.bfloat16)
 
 
 def shifted_rows(fan_ref, slot, phases):
@@ -115,8 +115,8 @@
 
 
 def prep_kernel(
-    token, first_in, second_in, rows_in, low_in, high_in, observed_in,
-    bands, first_out, second_out, rows_out, inside, seen, seen_later,
+    own_ref, got_ref, first_in, second_in, rows_in, low_in, high_in, observed_in,
+    bands, fan_ref, first_out, second_out, rows_out, inside, seen, seen_later,
     staged, low_ref, high_ref, sems,
 ):
     copies = fetch(
@@ -125,6 +125,7 @@
         sems,
     )
     bands[...] = jnp.zeros_like(bands)
+    build_phases([own_ref, got_ref], fan_ref, 0)
     for copy in copies:
         copy.wait()
     pairs = inside.shape[0]
@@ -166,15 +167,14 @@
     lax.fori_loop(0, count, step, 0, unroll=min(count, 16))
 
 
-def corr_first_kernel(order, first_in, second_in, *refs):
+def corr_first_kernel(order, first_in, second_in, fan_in, *refs):
     given = refs[:-6]
     corr_ref, fan_ref, heads, first_ref, second_ref, sems = refs[-6:]
     copies = fetch((first_in, second_in), (first_ref, second_ref), sems)
-    slot_refs = [None] * (2 * len(given) - 2)
-    for j, ref in zip(order, given[:-2]):
-        slot_refs[2 * j:2 * j + 2] = [ref.at[0], ref.at[1]]
-    slot_refs[:2] = given[-2:]
-    build_phases(slot_refs, fan_ref)
+    slot_refs = [None] * (2 * len(given))
+    for j, ref in zip(order, given):
+        slot_refs[2 * j - 2:2 * j] = [ref.at[0], ref.at[1]]
+    build_phases(slot_refs, fan_ref, 2)
     height = CHANS * WIDE
     row = lax.broadcasted_iota(jnp.int32, (height, height), 0)
     column = lax.broadcasted_iota(jnp.int32, (height, height), 1)
@@ -423,12 +423,14 @@
     cost = pl.CostEstimate(flops=2 * 10**9, bytes_accessed=2**22, transcendentals=0)
     seen = jnp.transpose(observed, (1, 2, 0, 3)).reshape(combos, pairs, LAGS)
     seen = pltpu.with_memory_space_constraint(seen, pltpu.HBM)
-    bands, firsts, seconds, rows_copy, inside, seen, seen_later = pl.pallas_call(
+    order, arrived = across(swap, keep, 1, lambda n: list(range(1,n)))
+    bands, fan, firsts, seconds, rows_copy, inside, seen, seen_later = pl.pallas_call(
         prep_kernel,
-        in_specs=[pl.BlockSpec(memory_space=pl.ANY)] + [any_space] * 6,
-        out_specs=[vmem()] * 7,
+        in_specs=[vmem()] * 2 + [any_space] * 6,
+        out_specs=[vmem()] * 8,
         out_shape=[
             bands_shape,
+            fan_shape,
             index_shape,
             index_shape,
             jax.ShapeDtypeStruct((slots,), jnp.int32),
@@ -445,12 +447,11 @@
         compiler_params=small,
         cost_estimate=cost,
         name="prep",
-    )(swap, pair_first, pair_second, send_rows, lag_lo, lag_hi, seen)
-    order, arrived = across(swap, keep, 1, lambda n: list(range(1,n)))
+    )(*arrived[-2:], pair_first, pair_second, send_rows, lag_lo, lag_hi, seen)
 
     corr, fan, heads = pl.pallas_call(
         functools.partial(corr_first_kernel, order),
-        in_specs=[vmem()] * (chips + 3),
+        in_specs=[vmem()] * (chips + 2),
         out_specs=[vmem()] * 3,
         out_shape=[
             corr_shape,
@@ -460,10 +461,11 @@
             ),
         ],
         scratch_shapes=[index_scratch, index_scratch, pltpu.SemaphoreType.DMA((2,))],
+        input_output_aliases={2: 1},
         compiler_params=small,
         cost_estimate=cost,
         name="corr_first",
-    )(firsts, seconds, *arrived)
+    )(firsts, seconds, fan, *arrived[:-2])
     parts = window_parts(corr)
     later = pl.pallas_call(
         functools.partial(corr_second_kernel, early),

time: 50.5 us -> 50.2 us (level)
  transfers between devices with their start and end apart: 14 -> 14, of which waited for: 7 -> 7; matrix products, arithmetic and copies ran while one was open for 0% -> 0% of each run, Pallas kernels for 12% -> 13%
where the time goes in v6:
time: 50.2 us; the launch traced here: 50 us
  starting transfers between devices  21.1 us (42%)
  Pallas kernels  16 us (32%)
  waiting for transfers between devices  12.1 us (24%)
  between operations  0.77 us (2%)
    ppermute x6, starting transfers between devices, across(): blocks.append(lax.ppermute(jnp.stack([keep[j], got[j]]), 'stn', pairs))  12.3 us
    ppermute x6, waiting for transfers between devices, across(): blocks.append(lax.ppermute(jnp.stack([keep[j], got[j]]), 'stn', pairs))  9.98 us
    ppermute x8, starting transfers between devices, flipped(): return lax.ppermute(x, axis, [(k, k ^ bits) for k in range(count)])  8.8 us
    pallas_call x1, Pallas kernels, shards(): pl.pallas_call(functools.partial(corr_first_kernel, order), in_specs=[vme...  3.26 us
    pallas_call x1, Pallas kernels, shards(): pl.pallas_call(functools.partial(adjoint_kernel, corr_scale, adj_scale),...  2.82 us
    pallas_call x1, Pallas kernels, shards(): pl.pallas_call(functools.partial(bands_kernel, corr_scale), in_specs=[vme...  2.09 us
    ppermute x8, waiting for transfers between devices, flipped(): return lax.ppermute(x, axis, [(k, k ^ bits) for k in range(count)])  2.09 us
    pallas_call x1, Pallas kernels, shards(): pl.pallas_call(functools.partial(unpack_kernel, order), in_specs=[vmem()]...  1.96 us
  transfers between devices with their start and end apart: 14, of which 7 were waited for; matrix products, arithmetic and copies ran while one was open for 0% of the time, Pallas kernels for 13%

profile of v6, /device:TPU:0, one launch (start us, length us, event | category | flops | bytes accessed | tf_op | source)
XLA Modules:
  0.0 50.0 jit_solution(3988231568322532506)
XLA Ops:
  0.6 1.5 %pack.1 = (bf16[4,3,64,128]{3,2,1,0:T(8,128)(2,1)S(1)}, bf16[3,64,128]{2,1,0:T(8,128)(2,1)S(1)}, bf16[3,64,128]{2,1,0:T(8,128)(2,1)S(1)}, bf16[3,64,128]{2,1,0:T(8,128)(2,1)S(1)}, bf16[3,64,128]{2,1,0:T(8,128)(2,1)S(1)}) custom-call(s32[8]{0:T(128)} %bitcast.31, bf16[3,16,8192]{2,1,0:T(8,128)(2,1)} %bitcast.29), custom_call_target="tpu_custom_call" | custom-call | tf_op jit(solution)/shard_map/pack/pallas_call | solution.py:399
  2.1 0.5 %collective-permute-start = (bf16[4,3,64,128]{3,2,1,0:T(8,128)(2,1)S(1)}, bf16[4,3,64,128]{3,2,1,0:T(8,128)(2,1)S(1)}, u32[]{:S(2)}, u32[]{:S(2)}) collective-permute-start(bf16[4,3,64,128]{3,2,1,0:T(8,128)(2,1)S(1)} %get-tuple-element.28), channel_id=1, source_target_pairs={{0,4},{4,0},{8,12},{12,8},{16,20},{20,16},{24,28},{28,24},{1,5},{5... | collective-permute-start | bytes 589832 | tf_op jit(solution)/shard_map/ppermute | solution.py:354
  2.7 1.1 %collective-permute-done = bf16[4,3,64,128]{3,2,1,0:T(8,128)(2,1)S(1)} collective-permute-done((bf16[4,3,64,128]{3,2,1,0:T(8,128)(2,1)S(1)}, bf16[4,3,64,128]{3,2,1,0:T(8,128)(2,1)S(1)}, u32[]{:S(2)}, u32[]{:S(2)}) %collective-permute-start) | collective-permute-done | bytes 196640 | tf_op jit(solution)/shard_map/ppermute | solution.py:354
  3.8 3.0 %collective-permute-start.1 = (bf16[2,3,64,128]{3,2,1,0:T(8,128)(2,1)S(1)}, bf16[2,3,64,128]{3,2,1,0:T(8,128)(2,1)S(1)}, u32[]{:S(2)}, u32[]{:S(2)}) collective-permute-start(bf16[2,3,64,128]{3,2,1,0:T(8,128)(2,1)S(1)} %pad_maximum_fusion), channel_id=1, source_target_pairs={{0,8},{4,12},{8,16},{12,20},{16,24},{20,28},{24,0},{28,4},{1,9},{5... | collective-permute-start | bytes 294920 | tf_op jit(solution)/shard_map/ppermute | solution.py:364
  6.8 2.7 %collective-permute-start.2 = (bf16[2,3,64,128]{3,2,1,0:T(8,128)(2,1)S(1)}, bf16[2,3,64,128]{3,2,1,0:T(8,128)(2,1)S(1)}, u32[]{:S(2)}, u32[]{:S(2)}) collective-permute-start(bf16[2,3,64,128]{3,2,1,0:T(8,128)(2,1)S(1)} %pad_maximum_fusion.1), channel_id=1, source_target_pairs={{0,16},{4,20},{8,24},{12,28},{16,0},{20,4},{24,8},{28,12},{1,17},{... | collective-permute-start | bytes 294920 | tf_op jit(solution)/shard_map/ppermute | solution.py:364
  9.5 1.4 %collective-permute-start.3 = (bf16[2,3,64,128]{3,2,1,0:T(8,128)(2,1)S(1)}, bf16[2,3,64,128]{3,2,1,0:T(8,128)(2,1)S(1)}, u32[]{:S(2)}, u32[]{:S(2)}) collective-permute-start(bf16[2,3,64,128]{3,2,1,0:T(8,128)(2,1)S(1)} %pad_maximum_fusion.2), channel_id=1, source_target_pairs={{0,24},{4,28},{8,0},{12,4},{16,8},{20,12},{24,16},{28,20},{1,25},{... | collective-permute-start | bytes 294920 | tf_op jit(solution)/shard_map/ppermute | solution.py:364
  10.9 1.4 %prep.1 = (bf16[8,384,896]{2,1,0:T(8,128)(2,1)S(1)}, bf16[24,320,128]{2,1,0:T(8,128)(2,1)S(1)}, s32[16]{0:T(128)S(1)}, s32[16]{0:T(128)S(1)}, s32[8]{0:T(128)S(1...) custom-call(bf16[3,64,128]{2,1,0:T(8,128)(2,1)S(1)} %get-tuple-element.27.own_ref, ...), custom_call_target="tpu_custom_call" | custom-call | flops 2000000000 | bytes 4194304 | tf_op jit(solution)/shard_map/prep/pallas_call | solution.py:427
  12.3 0.2 collective-permute-done.1.refs_0_
  12.5 3.8 %collective-permute-done.2.refs_1_ = bf16[2,3,64,128]{3,2,1,0:T(8,128)(2,1)S(1)} collective-permute-done((bf16[2,3,64,128]{3,2,1,0:T(8,128)(2,1)S(1)}, bf16[2,3,64,128]{3,2,1,0:T(8,128)(2,1)S(1)}, u32[]{:S(2)}, u32[]{:S(2)}) %collective-permute-start.2) | collective-permute-done | bytes 98336 | tf_op jit(solution)/shard_map/ppermute | solution.py:364
  16.2 0.0 collective-permute-done.3.refs_2_
  16.2 3.3 %corr_first.1 = (f32[9,14,256]{2,1,0:T(8,128)S(1)}, bf16[24,320,128]{2,1,0:T(8,128)(2,1)S(1)}, bf16[8,96,256]{2,1,0:T(8,128)(2,1)S(1)}) custom-call(s32[16]{0:T(128)S(1)} %get-tuple-element.30.first_in.first_ref, s32[16]{0:T(128)S(1)} %get-tuple-element.31.second_in.second_ref, ...), custom_call_target="tpu_custom_call", output_to_operand_aliasing={{1}: (2, {})} | custom-call | flops 2000000000 | bytes 4194304 | tf_op jit(solution)/shard_map/corr_first/pallas_call | solution.py:452
  19.5 2.6 %collective-permute-start.6 = (f32[9,14,256]{2,1,0:T(8,128)S(1)}, f32[9,14,256]{2,1,0:T(8,128)S(1)}, u32[]{:S(2)}, u32[]{:S(2)}) collective-permute-start(f32[9,14,256]{2,1,0:T(8,128)S(1)} %get-tuple-element.40.refs_0_), channel_id=1, source_target_pairs={{0,3},{1,2},{2,1},{3,0},{4,7},{5,6},{6,5},{7,4},{8,11},{9,10},{10,... | collective-permute-start | bytes 387080 | tf_op jit(solution)/shard_map/ppermute | solution.py:354
  22.1 0.5 %collective-permute-start.5 = (f32[9,14,256]{2,1,0:T(8,128)S(1)}, f32[9,14,256]{2,1,0:T(8,128)S(1)}, u32[]{:S(2)}, u32[]{:S(2)}) collective-permute-start(f32[9,14,256]{2,1,0:T(8,128)S(1)} %get-tuple-element.40.refs_0_), channel_id=1, source_target_pairs={{0,2},{1,3},{2,0},{3,1},{4,6},{5,7},{6,4},{7,5},{8,10},{9,11},{10,... | collective-permute-start | bytes 387080 | tf_op jit(solution)/shard_map/ppermute | solution.py:354
  22.6 0.5 collective-permute-start.4
  23.1 1.1 %corr_second.1.refs_0_ = f32[9,2,256]{2,1,0:T(2,128)S(1)} custom-call(s32[16]{0:T(128)S(1)} %get-tuple-element.30.first_in.first_ref, s32[16]{0:T(128)S(1)} %get-tuple-element.31.second_in.second_ref, bf16[24,320,128]{2,1,0:T(8,128)(2,1)S(1)} %get-tuple-element.42.fan_ref, bf16[8,96,256]{2,1,0:T(8,128)(2,1)S(1)} %get-tuple-element.44.heads), custom_call_target="tpu_custom_call" | custom-call | flops 2000000000 | bytes 4194304 | tf_op jit(solution)/shard_map/corr_second/pallas_call | solution.py:470
  24.1 2.6 %collective-permute-start.9 = (f32[9,2,256]{2,1,0:T(2,128)S(1)}, f32[9,2,256]{2,1,0:T(2,128)S(1)}, u32[]{:S(2)}, u32[]{:S(2)}) collective-permute-start(f32[9,2,256]{2,1,0:T(2,128)S(1)} %corr_second.1.refs_0_), channel_id=1, source_target_pairs={{0,3},{1,2},{2,1},{3,0},{4,7},{5,6},{6,5},{7,4},{8,11},{9,10},{10,... | collective-permute-start | bytes 55304 | tf_op jit(solution)/shard_map/ppermute | solution.py:354
  26.7 0.5 %collective-permute-start.8 = (f32[9,2,256]{2,1,0:T(2,128)S(1)}, f32[9,2,256]{2,1,0:T(2,128)S(1)}, u32[]{:S(2)}, u32[]{:S(2)}) collective-permute-start(f32[9,2,256]{2,1,0:T(2,128)S(1)} %corr_second.1.refs_0_), channel_id=1, source_target_pairs={{0,2},{1,3},{2,0},{3,1},{4,6},{5,7},{6,4},{7,5},{8,10},{9,11},{10,... | collective-permute-start | bytes 55304 | tf_op jit(solution)/shard_map/ppermute | solution.py:354
  27.2 0.0 collective-permute-done.6.refs_3_
  27.2 1.6 %collective-permute-start.7 = (f32[9,2,256]{2,1,0:T(2,128)S(1)}, f32[9,2,256]{2,1,0:T(2,128)S(1)}, u32[]{:S(2)}, u32[]{:S(2)}) collective-permute-start(f32[9,2,256]{2,1,0:T(2,128)S(1)} %corr_second.1.refs_0_), channel_id=1, source_target_pairs={{0,1},{1,0},{2,3},{3,2},{4,5},{5,4},{6,7},{7,6},{8,9},{9,8},{10,11... | collective-permute-start | bytes 55304 | tf_op jit(solution)/shard_map/ppermute | solution.py:354
  28.8 0.8 %collective-permute-done.5.refs_2_ = f32[9,14,256]{2,1,0:T(8,128)S(1)} collective-permute-done((f32[9,14,256]{2,1,0:T(8,128)S(1)}, f32[9,14,256]{2,1,0:T(8,128)S(1)}, u32[]{:S(2)}, u32[]{:S(2)}) %collective-permute-start.5) | collective-permute-done | bytes 129056 | tf_op jit(solution)/shard_map/ppermute | solution.py:354
  29.6 0.2 collective-permute-done.4.refs_1_
  29.8 2.1 %bands.1 = (bf16[8,384,896]{2,1,0:T(8,128)(2,1)S(1)}, f32[9,14,256]{2,1,0:T(8,128)S(1)}) custom-call(s32[16]{0:T(128)S(1)} %get-tuple-element.30.first_in.first_ref, s32[16]{0:T(128)S(1)} %get-tuple-element.31.second_in.second_ref, s32[16,256]{1,0:T(8,128)S(1)} %get-tuple-element.32.inside_ref, ...), custom_call_target="tpu_custom_call", output_to_operand_aliasing={{0}: (4, {})} | custom-call | flops 2000000000 | bytes 4194304 | tf_op jit(solution)/shard_map/bands/pallas_call | solution.py:482
  31.9 0.0 collective-permute-done.9.refs_3_
  31.9 0.0 collective-permute-done.8.refs_2_
  31.9 0.0 collective-permute-done.7.refs_1_
  31.9 2.8 %adjoint.1 = (bf16[8,384,896]{2,1,0:T(8,128)(2,1)S(1)}, bf16[4,3,64,128]{3,2,1,0:T(8,128)(2,1)S(1)}, f32[9,4,256]{2,1,0:T(4,128)}) custom-call(s32[16]{0:T(128)S(1)} %get-tuple-element.30.first_in.first_ref, s32[16]{0:T(128)S(1)} %get-tuple-element.31.second_in.second_ref, ...), custom_call_target="tpu_custom_call", output_to_operand_aliasing={{0}: (4, {})} | custom-call | flops 2000000000 | bytes 4194304 | tf_op jit(solution)/shard_map/adjoint/pallas_call | solution.py:497
  34.8 0.1 collective-permute-start.10
  34.8 1.8 %keep.1 = (bf16[3,64,128]{2,1,0:T(8,128)(2,1)S(1)}, bf16[3,64,128]{2,1,0:T(8,128)(2,1)S(1)}, bf16[3,64,128]{2,1,0:T(8,128)(2,1)S(1)}, bf16[3,64,128]{2,1,0:T(8,128)(2,1)S(1)}) custom-call(bf16[8,384,896]{2,1,0:T(8,128)(2,1)S(1)} %get-tuple-element.45.bands, bf16[24,320,128]{2,1,0:T(8,128)(2,1)S(1)} %get-tuple-element.42.fan_ref), custom_call_target="tpu_custom_call" | custom-call | flops 2000000000 | bytes 4194304 | tf_op jit(solution)/shard_map/keep/pallas_call | solution.py:516
  36.7 0.0 collective-permute-done.10
  36.7 2.7 %collective-permute-start.11 = (bf16[2,3,64,128]{3,2,1,0:T(8,128)(2,1)S(1)}, bf16[2,3,64,128]{3,2,1,0:T(8,128)(2,1)S(1)}, u32[]{:S(2)}, u32[]{:S(2)}) collective-permute-start(bf16[2,3,64,128]{3,2,1,0:T(8,128)(2,1)S(1)} %pad_maximum_fusion.3), channel_id=1, source_target_pairs={{0,8},{4,12},{8,16},{12,20},{16,24},{20,28},{24,0},{28,4},{1,9},{5... | collective-permute-start | bytes 294920 | tf_op jit(solution)/shard_map/ppermute | solution.py:364
  39.5 0.9 %collective-permute-start.12 = (bf16[2,3,64,128]{3,2,1,0:T(8,128)(2,1)S(1)}, bf16[2,3,64,128]{3,2,1,0:T(8,128)(2,1)S(1)}, u32[]{:S(2)}, u32[]{:S(2)}) collective-permute-start(bf16[2,3,64,128]{3,2,1,0:T(8,128)(2,1)S(1)} %pad_maximum_fusion.4), channel_id=1, source_target_pairs={{0,16},{4,20},{8,24},{12,28},{16,0},{20,4},{24,8},{28,12},{1,17},{... | collective-permute-start | bytes 294920 | tf_op jit(solution)/shard_map/ppermute | solution.py:364
  40.4 1.6 %collective-permute-start.13 = (bf16[2,3,64,128]{3,2,1,0:T(8,128)(2,1)S(1)}, bf16[2,3,64,128]{3,2,1,0:T(8,128)(2,1)S(1)}, u32[]{:S(2)}, u32[]{:S(2)}) collective-permute-start(bf16[2,3,64,128]{3,2,1,0:T(8,128)(2,1)S(1)} %pad_maximum_fusion.5), channel_id=1, source_target_pairs={{0,24},{4,28},{8,0},{12,4},{16,8},{20,12},{24,16},{28,20},{1,25},{... | collective-permute-start | bytes 294920 | tf_op jit(solution)/shard_map/ppermute | solution.py:364
  42.0 2.3 %collective-permute-done.11.refs_0_ = bf16[2,3,64,128]{3,2,1,0:T(8,128)(2,1)S(1)} collective-permute-done((bf16[2,3,64,128]{3,2,1,0:T(8,128)(2,1)S(1)}, bf16[2,3,64,128]{3,2,1,0:T(8,128)(2,1)S(1)}, u32[]{:S(2)}, u32[]{:S(2)}) %collective-permute-start.11) | collective-permute-done | bytes 98336 | tf_op jit(solution)/shard_map/ppermute | solution.py:364
  44.3 3.8 %collective-permute-done.12.refs_1_ = bf16[2,3,64,128]{3,2,1,0:T(8,128)(2,1)S(1)} collective-permute-done((bf16[2,3,64,128]{3,2,1,0:T(8,128)(2,1)S(1)}, bf16[2,3,64,128]{3,2,1,0:T(8,128)(2,1)S(1)}, u32[]{:S(2)}, u32[]{:S(2)}) %collective-permute-start.12) | collective-permute-done | bytes 98336 | tf_op jit(solution)/shard_map/ppermute | solution.py:364
  48.1 0.0 collective-permute-done.13.refs_2_
  48.1 2.0 %unpack.1 = bf16[3,16,8192]{2,1,0:T(8,128)(2,1)} custom-call(s32[8]{0:T(128)S(1)} %get-tuple-element.29.rows_in, bf16[2,3,64,128]{3,2,1,0:T(8,128)(2,1)S(1)} %collective-permute-done.11.refs_0_, bf16[2,3,64,128]{3,2,1,0:T(8,128)(2,1)S(1)} %collective-permute-done.12.refs_1_, bf16[2,3,64,128]{3,2,1,0:T(8,128)(2,1)S(1)} %collective-permute-done.13.refs_2_, ...), custom_call_target="tpu_custom_call" | custom-call | tf_op jit(solution)/shard_map/unpack/pallas_call | solution.py:527
  (8 shorter events, 0.1 us)
Async XLA Ops:
  2.1 1.6 %collective-permute-start = (bf16[4,3,64,128]{3,2,1,0:T(8,128)(2,1)S(1)}, bf16[4,3,64,128]{3,2,1,0:T(8,128)(2,1)S(1)}, u32[]{:S(2)}, u32[]{:S(2)}) collective-permute-start(bf16[4,3,64,128]{3,2,1,0:T(8,128)(2,1)S(1)} %get-tuple-element.28), channel_id=1, source_target_pairs={{0,4},{4,0},{8,12},{12,8},{16,20},{20,16},{24,28},{28,24},{1,5},{5... | collective-permute-start | bytes 589832 | tf_op jit(solution)/shard_map/ppermute | solution.py:354
  3.8 8.7 %collective-permute-start.1 = (bf16[2,3,64,128]{3,2,1,0:T(8,128)(2,1)S(1)}, bf16[2,3,64,128]{3,2,1,0:T(8,128)(2,1)S(1)}, u32[]{:S(2)}, u32[]{:S(2)}) collective-permute-start(bf16[2,3,64,128]{3,2,1,0:T(8,128)(2,1)S(1)} %pad_maximum_fusion), channel_id=1, source_target_pairs={{0,8},{4,12},{8,16},{12,20},{16,24},{20,28},{24,0},{28,4},{1,9},{5... | collective-permute-start | bytes 294920 | tf_op jit(solution)/shard_map/ppermute | solution.py:364
  6.8 9.4 %collective-permute-start.2 = (bf16[2,3,64,128]{3,2,1,0:T(8,128)(2,1)S(1)}, bf16[2,3,64,128]{3,2,1,0:T(8,128)(2,1)S(1)}, u32[]{:S(2)}, u32[]{:S(2)}) collective-permute-start(bf16[2,3,64,128]{3,2,1,0:T(8,128)(2,1)S(1)} %pad_maximum_fusion.1), channel_id=1, source_target_pairs={{0,16},{4,20},{8,24},{12,28},{16,0},{20,4},{24,8},{28,12},{1,17},{... | collective-permute-start | bytes 294920 | tf_op jit(solution)/shard_map/ppermute | solution.py:364
  9.5 6.8 %collective-permute-start.3 = (bf16[2,3,64,128]{3,2,1,0:T(8,128)(2,1)S(1)}, bf16[2,3,64,128]{3,2,1,0:T(8,128)(2,1)S(1)}, u32[]{:S(2)}, u32[]{:S(2)}) collective-permute-start(bf16[2,3,64,128]{3,2,1,0:T(8,128)(2,1)S(1)} %pad_maximum_fusion.2), channel_id=1, source_target_pairs={{0,24},{4,28},{8,0},{12,4},{16,8},{20,12},{24,16},{28,20},{1,25},{... | collective-permute-start | bytes 294920 | tf_op jit(solution)/shard_map/ppermute | solution.py:364
  19.5 7.7 %collective-permute-start.6 = (f32[9,14,256]{2,1,0:T(8,128)S(1)}, f32[9,14,256]{2,1,0:T(8,128)S(1)}, u32[]{:S(2)}, u32[]{:S(2)}) collective-permute-start(f32[9,14,256]{2,1,0:T(8,128)S(1)} %get-tuple-element.40.refs_0_), channel_id=1, source_target_pairs={{0,3},{1,2},{2,1},{3,0},{4,7},{5,6},{6,5},{7,4},{8,11},{9,10},{10,... | collective-permute-start | bytes 387080 | tf_op jit(solution)/shard_map/ppermute | solution.py:354
  22.1 7.5 %collective-permute-start.5 = (f32[9,14,256]{2,1,0:T(8,128)S(1)}, f32[9,14,256]{2,1,0:T(8,128)S(1)}, u32[]{:S(2)}, u32[]{:S(2)}) collective-permute-start(f32[9,14,256]{2,1,0:T(8,128)S(1)} %get-tuple-element.40.refs_0_), channel_id=1, source_target_pairs={{0,2},{1,3},{2,0},{3,1},{4,6},{5,7},{6,4},{7,5},{8,10},{9,11},{10,... | collective-permute-start | bytes 387080 | tf_op jit(solution)/shard_map/ppermute | solution.py:354
  22.6 7.2 %collective-permute-start.4 = (f32[9,14,256]{2,1,0:T(8,128)S(1)}, f32[9,14,256]{2,1,0:T(8,128)S(1)}, u32[]{:S(2)}, u32[]{:S(2)}) collective-permute-start(f32[9,14,256]{2,1,0:T(8,128)S(1)} %get-tuple-element.40.refs_0_), channel_id=1, source_target_pairs={{0,1},{1,0},{2,3},{3,2},{4,5},{5,4},{6,7},{7,6},{8,9},{9,8},{10,11... | collective-permute-start | bytes 387080 | tf_op jit(solution)/shard_map/ppermute | solution.py:354
  24.1 7.8 %collective-permute-start.9 = (f32[9,2,256]{2,1,0:T(2,128)S(1)}, f32[9,2,256]{2,1,0:T(2,128)S(1)}, u32[]{:S(2)}, u32[]{:S(2)}) collective-permute-start(f32[9,2,256]{2,1,0:T(2,128)S(1)} %corr_second.1.refs_0_), channel_id=1, source_target_pairs={{0,3},{1,2},{2,1},{3,0},{4,7},{5,6},{6,5},{7,4},{8,11},{9,10},{10,... | collective-permute-start | bytes 55304 | tf_op jit(solution)/shard_map/ppermute | solution.py:354
  26.7 5.2 %collective-permute-start.8 = (f32[9,2,256]{2,1,0:T(2,128)S(1)}, f32[9,2,256]{2,1,0:T(2,128)S(1)}, u32[]{:S(2)}, u32[]{:S(2)}) collective-permute-start(f32[9,2,256]{2,1,0:T(2,128)S(1)} %corr_second.1.refs_0_), channel_id=1, source_target_pairs={{0,2},{1,3},{2,0},{3,1},{4,6},{5,7},{6,4},{7,5},{8,10},{9,11},{10,... | collective-permute-start | bytes 55304 | tf_op jit(solution)/shard_map/ppermute | solution.py:354
  27.2 4.7 %collective-permute-start.7 = (f32[9,2,256]{2,1,0:T(2,128)S(1)}, f32[9,2,256]{2,1,0:T(2,128)S(1)}, u32[]{:S(2)}, u32[]{:S(2)}) collective-permute-start(f32[9,2,256]{2,1,0:T(2,128)S(1)} %corr_second.1.refs_0_), channel_id=1, source_target_pairs={{0,1},{1,0},{2,3},{3,2},{4,5},{5,4},{6,7},{7,6},{8,9},{9,8},{10,11... | collective-permute-start | bytes 55304 | tf_op jit(solution)/shard_map/ppermute | solution.py:354
  34.8 1.9 %collective-permute-start.10 = (bf16[4,3,64,128]{3,2,1,0:T(8,128)(2,1)S(1)}, bf16[4,3,64,128]{3,2,1,0:T(8,128)(2,1)S(1)}, u32[]{:S(2)}, u32[]{:S(2)}) collective-permute-start(bf16[4,3,64,128]{3,2,1,0:T(8,128)(2,1)S(1)} %get-tuple-element.47), channel_id=1, source_target_pairs={{0,4},{4,0},{8,12},{12,8},{16,20},{20,16},{24,28},{28,24},{1,5},{5... | collective-permute-start | bytes 589832 | tf_op jit(solution)/shard_map/ppermute | solution.py:354
  36.7 7.5 %collective-permute-start.11 = (bf16[2,3,64,128]{3,2,1,0:T(8,128)(2,1)S(1)}, bf16[2,3,64,128]{3,2,1,0:T(8,128)(2,1)S(1)}, u32[]{:S(2)}, u32[]{:S(2)}) collective-permute-start(bf16[2,3,64,128]{3,2,1,0:T(8,128)(2,1)S(1)} %pad_maximum_fusion.3), channel_id=1, source_target_pairs={{0,8},{4,12},{8,16},{12,20},{16,24},{20,28},{24,0},{28,4},{1,9},{5... | collective-permute-start | bytes 294920 | tf_op jit(solution)/shard_map/ppermute | solution.py:364
  39.5 8.6 %collective-permute-start.12 = (bf16[2,3,64,128]{3,2,1,0:T(8,128)(2,1)S(1)}, bf16[2,3,64,128]{3,2,1,0:T(8,128)(2,1)S(1)}, u32[]{:S(2)}, u32[]{:S(2)}) collective-permute-start(bf16[2,3,64,128]{3,2,1,0:T(8,128)(2,1)S(1)} %pad_maximum_fusion.4), channel_id=1, source_target_pairs={{0,16},{4,20},{8,24},{12,28},{16,0},{20,4},{24,8},{28,12},{1,17},{... | collective-permute-start | bytes 294920 | tf_op jit(solution)/shard_map/ppermute | solution.py:364
  40.4 7.7 %collective-permute-start.13 = (bf16[2,3,64,128]{3,2,1,0:T(8,128)(2,1)S(1)}, bf16[2,3,64,128]{3,2,1,0:T(8,128)(2,1)S(1)}, u32[]{:S(2)}, u32[]{:S(2)}) collective-permute-start(bf16[2,3,64,128]{3,2,1,0:T(8,128)(2,1)S(1)} %pad_maximum_fusion.5), channel_id=1, source_target_pairs={{0,24},{4,28},{8,0},{12,4},{16,8},{20,12},{24,16},{28,20},{1,25},{... | collective-permute-start | bytes 294920 | tf_op jit(solution)/shard_map/ppermute | solution.py:364

commit v7 on v6

--- a/solution.py
+++ b/solution.py
@@ -14,7 +14,7 @@
 HALF_TILE = LANES // 2
 PHASES = 16
 WIDE = 32
-EARLY = 14
+EARLY = 13
 CHANS = 3
 WINDOW = 3 * LANES
 DEPTH = 7 * LANES

time: 50.2 us -> 50.5 us (level)
  no operation moved by 1% of the time
where the time goes in v7:
time: 50.5 us; the launch traced here: 50.3 us
  starting transfers between devices  21 us (42%)
  Pallas kernels  16 us (32%)
  waiting for transfers between devices  12.5 us (25%)
  between operations  0.77 us (2%)
    ppermute x6, starting transfers between devices, across(): blocks.append(lax.ppermute(jnp.stack([keep[j], got[j]]), 'stn', pairs))  12.3 us
    ppermute x6, waiting for transfers between devices, across(): blocks.append(lax.ppermute(jnp.stack([keep[j], got[j]]), 'stn', pairs))  9.98 us
    ppermute x8, starting transfers between devices, flipped(): return lax.ppermute(x, axis, [(k, k ^ bits) for k in range(count)])  8.67 us
    pallas_call x1, Pallas kernels, shards(): pl.pallas_call(functools.partial(corr_first_kernel, order), in_specs=[vme...  3.14 us
    pallas_call x1, Pallas kernels, shards(): pl.pallas_call(functools.partial(adjoint_kernel, corr_scale, adj_scale),...  2.93 us
    ppermute x8, waiting for transfers between devices, flipped(): return lax.ppermute(x, axis, [(k, k ^ bits) for k in range(count)])  2.48 us
    pallas_call x1, Pallas kernels, shards(): pl.pallas_call(functools.partial(bands_kernel, corr_scale), in_specs=[vme...  1.98 us
    pallas_call x1, Pallas kernels, shards(): pl.pallas_call(functools.partial(unpack_kernel, order), in_specs=[vmem()]...  1.95 us
  transfers between devices with their start and end apart: 14, of which 7 were waited for; matrix products, arithmetic and copies ran while one was open for 0% of the time, Pallas kernels for 13%

profile of v7, /device:TPU:0, one launch (start us, length us, event | category | flops | bytes accessed | tf_op | source)
XLA Modules:
  0.0 50.3 jit_solution(4967406574921367427)
XLA Ops:
  0.6 1.5 %pack.1 = (bf16[4,3,64,128]{3,2,1,0:T(8,128)(2,1)S(1)}, bf16[3,64,128]{2,1,0:T(8,128)(2,1)S(1)}, bf16[3,64,128]{2,1,0:T(8,128)(2,1)S(1)}, bf16[3,64,128]{2,1,0:T(8,128)(2,1)S(1)}, bf16[3,64,128]{2,1,0:T(8,128)(2,1)S(1)}) custom-call(s32[8]{0:T(128)} %bitcast.31, bf16[3,16,8192]{2,1,0:T(8,128)(2,1)} %bitcast.29), custom_call_target="tpu_custom_call" | custom-call | tf_op jit(solution)/shard_map/pack/pallas_call | solution.py:399
  2.1 0.5 %collective-permute-start = (bf16[4,3,64,128]{3,2,1,0:T(8,128)(2,1)S(1)}, bf16[4,3,64,128]{3,2,1,0:T(8,128)(2,1)S(1)}, u32[]{:S(2)}, u32[]{:S(2)}) collective-permute-start(bf16[4,3,64,128]{3,2,1,0:T(8,128)(2,1)S(1)} %get-tuple-element.28), channel_id=1, source_target_pairs={{0,4},{4,0},{8,12},{12,8},{16,20},{20,16},{24,28},{28,24},{1,5},{5... | collective-permute-start | bytes 589832 | tf_op jit(solution)/shard_map/ppermute | solution.py:354
  2.7 1.1 %collective-permute-done = bf16[4,3,64,128]{3,2,1,0:T(8,128)(2,1)S(1)} collective-permute-done((bf16[4,3,64,128]{3,2,1,0:T(8,128)(2,1)S(1)}, bf16[4,3,64,128]{3,2,1,0:T(8,128)(2,1)S(1)}, u32[]{:S(2)}, u32[]{:S(2)}) %collective-permute-start) | collective-permute-done | bytes 196640 | tf_op jit(solution)/shard_map/ppermute | solution.py:354
  3.8 3.0 %collective-permute-start.1 = (bf16[2,3,64,128]{3,2,1,0:T(8,128)(2,1)S(1)}, bf16[2,3,64,128]{3,2,1,0:T(8,128)(2,1)S(1)}, u32[]{:S(2)}, u32[]{:S(2)}) collective-permute-start(bf16[2,3,64,128]{3,2,1,0:T(8,128)(2,1)S(1)} %pad_maximum_fusion), channel_id=1, source_target_pairs={{0,8},{4,12},{8,16},{12,20},{16,24},{20,28},{24,0},{28,4},{1,9},{5... | collective-permute-start | bytes 294920 | tf_op jit(solution)/shard_map/ppermute | solution.py:364
  6.8 2.7 %collective-permute-start.2 = (bf16[2,3,64,128]{3,2,1,0:T(8,128)(2,1)S(1)}, bf16[2,3,64,128]{3,2,1,0:T(8,128)(2,1)S(1)}, u32[]{:S(2)}, u32[]{:S(2)}) collective-permute-start(bf16[2,3,64,128]{3,2,1,0:T(8,128)(2,1)S(1)} %pad_maximum_fusion.1), channel_id=1, source_target_pairs={{0,16},{4,20},{8,24},{12,28},{16,0},{20,4},{24,8},{28,12},{1,17},{... | collective-permute-start | bytes 294920 | tf_op jit(solution)/shard_map/ppermute | solution.py:364
  9.5 1.4 %collective-permute-start.3 = (bf16[2,3,64,128]{3,2,1,0:T(8,128)(2,1)S(1)}, bf16[2,3,64,128]{3,2,1,0:T(8,128)(2,1)S(1)}, u32[]{:S(2)}, u32[]{:S(2)}) collective-permute-start(bf16[2,3,64,128]{3,2,1,0:T(8,128)(2,1)S(1)} %pad_maximum_fusion.2), channel_id=1, source_target_pairs={{0,24},{4,28},{8,0},{12,4},{16,8},{20,12},{24,16},{28,20},{1,25},{... | collective-permute-start | bytes 294920 | tf_op jit(solution)/shard_map/ppermute | solution.py:364
  10.9 1.4 %prep.1 = (bf16[8,384,896]{2,1,0:T(8,128)(2,1)S(1)}, bf16[24,320,128]{2,1,0:T(8,128)(2,1)S(1)}, s32[16]{0:T(128)S(1)}, s32[16]{0:T(128)S(1)}, s32[8]{0:T(128)S(1...) custom-call(bf16[3,64,128]{2,1,0:T(8,128)(2,1)S(1)} %get-tuple-element.27.own_ref, ...), custom_call_target="tpu_custom_call" | custom-call | flops 2000000000 | bytes 4194304 | tf_op jit(solution)/shard_map/prep/pallas_call | solution.py:427
  12.3 0.2 collective-permute-done.1.refs_0_
  12.5 3.8 %collective-permute-done.2.refs_1_ = bf16[2,3,64,128]{3,2,1,0:T(8,128)(2,1)S(1)} collective-permute-done((bf16[2,3,64,128]{3,2,1,0:T(8,128)(2,1)S(1)}, bf16[2,3,64,128]{3,2,1,0:T(8,128)(2,1)S(1)}, u32[]{:S(2)}, u32[]{:S(2)}) %collective-permute-start.2) | collective-permute-done | bytes 98336 | tf_op jit(solution)/shard_map/ppermute | solution.py:364
  16.2 0.0 collective-permute-done.3.refs_2_
  16.2 3.1 %corr_first.1 = (f32[9,13,256]{2,1,0:T(8,128)S(1)}, bf16[24,320,128]{2,1,0:T(8,128)(2,1)S(1)}, bf16[8,96,256]{2,1,0:T(8,128)(2,1)S(1)}) custom-call(s32[16]{0:T(128)S(1)} %get-tuple-element.30.first_in.first_ref, s32[16]{0:T(128)S(1)} %get-tuple-element.31.second_in.second_ref, ...), custom_call_target="tpu_custom_call", output_to_operand_aliasing={{1}: (2, {})} | custom-call | flops 2000000000 | bytes 4194304 | tf_op jit(solution)/shard_map/corr_first/pallas_call | solution.py:452
  19.4 2.6 %collective-permute-start.6 = (f32[9,13,256]{2,1,0:T(8,128)S(1)}, f32[9,13,256]{2,1,0:T(8,128)S(1)}, u32[]{:S(2)}, u32[]{:S(2)}) collective-permute-start(f32[9,13,256]{2,1,0:T(8,128)S(1)} %get-tuple-element.40.refs_0_), channel_id=1, source_target_pairs={{0,3},{1,2},{2,1},{3,0},{4,7},{5,6},{6,5},{7,4},{8,11},{9,10},{10,... | collective-permute-start | bytes 359432 | tf_op jit(solution)/shard_map/ppermute | solution.py:354
  22.0 0.5 %collective-permute-start.5 = (f32[9,13,256]{2,1,0:T(8,128)S(1)}, f32[9,13,256]{2,1,0:T(8,128)S(1)}, u32[]{:S(2)}, u32[]{:S(2)}) collective-permute-start(f32[9,13,256]{2,1,0:T(8,128)S(1)} %get-tuple-element.40.refs_0_), channel_id=1, source_target_pairs={{0,2},{1,3},{2,0},{3,1},{4,6},{5,7},{6,4},{7,5},{8,10},{9,11},{10,... | collective-permute-start | bytes 359432 | tf_op jit(solution)/shard_map/ppermute | solution.py:354
  22.5 0.5 collective-permute-start.4
  22.9 1.2 %corr_second.1.refs_0_ = f32[9,3,256]{2,1,0:T(4,128)S(1)} custom-call(s32[16]{0:T(128)S(1)} %get-tuple-element.30.first_in.first_ref, s32[16]{0:T(128)S(1)} %get-tuple-element.31.second_in.second_ref, bf16[24,320,128]{2,1,0:T(8,128)(2,1)S(1)} %get-tuple-element.42.fan_ref, bf16[8,96,256]{2,1,0:T(8,128)(2,1)S(1)} %get-tuple-element.44.heads), custom_call_target="tpu_custom_call" | custom-call | flops 2000000000 | bytes 4194304 | tf_op jit(solution)/shard_map/corr_second/pallas_call | solution.py:470
  24.1 2.6 %collective-permute-start.9 = (f32[9,3,256]{2,1,0:T(4,128)S(1)}, f32[9,3,256]{2,1,0:T(4,128)S(1)}, u32[]{:S(2)}, u32[]{:S(2)}) collective-permute-start(f32[9,3,256]{2,1,0:T(4,128)S(1)} %corr_second.1.refs_0_), channel_id=1, source_target_pairs={{0,3},{1,2},{2,1},{3,0},{4,7},{5,6},{6,5},{7,4},{8,11},{9,10},{10,... | collective-permute-start | bytes 82952 | tf_op jit(solution)/shard_map/ppermute | solution.py:354
  26.7 0.5 %collective-permute-start.8 = (f32[9,3,256]{2,1,0:T(4,128)S(1)}, f32[9,3,256]{2,1,0:T(4,128)S(1)}, u32[]{:S(2)}, u32[]{:S(2)}) collective-permute-start(f32[9,3,256]{2,1,0:T(4,128)S(1)} %corr_second.1.refs_0_), channel_id=1, source_target_pairs={{0,2},{1,3},{2,0},{3,1},{4,6},{5,7},{6,4},{7,5},{8,10},{9,11},{10,... | collective-permute-start | bytes 82952 | tf_op jit(solution)/shard_map/ppermute | solution.py:354
  27.2 0.0 collective-permute-done.6.refs_3_
  27.2 1.4 %collective-permute-start.7 = (f32[9,3,256]{2,1,0:T(4,128)S(1)}, f32[9,3,256]{2,1,0:T(4,128)S(1)}, u32[]{:S(2)}, u32[]{:S(2)}) collective-permute-start(f32[9,3,256]{2,1,0:T(4,128)S(1)} %corr_second.1.refs_0_), channel_id=1, source_target_pairs={{0,1},{1,0},{2,3},{3,2},{4,5},{5,4},{6,7},{7,6},{8,9},{9,8},{10,11... | collective-permute-start | bytes 82952 | tf_op jit(solution)/shard_map/ppermute | solution.py:354
  28.7 1.0 %collective-permute-done.5.refs_2_ = f32[9,13,256]{2,1,0:T(8,128)S(1)} collective-permute-done((f32[9,13,256]{2,1,0:T(8,128)S(1)}, f32[9,13,256]{2,1,0:T(8,128)S(1)}, u32[]{:S(2)}, u32[]{:S(2)}) %collective-permute-start.5) | collective-permute-done | bytes 119840 | tf_op jit(solution)/shard_map/ppermute | solution.py:354
  29.7 0.4 collective-permute-done.4.refs_1_
  30.1 2.0 %bands.1 = (bf16[8,384,896]{2,1,0:T(8,128)(2,1)S(1)}, f32[9,13,256]{2,1,0:T(8,128)S(1)}) custom-call(s32[16]{0:T(128)S(1)} %get-tuple-element.30.first_in.first_ref, s32[16]{0:T(128)S(1)} %get-tuple-element.31.second_in.second_ref, s32[16,256]{1,0:T(8,128)S(1)} %get-tuple-element.32.inside_ref, ...), custom_call_target="tpu_custom_call", output_to_operand_aliasing={{0}: (4, {})} | custom-call | flops 2000000000 | bytes 4194304 | tf_op jit(solution)/shard_map/bands/pallas_call | solution.py:482
  32.1 0.0 collective-permute-done.9.refs_3_
  32.1 0.0 collective-permute-done.8.refs_2_
  32.1 0.0 collective-permute-done.7.refs_1_
  32.1 2.9 %adjoint.1 = (bf16[8,384,896]{2,1,0:T(8,128)(2,1)S(1)}, bf16[4,3,64,128]{3,2,1,0:T(8,128)(2,1)S(1)}, f32[9,4,256]{2,1,0:T(4,128)}) custom-call(s32[16]{0:T(128)S(1)} %get-tuple-element.30.first_in.first_ref, s32[16]{0:T(128)S(1)} %get-tuple-element.31.second_in.second_ref, ...), custom_call_target="tpu_custom_call", output_to_operand_aliasing={{0}: (4, {})} | custom-call | flops 2000000000 | bytes 4194304 | tf_op jit(solution)/shard_map/adjoint/pallas_call | solution.py:497
  35.0 0.1 collective-permute-start.10
  35.1 1.8 %keep.1 = (bf16[3,64,128]{2,1,0:T(8,128)(2,1)S(1)}, bf16[3,64,128]{2,1,0:T(8,128)(2,1)S(1)}, bf16[3,64,128]{2,1,0:T(8,128)(2,1)S(1)}, bf16[3,64,128]{2,1,0:T(8,128)(2,1)S(1)}) custom-call(bf16[8,384,896]{2,1,0:T(8,128)(2,1)S(1)} %get-tuple-element.45.bands, bf16[24,320,128]{2,1,0:T(8,128)(2,1)S(1)} %get-tuple-element.42.fan_ref), custom_call_target="tpu_custom_call" | custom-call | flops 2000000000 | bytes 4194304 | tf_op jit(solution)/shard_map/keep/pallas_call | solution.py:516
  37.0 0.0 collective-permute-done.10
  37.0 2.7 %collective-permute-start.11 = (bf16[2,3,64,128]{3,2,1,0:T(8,128)(2,1)S(1)}, bf16[2,3,64,128]{3,2,1,0:T(8,128)(2,1)S(1)}, u32[]{:S(2)}, u32[]{:S(2)}) collective-permute-start(bf16[2,3,64,128]{3,2,1,0:T(8,128)(2,1)S(1)} %pad_maximum_fusion.3), channel_id=1, source_target_pairs={{0,8},{4,12},{8,16},{12,20},{16,24},{20,28},{24,0},{28,4},{1,9},{5... | collective-permute-start | bytes 294920 | tf_op jit(solution)/shard_map/ppermute | solution.py:364
  39.8 0.9 %collective-permute-start.12 = (bf16[2,3,64,128]{3,2,1,0:T(8,128)(2,1)S(1)}, bf16[2,3,64,128]{3,2,1,0:T(8,128)(2,1)S(1)}, u32[]{:S(2)}, u32[]{:S(2)}) collective-permute-start(bf16[2,3,64,128]{3,2,1,0:T(8,128)(2,1)S(1)} %pad_maximum_fusion.4), channel_id=1, source_target_pairs={{0,16},{4,20},{8,24},{12,28},{16,0},{20,4},{24,8},{28,12},{1,17},{... | collective-permute-start | bytes 294920 | tf_op jit(solution)/shard_map/ppermute | solution.py:364
  40.7 1.6 %collective-permute-start.13 = (bf16[2,3,64,128]{3,2,1,0:T(8,128)(2,1)S(1)}, bf16[2,3,64,128]{3,2,1,0:T(8,128)(2,1)S(1)}, u32[]{:S(2)}, u32[]{:S(2)}) collective-permute-start(bf16[2,3,64,128]{3,2,1,0:T(8,128)(2,1)S(1)} %pad_maximum_fusion.5), channel_id=1, source_target_pairs={{0,24},{4,28},{8,0},{12,4},{16,8},{20,12},{24,16},{28,20},{1,25},{... | collective-permute-start | bytes 294920 | tf_op jit(solution)/shard_map/ppermute | solution.py:364
  42.3 2.3 %collective-permute-done.11.refs_0_ = bf16[2,3,64,128]{3,2,1,0:T(8,128)(2,1)S(1)} collective-permute-done((bf16[2,3,64,128]{3,2,1,0:T(8,128)(2,1)S(1)}, bf16[2,3,64,128]{3,2,1,0:T(8,128)(2,1)S(1)}, u32[]{:S(2)}, u32[]{:S(2)}) %collective-permute-start.11) | collective-permute-done | bytes 98336 | tf_op jit(solution)/shard_map/ppermute | solution.py:364
  44.6 3.8 %collective-permute-done.12.refs_1_ = bf16[2,3,64,128]{3,2,1,0:T(8,128)(2,1)S(1)} collective-permute-done((bf16[2,3,64,128]{3,2,1,0:T(8,128)(2,1)S(1)}, bf16[2,3,64,128]{3,2,1,0:T(8,128)(2,1)S(1)}, u32[]{:S(2)}, u32[]{:S(2)}) %collective-permute-start.12) | collective-permute-done | bytes 98336 | tf_op jit(solution)/shard_map/ppermute | solution.py:364
  48.3 0.0 collective-permute-done.13.refs_2_
  48.3 2.0 %unpack.1 = bf16[3,16,8192]{2,1,0:T(8,128)(2,1)} custom-call(s32[8]{0:T(128)S(1)} %get-tuple-element.29.rows_in, bf16[2,3,64,128]{3,2,1,0:T(8,128)(2,1)S(1)} %collective-permute-done.11.refs_0_, bf16[2,3,64,128]{3,2,1,0:T(8,128)(2,1)S(1)} %collective-permute-done.12.refs_1_, bf16[2,3,64,128]{3,2,1,0:T(8,128)(2,1)S(1)} %collective-permute-done.13.refs_2_, ...), custom_call_target="tpu_custom_call" | custom-call | tf_op jit(solution)/shard_map/unpack/pallas_call | solution.py:527
  (8 shorter events, 0.1 us)
Async XLA Ops:
  2.1 1.6 %collective-permute-start = (bf16[4,3,64,128]{3,2,1,0:T(8,128)(2,1)S(1)}, bf16[4,3,64,128]{3,2,1,0:T(8,128)(2,1)S(1)}, u32[]{:S(2)}, u32[]{:S(2)}) collective-permute-start(bf16[4,3,64,128]{3,2,1,0:T(8,128)(2,1)S(1)} %get-tuple-element.28), channel_id=1, source_target_pairs={{0,4},{4,0},{8,12},{12,8},{16,20},{20,16},{24,28},{28,24},{1,5},{5... | collective-permute-start | bytes 589832 | tf_op jit(solution)/shard_map/ppermute | solution.py:354
  3.8 8.7 %collective-permute-start.1 = (bf16[2,3,64,128]{3,2,1,0:T(8,128)(2,1)S(1)}, bf16[2,3,64,128]{3,2,1,0:T(8,128)(2,1)S(1)}, u32[]{:S(2)}, u32[]{:S(2)}) collective-permute-start(bf16[2,3,64,128]{3,2,1,0:T(8,128)(2,1)S(1)} %pad_maximum_fusion), channel_id=1, source_target_pairs={{0,8},{4,12},{8,16},{12,20},{16,24},{20,28},{24,0},{28,4},{1,9},{5... | collective-permute-start | bytes 294920 | tf_op jit(solution)/shard_map/ppermute | solution.py:364
  6.8 9.4 %collective-permute-start.2 = (bf16[2,3,64,128]{3,2,1,0:T(8,128)(2,1)S(1)}, bf16[2,3,64,128]{3,2,1,0:T(8,128)(2,1)S(1)}, u32[]{:S(2)}, u32[]{:S(2)}) collective-permute-start(bf16[2,3,64,128]{3,2,1,0:T(8,128)(2,1)S(1)} %pad_maximum_fusion.1), channel_id=1, source_target_pairs={{0,16},{4,20},{8,24},{12,28},{16,0},{20,4},{24,8},{28,12},{1,17},{... | collective-permute-start | bytes 294920 | tf_op jit(solution)/shard_map/ppermute | solution.py:364
  9.5 6.8 %collective-permute-start.3 = (bf16[2,3,64,128]{3,2,1,0:T(8,128)(2,1)S(1)}, bf16[2,3,64,128]{3,2,1,0:T(8,128)(2,1)S(1)}, u32[]{:S(2)}, u32[]{:S(2)}) collective-permute-start(bf16[2,3,64,128]{3,2,1,0:T(8,128)(2,1)S(1)} %pad_maximum_fusion.2), channel_id=1, source_target_pairs={{0,24},{4,28},{8,0},{12,4},{16,8},{20,12},{24,16},{28,20},{1,25},{... | collective-permute-start | bytes 294920 | tf_op jit(solution)/shard_map/ppermute | solution.py:364
  19.4 7.9 %collective-permute-start.6 = (f32[9,13,256]{2,1,0:T(8,128)S(1)}, f32[9,13,256]{2,1,0:T(8,128)S(1)}, u32[]{:S(2)}, u32[]{:S(2)}) collective-permute-start(f32[9,13,256]{2,1,0:T(8,128)S(1)} %get-tuple-element.40.refs_0_), channel_id=1, source_target_pairs={{0,3},{1,2},{2,1},{3,0},{4,7},{5,6},{6,5},{7,4},{8,11},{9,10},{10,... | collective-permute-start | bytes 359432 | tf_op jit(solution)/shard_map/ppermute | solution.py:354
  22.0 7.7 %collective-permute-start.5 = (f32[9,13,256]{2,1,0:T(8,128)S(1)}, f32[9,13,256]{2,1,0:T(8,128)S(1)}, u32[]{:S(2)}, u32[]{:S(2)}) collective-permute-start(f32[9,13,256]{2,1,0:T(8,128)S(1)} %get-tuple-element.40.refs_0_), channel_id=1, source_target_pairs={{0,2},{1,3},{2,0},{3,1},{4,6},{5,7},{6,4},{7,5},{8,10},{9,11},{10,... | collective-permute-start | bytes 359432 | tf_op jit(solution)/shard_map/ppermute | solution.py:354
  22.5 7.6 %collective-permute-start.4 = (f32[9,13,256]{2,1,0:T(8,128)S(1)}, f32[9,13,256]{2,1,0:T(8,128)S(1)}, u32[]{:S(2)}, u32[]{:S(2)}) collective-permute-start(f32[9,13,256]{2,1,0:T(8,128)S(1)} %get-tuple-element.40.refs_0_), channel_id=1, source_target_pairs={{0,1},{1,0},{2,3},{3,2},{4,5},{5,4},{6,7},{7,6},{8,9},{9,8},{10,11... | collective-permute-start | bytes 359432 | tf_op jit(solution)/shard_map/ppermute | solution.py:354
  24.1 7.9 %collective-permute-start.9 = (f32[9,3,256]{2,1,0:T(4,128)S(1)}, f32[9,3,256]{2,1,0:T(4,128)S(1)}, u32[]{:S(2)}, u32[]{:S(2)}) collective-permute-start(f32[9,3,256]{2,1,0:T(4,128)S(1)} %corr_second.1.refs_0_), channel_id=1, source_target_pairs={{0,3},{1,2},{2,1},{3,0},{4,7},{5,6},{6,5},{7,4},{8,11},{9,10},{10,... | collective-permute-start | bytes 82952 | tf_op jit(solution)/shard_map/ppermute | solution.py:354
  26.7 5.3 %collective-permute-start.8 = (f32[9,3,256]{2,1,0:T(4,128)S(1)}, f32[9,3,256]{2,1,0:T(4,128)S(1)}, u32[]{:S(2)}, u32[]{:S(2)}) collective-permute-start(f32[9,3,256]{2,1,0:T(4,128)S(1)} %corr_second.1.refs_0_), channel_id=1, source_target_pairs={{0,2},{1,3},{2,0},{3,1},{4,6},{5,7},{6,4},{7,5},{8,10},{9,11},{10,... | collective-permute-start | bytes 82952 | tf_op jit(solution)/shard_map/ppermute | solution.py:354
  27.2 4.8 %collective-permute-start.7 = (f32[9,3,256]{2,1,0:T(4,128)S(1)}, f32[9,3,256]{2,1,0:T(4,128)S(1)}, u32[]{:S(2)}, u32[]{:S(2)}) collective-permute-start(f32[9,3,256]{2,1,0:T(4,128)S(1)} %corr_second.1.refs_0_), channel_id=1, source_target_pairs={{0,1},{1,0},{2,3},{3,2},{4,5},{5,4},{6,7},{7,6},{8,9},{9,8},{10,11... | collective-permute-start | bytes 82952 | tf_op jit(solution)/shard_map/ppermute | solution.py:354
  35.0 1.9 %collective-permute-start.10 = (bf16[4,3,64,128]{3,2,1,0:T(8,128)(2,1)S(1)}, bf16[4,3,64,128]{3,2,1,0:T(8,128)(2,1)S(1)}, u32[]{:S(2)}, u32[]{:S(2)}) collective-permute-start(bf16[4,3,64,128]{3,2,1,0:T(8,128)(2,1)S(1)} %get-tuple-element.47), channel_id=1, source_target_pairs={{0,4},{4,0},{8,12},{12,8},{16,20},{20,16},{24,28},{28,24},{1,5},{5... | collective-permute-start | bytes 589832 | tf_op jit(solution)/shard_map/ppermute | solution.py:354
  37.0 7.5 %collective-permute-start.11 = (bf16[2,3,64,128]{3,2,1,0:T(8,128)(2,1)S(1)}, bf16[2,3,64,128]{3,2,1,0:T(8,128)(2,1)S(1)}, u32[]{:S(2)}, u32[]{:S(2)}) collective-permute-start(bf16[2,3,64,128]{3,2,1,0:T(8,128)(2,1)S(1)} %pad_maximum_fusion.3), channel_id=1, source_target_pairs={{0,8},{4,12},{8,16},{12,20},{16,24},{20,28},{24,0},{28,4},{1,9},{5... | collective-permute-start | bytes 294920 | tf_op jit(solution)/shard_map/ppermute | solution.py:364
  39.8 8.6 %collective-permute-start.12 = (bf16[2,3,64,128]{3,2,1,0:T(8,128)(2,1)S(1)}, bf16[2,3,64,128]{3,2,1,0:T(8,128)(2,1)S(1)}, u32[]{:S(2)}, u32[]{:S(2)}) collective-permute-start(bf16[2,3,64,128]{3,2,1,0:T(8,128)(2,1)S(1)} %pad_maximum_fusion.4), channel_id=1, source_target_pairs={{0,16},{4,20},{8,24},{12,28},{16,0},{20,4},{24,8},{28,12},{1,17},{... | collective-permute-start | bytes 294920 | tf_op jit(solution)/shard_map/ppermute | solution.py:364
  40.7 7.7 %collective-permute-start.13 = (bf16[2,3,64,128]{3,2,1,0:T(8,128)(2,1)S(1)}, bf16[2,3,64,128]{3,2,1,0:T(8,128)(2,1)S(1)}, u32[]{:S(2)}, u32[]{:S(2)}) collective-permute-start(bf16[2,3,64,128]{3,2,1,0:T(8,128)(2,1)S(1)} %pad_maximum_fusion.5), channel_id=1, source_target_pairs={{0,24},{4,28},{8,0},{12,4},{16,8},{20,12},{24,16},{28,20},{1,25},{... | collective-permute-start | bytes 294920 | tf_op jit(solution)/shard_map/ppermute | solution.py:364
